TPU v7x, 32 devices: a whole 2x2x4 slice. The times are simulated.
32 devices in a mesh: dp: 4 (over y, core), expert: 8 (over z, x).
Axes of the slice: x: 2, y: 2, z: 4, core: 2. Of those that a mesh axis runs over, the one named last changes fastest.
Arguments:
- images: bfloat16 [192, 197, 768], P(('dp', 'expert')), may hold values from -6 to 6
- first_gain: bfloat16 [768], P('dp'), may hold values from 0.5 to 1.5
- first_shift: bfloat16 [768], P('dp'), may hold values from -1.5 to 1.5
- attn_in: bfloat16 [768, 2304], P('dp'), may hold values from -0.21875 to 0.21875
- attn_out: bfloat16 [768, 768], P('dp'), may hold values from -2 to 2
- second_gain: bfloat16 [768], P('dp'), may hold values from 0.5 to 1.5
- second_shift: bfloat16 [768], P('dp'), may hold values from -1.5 to 1.5
- router: bfloat16 [768, 8], P('dp'), may hold values from -0.15625 to 0.15625
- expert_in: bfloat16 [8, 3072, 768], P('expert', 'dp'), may hold values from -0.21875 to 0.21875
- expert_bias: bfloat16 [8, 3072], P('expert', 'dp'), may hold values from -2.5 to 2.5
- expert_out: bfloat16 [8, 3072, 768], P('expert', 'dp'), may hold values from -0.625 to 0.625
- routes: int32 [192, 197, 2], P(('dp', 'expert')), may hold values from 0 to 7, all different within a row
- out_grad: bfloat16 [192, 197, 768], P(('dp', 'expert')), may hold values from -6 to 6
Outputs:
- block_out: bfloat16 [192, 197, 768], P(('dp', 'expert'))
- input_grad: float32 [192, 197, 768], P(('dp', 'expert'))
- grad_first_gain: float32 [768], P('dp')
- grad_first_shift: float32 [768], P('dp')
- grad_attn_in: float32 [768, 2304], P('dp')
- grad_attn_out: float32 [768, 768], P('dp')
- grad_second_gain: float32 [768], P('dp')
- grad_second_shift: float32 [768], P('dp')
- grad_router: float32 [768, 8], P('dp')
- grad_expert_in: float32 [8, 3072, 768], P('expert', 'dp')
- grad_expert_bias: float32 [8, 3072], P('expert', 'dp')
- grad_expert_out: float32 [8, 3072, 768], P('expert', 'dp')
Inputs may be any that keep to these rules, and one draw needn't show every extreme that they name: `routes`: the 2 entries of a token name different experts; every expert is named by some token.
All inputs are finite; a program needn't handle non-finite values.
Results may differ from a plain program's by a relative error of at most 0.024.
Values may be sent and summed in bfloat16 or wider, within the bound.
A program may use at most 320 MiB of HBM per device.

v0:
```python
from functools import reduce

import jax
import jax.numpy as jnp
from jax import lax
from jax.sharding import PartitionSpec as P

HEADS = 12
HEAD_DIM = 64
SEQ = 197
MICRO = 2
IMG_MB = 3


epsilon = 1e-06
highest = lax.Precision.HIGHEST


def matmul(left_side, right_side):
    return jnp.dot(left_side, right_side, preferred_element_type=jnp.float32)


def contract(formula, left_side, right_side):
    return jnp.einsum(formula, left_side, right_side, preferred_element_type=jnp.float32)


def total(items):
    return reduce(lambda total_left, total_right: total_left + total_right, items)


def gelu_exact(values):
    return jax.nn.gelu(values, approximate=False)


def norm_forward(values):
    row_mean = jnp.mean(values, axis=-1, keepdims=True)
    centred = values - row_mean
    row_var = jnp.mean(centred * centred, axis=-1, keepdims=True)
    inverse = lax.rsqrt(row_var + epsilon)
    return (centred * inverse, inverse)


def norm_backward(grad_normed, normed, inverse):
    mean_grad = jnp.mean(grad_normed, axis=-1, keepdims=True)
    mean_cross = jnp.mean(grad_normed * normed, axis=-1, keepdims=True)
    return inverse * (grad_normed - mean_grad - normed * mean_cross)


def slot_tables(route_block, experts, capacity):
    token_count = route_block.shape[0]
    top_count = route_block.shape[1]
    pair_order = route_block.T.reshape(-1)
    onehot = (pair_order[:, None] == jnp.arange(experts, dtype=jnp.int32)[None, :]).astype(
        jnp.int32
    )
    earlier = jnp.cumsum(onehot, axis=0) - onehot
    position = jnp.sum(earlier * onehot, axis=1)
    kept_mask = position < capacity
    slot_index = jnp.where(kept_mask, pair_order * capacity + position, experts * capacity)
    token_ids = jnp.tile(jnp.arange(token_count, dtype=jnp.int32), top_count)
    owners = (
        jnp.full((experts * capacity + 1,), -1, jnp.int32)
        .at[slot_index]
        .set(token_ids)[: experts * capacity]
    )
    return (slot_index, owners)


def per_device(
    images,
    first_gain,
    first_shift,
    attn_in,
    attn_out,
    second_gain,
    second_shift,
    router,
    expert_in,
    expert_bias,
    expert_out,
    routes,
    out_grad,
):
    features = images.shape[2]
    experts = router.shape[1]
    top_count = routes.shape[2]
    tok_mb = IMG_MB * SEQ
    capacity = max(2, (5 * top_count * tok_mb // (4 * experts) + 7) // 8 * 8)
    scale_factor = HEAD_DIM ** (-0.5)
    head_shape = (IMG_MB, SEQ, HEADS, HEAD_DIM)
    expert_ids = jnp.arange(experts, dtype=jnp.int32)

    def fetch_dense():
        return (
            lax.all_gather(attn_in, "dp", axis=0, tiled=True),
            lax.all_gather(attn_out, "dp", axis=0, tiled=True),
            lax.all_gather(router, "dp", axis=0, tiled=True),
            lax.all_gather(first_gain, "dp", axis=0, tiled=True),
            lax.all_gather(first_shift, "dp", axis=0, tiled=True),
            lax.all_gather(second_gain, "dp", axis=0, tiled=True),
            lax.all_gather(second_shift, "dp", axis=0, tiled=True),
        )

    def fetch_experts():
        fetched = (
            lax.all_gather(expert_in, "dp", axis=1, tiled=True),
            lax.all_gather(expert_out, "dp", axis=1, tiled=True),
            lax.all_gather(expert_bias, "dp", axis=1, tiled=True),
        )
        return (fetched[0][0], fetched[1][0], fetched[2][0])

    out_blocks = []
    grad_blocks = []
    acc_attn_in = []
    acc_attn_out = []
    acc_router = []
    acc_gain_one = []
    acc_shift_one = []
    acc_gain_two = []
    acc_shift_two = []
    acc_expert_in = []
    acc_expert_out = []
    acc_expert_bias = []
    for micro_index in range(MICRO):
        attn_in_full, attn_out_full, router_full, gain_one, shift_one, gain_two, shift_two = (
            fetch_dense()
        )
        weight_in, weight_out, bias_row = fetch_experts()
        first_image = micro_index * IMG_MB
        image_block = (
            lax.slice_in_dim(images, first_image, first_image + IMG_MB, axis=0)
            .astype(jnp.float32)
            .reshape(tok_mb, features)
        )
        route_block = lax.slice_in_dim(routes, first_image, first_image + IMG_MB, axis=0).reshape(
            tok_mb, top_count
        )
        grad_top = (
            lax.slice_in_dim(out_grad, first_image, first_image + IMG_MB, axis=0)
            .astype(jnp.float32)
            .reshape(tok_mb, features)
        )
        normed_one, inverse_one = norm_forward(image_block)
        attn_input = (
            normed_one * gain_one.astype(jnp.float32) + shift_one.astype(jnp.float32)
        ).astype(jnp.bfloat16)
        projected = matmul(attn_input, attn_in_full).astype(jnp.bfloat16)
        queries = projected[:, :features].reshape(head_shape)
        key_heads = projected[:, features : 2 * features].reshape(head_shape)
        values = projected[:, 2 * features :].reshape(head_shape)
        scores = contract("iqhc,ikhc->ihqk", queries, key_heads) * scale_factor
        attn_probs = jax.nn.softmax(scores, axis=-1)
        attn_weights = attn_probs.astype(jnp.bfloat16)
        mixed_heads = (
            contract("ihqk,ikhc->iqhc", attn_weights, values)
            .astype(jnp.bfloat16)
            .reshape(tok_mb, features)
        )
        residual = image_block + matmul(mixed_heads, attn_out_full)
        normed_two, inverse_two = norm_forward(residual)
        hidden = (normed_two * gain_two.astype(jnp.float32) + shift_two.astype(jnp.float32)).astype(
            jnp.bfloat16
        )
        router_probs = jax.nn.softmax(matmul(hidden, router_full), axis=-1)
        gate_values = jnp.take_along_axis(router_probs, route_block, axis=1)
        slot_index, owners = slot_tables(route_block, experts, capacity)
        dispatched = jnp.where(
            (owners >= 0)[:, None], hidden[jnp.maximum(owners, 0)], jnp.zeros((), jnp.bfloat16)
        )
        received = lax.all_to_all(
            dispatched.reshape(experts, capacity, features),
            "expert",
            split_axis=0,
            concat_axis=0,
            tiled=True,
        ).reshape(experts * capacity, features)
        expert_pre = contract("rd,fd->rf", received, weight_in) + bias_row.astype(jnp.float32)
        activation, gelu_pull = jax.vjp(gelu_exact, expert_pre)
        expert_act = activation.astype(jnp.bfloat16)
        expert_result = matmul(expert_act, weight_out).astype(jnp.bfloat16)
        returned = lax.all_to_all(
            expert_result.reshape(experts, capacity, features),
            "expert",
            split_axis=0,
            concat_axis=0,
            tiled=True,
        ).reshape(experts * capacity, features)
        padded = jnp.concatenate(
            [returned.astype(jnp.float32), jnp.zeros((1, features), jnp.float32)], axis=0
        )
        picked = padded[slot_index].reshape(top_count, tok_mb, features)
        expert_mix = jnp.sum(gate_values.T[:, :, None] * picked, axis=0)
        out_blocks.append(
            (residual + expert_mix).astype(jnp.bfloat16).reshape(IMG_MB, SEQ, features)
        )
        grad_gates = jnp.sum(grad_top[None, :, :] * picked, axis=2)
        grad_picked = (gate_values.T[:, :, None] * grad_top[None, :, :]).reshape(
            top_count * tok_mb, features
        )
        grad_slots = (
            jnp.zeros((experts * capacity + 1, features), jnp.float32)
            .at[slot_index]
            .set(grad_picked)[: experts * capacity]
            .astype(jnp.bfloat16)
        )
        grad_rows = lax.all_to_all(
            grad_slots.reshape(experts, capacity, features),
            "expert",
            split_axis=0,
            concat_axis=0,
            tiled=True,
        ).reshape(experts * capacity, features)
        attn_in_full, attn_out_full, router_full, gain_one, shift_one, gain_two, shift_two = (
            fetch_dense()
        )
        weight_in, weight_out, bias_row = fetch_experts()
        grad_act = contract("rd,fd->rf", grad_rows, weight_out)
        grad_pre = gelu_pull(grad_act)[0].astype(jnp.bfloat16)
        acc_expert_out.append(contract("rf,rd->fd", expert_act, grad_rows))
        acc_expert_in.append(contract("rf,rd->fd", grad_pre, received))
        acc_expert_bias.append(jnp.sum(grad_pre.astype(jnp.float32), axis=0))
        grad_dispatched = matmul(grad_pre, weight_in).astype(jnp.bfloat16)
        grad_sent = lax.all_to_all(
            grad_dispatched.reshape(experts, capacity, features),
            "expert",
            split_axis=0,
            concat_axis=0,
            tiled=True,
        ).reshape(experts * capacity, features)
        back_padded = jnp.concatenate(
            [grad_sent.astype(jnp.float32), jnp.zeros((1, features), jnp.float32)], axis=0
        )
        grad_hidden = jnp.sum(back_padded[slot_index].reshape(top_count, tok_mb, features), axis=0)
        route_match = (route_block[:, :, None] == expert_ids[None, None, :]).astype(jnp.float32)
        grad_router_probs = jnp.sum(route_match * grad_gates.T[:, :, None], axis=1)
        grad_logits = router_probs * (
            grad_router_probs - jnp.sum(grad_router_probs * router_probs, axis=-1, keepdims=True)
        )
        router_wide = router_full.astype(jnp.float32)
        grad_hidden = grad_hidden + jnp.dot(grad_logits, router_wide.T, precision=highest)
        acc_router.append(jnp.dot(hidden.astype(jnp.float32).T, grad_logits, precision=highest))
        acc_gain_two.append(jnp.sum(grad_hidden * normed_two, axis=0))
        acc_shift_two.append(jnp.sum(grad_hidden, axis=0))
        grad_residual = grad_top + norm_backward(
            grad_hidden * gain_two.astype(jnp.float32), normed_two, inverse_two
        )
        grad_branch = grad_residual.astype(jnp.bfloat16)
        acc_attn_out.append(contract("td,te->de", mixed_heads, grad_branch))
        grad_mixed = (
            contract("te,de->td", grad_branch, attn_out_full)
            .astype(jnp.bfloat16)
            .reshape(head_shape)
        )
        grad_weights = contract("iqhc,ikhc->ihqk", grad_mixed, values)
        grad_values = contract("ihqk,iqhc->ikhc", attn_weights, grad_mixed)
        row_inner = jnp.sum(grad_weights * attn_probs, axis=-1, keepdims=True)
        grad_scores = (attn_probs * (grad_weights - row_inner)).astype(jnp.bfloat16)
        grad_queries = contract("ihqk,ikhc->iqhc", grad_scores, key_heads) * scale_factor
        grad_keys = contract("ihqk,iqhc->ikhc", grad_scores, queries) * scale_factor
        grad_projected = jnp.concatenate(
            [
                grad_queries.reshape(tok_mb, features),
                grad_keys.reshape(tok_mb, features),
                grad_values.reshape(tok_mb, features),
            ],
            axis=1,
        ).astype(jnp.bfloat16)
        acc_attn_in.append(contract("td,te->de", attn_input, grad_projected))
        grad_attn_input = contract("te,de->td", grad_projected, attn_in_full)
        acc_gain_one.append(jnp.sum(grad_attn_input * normed_one, axis=0))
        acc_shift_one.append(jnp.sum(grad_attn_input, axis=0))
        input_block = grad_residual + norm_backward(
            grad_attn_input * gain_one.astype(jnp.float32), normed_one, inverse_one
        )
        grad_blocks.append(input_block.reshape(IMG_MB, SEQ, features))
    owned = (
        lax.psum_scatter(
            total(acc_attn_in).astype(jnp.bfloat16), "dp", scatter_dimension=0, tiled=True
        ).astype(jnp.float32),
        lax.psum_scatter(
            total(acc_attn_out).astype(jnp.bfloat16), "dp", scatter_dimension=0, tiled=True
        ).astype(jnp.float32),
        lax.psum_scatter(
            total(acc_router).astype(jnp.bfloat16), "dp", scatter_dimension=0, tiled=True
        ).astype(jnp.float32),
        lax.psum_scatter(
            total(acc_gain_one).astype(jnp.bfloat16), "dp", scatter_dimension=0, tiled=True
        ).astype(jnp.float32),
        lax.psum_scatter(
            total(acc_shift_one).astype(jnp.bfloat16), "dp", scatter_dimension=0, tiled=True
        ).astype(jnp.float32),
        lax.psum_scatter(
            total(acc_gain_two).astype(jnp.bfloat16), "dp", scatter_dimension=0, tiled=True
        ).astype(jnp.float32),
        lax.psum_scatter(
            total(acc_shift_two).astype(jnp.bfloat16), "dp", scatter_dimension=0, tiled=True
        ).astype(jnp.float32),
    )
    (
        owned_attn_in,
        owned_attn_out,
        owned_router,
        owned_gain_one,
        owned_shift_one,
        owned_gain_two,
        owned_shift_two,
    ) = owned
    summed = (
        lax.psum(owned_attn_in.astype(jnp.bfloat16), "expert").astype(jnp.float32),
        lax.psum(owned_attn_out.astype(jnp.bfloat16), "expert").astype(jnp.float32),
        lax.psum(owned_router.astype(jnp.bfloat16), "expert").astype(jnp.float32),
        lax.psum(owned_gain_one.astype(jnp.bfloat16), "expert").astype(jnp.float32),
        lax.psum(owned_shift_one.astype(jnp.bfloat16), "expert").astype(jnp.float32),
        lax.psum(owned_gain_two.astype(jnp.bfloat16), "expert").astype(jnp.float32),
        lax.psum(owned_shift_two.astype(jnp.bfloat16), "expert").astype(jnp.float32),
    )
    grad_expert_in, grad_expert_out, grad_expert_bias = (
        lax.psum_scatter(
            total(acc_expert_in)[None].astype(jnp.bfloat16), "dp", scatter_dimension=1, tiled=True
        ).astype(jnp.float32),
        lax.psum_scatter(
            total(acc_expert_out)[None].astype(jnp.bfloat16), "dp", scatter_dimension=1, tiled=True
        ).astype(jnp.float32),
        lax.psum_scatter(
            total(acc_expert_bias)[None].astype(jnp.bfloat16), "dp", scatter_dimension=1, tiled=True
        ).astype(jnp.float32),
    )
    block_out = jnp.concatenate(out_blocks, axis=0)
    input_grad = jnp.concatenate(grad_blocks, axis=0)
    return (
        block_out,
        input_grad,
        summed[3],
        summed[4],
        summed[0],
        summed[1],
        summed[5],
        summed[6],
        summed[2],
        grad_expert_in,
        grad_expert_bias,
        grad_expert_out,
    )


def solution(mesh):
    return jax.shard_map(
        per_device,
        mesh=mesh,
        in_specs=(
            P(("dp", "expert"), None, None),
            P("dp"),
            P("dp"),
            P("dp", None),
            P("dp", None),
            P("dp"),
            P("dp"),
            P("dp", None),
            P("expert", "dp", None),
            P("expert", "dp"),
            P("expert", "dp", None),
            P(("dp", "expert"), None, None),
            P(("dp", "expert"), None, None),
        ),
        out_specs=(
            P(("dp", "expert"), None, None),
            P(("dp", "expert"), None, None),
            P("dp"),
            P("dp"),
            P("dp", None),
            P("dp", None),
            P("dp"),
            P("dp"),
            P("dp", None),
            P("expert", "dp", None),
            P("expert", "dp"),
            P("expert", "dp", None),
        ),
        check_vma=False,
    )
```

profile of v0, /device:TPU:0, one launch (start us, length us, event | category | flops | bytes accessed | tf_op | source)
XLA Modules:
  0.0 1125.7 jit_solution(17531690787599900574)
XLA Ops:
  174.2 40.4 %all-to-all-done.2 = bf16[8,184,768]{2,1,0:T(8,128)(2,1)} async-done(((bf16[8,184,768]{2,1,0:T(8,128)(2,1)}), bf16[8,184,768]{2,1,0:T(8,128)(2,1)}, u32[]{:S(2)}, u32[]{:S(2)}) %all-to-all-start.2) | async-done | bytes 2261024 | tf_op jit(solution)/shard_map/all_to_all | solution.py:170
  256.9 11.7 %gather_fusion.6 = f32[1182]{0:T(1024)S(1)} fusion(f32[591,8]{0,1:T(8,128)S(1)} %fusion.108, s32[1182]{0:T(1024)S(1)} %reshape.662), kind=kCustom, calls=%fused_computation.clone | custom fusion | bytes 18912 | tf_op jit(solution)/shard_map/jit(take_along_axis)/gather | solution.py:165
  269.2 15.6 %scatter_custom_fusion.2 = f32[1473,768]{1,0:T(8,128)} fusion(s32[1182]{0:T(1024)} %copy-done.99, f32[1182,768]{1,0:T(8,128)} %mul.445, f32[]{:T(128)} %constant.50.clone.1, f32[1182]{0:T(1024)S(1)} %mul.442), kind=kCustom, calls=%fused_computation.92 | custom fusion | flops 907776 | bytes 8167544 | tf_op jit(solution)/shard_map/scatter | solution.py:203
  289.7 11.9 %gather_fusion.7 = f32[1182]{0:T(1024)S(1)} fusion(f32[591,8]{0,1:T(8,128)S(1)} %fusion.110, s32[1182]{0:T(1024)S(1)} %reshape.667), kind=kCustom, calls=%fused_computation.1.clone | custom fusion | bytes 18912 | tf_op jit(solution)/shard_map/jit(take_along_axis)/gather | solution.py:165
  302.1 15.6 %scatter_custom_fusion.3 = f32[1473,768]{1,0:T(8,128)} fusion(s32[1182]{0:T(1024)} %copy-done.97, f32[1182,768]{1,0:T(8,128)} %mul.477, f32[]{:T(128)} %constant.50.clone.1, f32[1182]{0:T(1024)S(1)} %mul.474), kind=kCustom, calls=%fused_computation.89 | custom fusion | flops 907776 | bytes 8167544 | tf_op jit(solution)/shard_map/scatter | solution.py:203
  321.6 13.6 %fusion.30 = f32[1472,3072]{1,0:T(8,128)} fusion(bf16[1472,768]{1,0:T(8,128)(2,1)} %bitcast.22, bf16[1,3072,768]{2,1,0:T(8,128)(2,1)} %all-gather.10.cloned.1.call-done), kind=kOutput, calls=%fused_computation.73 | convolution fusion | flops 6945767424 | bytes 25067520 | tf_op jit(solution)/shard_map/rd,fd->rf/dot_general | solution.py:24
  341.5 90.6 %multiply_convert_fusion.1 = (bf16[1472,3072]{1,0:T(8,128)(2,1)}, f32[1472,3072]{1,0:T(8,128)}, bf16[1472,3072]{1,0:T(8,128)(2,1)}, f32[1472,3072]{1,0:T(8,128)}, f32[1472,3072]{1,0:T(8,128)}) fusion(f32[3072]{0:T(1024)S(1)} %bitcast.220, f32[1472,3072]{1,0:T(8,128)} %fusion.30, bf16[1472,768]{1,0:T(8,128)(2,1)} %bitcast.9, ...), kind=kOutput, calls=%fused_computation.35 | convolution fusion | flops 7542669312 | bytes 97431552 | tf_op jit(solution)/shard_map/rd,fd->rf/dot_general | solution.py:24
  438.6 25.3 %convert_reduce_fusion.1 = (f32[3072]{0:T(1024)S(1)}, bf16[1472,3072]{1,0:T(8,128)(2,1)}) fusion(f32[1472,3072]{1,0:T(8,128)} %get-tuple-element.53, bf16[1472,768]{1,0:T(8,128)(2,1)} %bitcast.26, bf16[1,3072,768]{2,1,0:T(8,128)(2,1)} %all-gather.12.cloned.1.call-done, f32[1472,3072]{1,0:T(8,128)} %get-tuple-element.91, f32[3072]{0:T(1024)S(1)} %bitcast.221), kind=kOutput, calls=%fused_computation.19 | convolution fusion | flops 7022638080 | bytes 52224000 | tf_op jit(solution)/shard_map/rd,fd->rf/dot_general | solution.py:24
  464.0 10.7 fusion.42
  474.6 15.5 %all-to-all-done.6 = bf16[8,184,768]{2,1,0:T(8,128)(2,1)S(1)} async-done(((bf16[8,184,768]{2,1,0:T(8,128)(2,1)}), bf16[8,184,768]{2,1,0:T(8,128)(2,1)S(1)}, u32[]{:S(2)}, u32[]{:S(2)}) %all-to-all-start.6) | async-done | bytes 2261024 | tf_op jit(solution)/shard_map/all_to_all | solution.py:206
  495.2 12.0 %fusion.48 = bf16[1472,768]{1,0:T(8,128)(2,1)} fusion(bf16[1472,3072]{1,0:T(8,128)(2,1)} %get-tuple-element.52, bf16[1,3072,768]{2,1,0:T(8,128)(2,1)} %all-gather.12.cloned.1.call-done), kind=kOutput, calls=%fused_computation.98 | convolution fusion | flops 6946897920 | bytes 16023552 | tf_op jit(solution)/shard_map/dot_general | solution.py:20
  507.3 39.9 %all-to-all-done.5 = bf16[8,184,768]{2,1,0:T(8,128)(2,1)S(1)} async-done(((bf16[8,184,768]{2,1,0:T(8,128)(2,1)}), bf16[8,184,768]{2,1,0:T(8,128)(2,1)S(1)}, u32[]{:S(2)}, u32[]{:S(2)}) %all-to-all-start.5) | async-done | bytes 2261024 | tf_op jit(solution)/shard_map/all_to_all | solution.py:223
  551.7 25.2 %convert_reduce_fusion = (f32[3072]{0:T(1024)S(1)}, bf16[1472,3072]{1,0:T(8,128)(2,1)}) fusion(f32[1472,3072]{1,0:T(8,128)} %get-tuple-element.71, bf16[1472,768]{1,0:T(8,128)(2,1)} %bitcast.205, bf16[1,3072,768]{2,1,0:T(8,128)(2,1)} %all-gather.12.cloned.1.call-done, f32[1472,3072]{1,0:T(8,128)} %fusion.30, f32[3072]{0:T(1024)S(1)} %bitcast.222), kind=kOutput, calls=%fused_computation.18 | convolution fusion | flops 7022638080 | bytes 52224000 | tf_op jit(solution)/shard_map/rd,fd->rf/dot_general | solution.py:24
  576.9 12.0 %fusion.45 = bf16[1472,768]{1,0:T(8,128)(2,1)} fusion(bf16[1472,3072]{1,0:T(8,128)(2,1)} %get-tuple-element.107, bf16[1,3072,768]{2,1,0:T(8,128)(2,1)} %all-gather.10.cloned.1.call-done), kind=kOutput, calls=%fused_computation.97 | convolution fusion | flops 6946897920 | bytes 16023552 | tf_op jit(solution)/shard_map/dot_general | solution.py:20
  588.9 14.1 %all-to-all-done.1 = bf16[8,184,768]{2,1,0:T(8,128)(2,1)} async-done(((bf16[8,184,768]{2,1,0:T(8,128)(2,1)}), bf16[8,184,768]{2,1,0:T(8,128)(2,1)}, u32[]{:S(2)}, u32[]{:S(2)}) %all-to-all-start.1) | async-done | bytes 2261024 | tf_op jit(solution)/shard_map/all_to_all | solution.py:181
  607.4 12.1 %fusion.51 = bf16[1472,768]{1,0:T(8,128)(2,1)} fusion(bf16[1472,3072]{1,0:T(8,128)(2,1)} %get-tuple-element.70, bf16[1,3072,768]{2,1,0:T(8,128)(2,1)} %all-gather.12.cloned.1.call-done), kind=kOutput, calls=%fused_computation.99 | convolution fusion | flops 6946897920 | bytes 16023552 | tf_op jit(solution)/shard_map/dot_general | solution.py:20
  619.5 39.2 %all-to-all-done.7 = bf16[8,184,768]{2,1,0:T(8,128)(2,1)} async-done(((bf16[8,184,768]{2,1,0:T(8,128)(2,1)}), bf16[8,184,768]{2,1,0:T(8,128)(2,1)}, u32[]{:S(2)}, u32[]{:S(2)}) %all-to-all-start.7) | async-done | bytes 2261024 | tf_op jit(solution)/shard_map/all_to_all | solution.py:223
  864.8 13.1 %fusion.136 = f32[3072,768]{1,0:T(8,128)} fusion(bf16[1472,3072]{1,0:T(8,128)(2,1)} %get-tuple-element.105, bf16[1472,768]{1,0:T(8,128)(2,1)} %bitcast.9), kind=kOutput, calls=%fused_computation.290 | convolution fusion | flops 6945767424 | bytes 20742144 | tf_op jit(solution)/shard_map/rf,rd->fd/dot_general | solution.py:24
  879.7 13.7 %fusion.34 = bf16[1,3072,768]{2,1,0:T(8,128)(2,1)} fusion(f32[3072,768]{1,0:T(8,128)} %fusion.136, bf16[1472,3072]{1,0:T(8,128)(2,1)} %get-tuple-element.107, bf16[1472,768]{1,0:T(8,128)(2,1)} %bitcast.22), kind=kOutput, calls=%fused_computation.81 | convolution fusion | flops 6950486016 | bytes 25460736 | tf_op jit(solution)/shard_map/rf,rd->fd/dot_general | solution.py:24
  893.5 11.4 %fusion.137 = f32[3072,768]{1,0:T(8,128)S(1)} fusion(bf16[1472,3072]{1,0:T(8,128)(2,1)} %get-tuple-element.52, bf16[1472,768]{1,0:T(8,128)(2,1)} %bitcast.26), kind=kOutput, calls=%fused_computation.291 | convolution fusion | flops 6945767424 | bytes 20742144 | tf_op jit(solution)/shard_map/rf,rd->fd/dot_general | solution.py:24
  904.9 13.7 %fusion.35 = bf16[1,3072,768]{2,1,0:T(8,128)(2,1)} fusion(f32[3072,768]{1,0:T(8,128)S(1)} %fusion.137, bf16[1472,3072]{1,0:T(8,128)(2,1)} %get-tuple-element.70, bf16[1472,768]{1,0:T(8,128)(2,1)S(1)} %bitcast.206), kind=kOutput, calls=%fused_computation.82 | convolution fusion | flops 6950486016 | bytes 25460736 | tf_op jit(solution)/shard_map/rf,rd->fd/dot_general | solution.py:24
  955.4 22.1 %all-reduce.14 = (bf16[192]{0:T(256)(128)(2,1)S(1)}, bf16[192]{0:T(256)(128)(2,1)S(1)}, bf16[192]{0:T(256)(128)(2,1)S(1)}, bf16[192]{0:T(256)(128)(2,1)S(1)}, bf16[192,8]{0,1:T(8,128)(2,1)S(1)}) all-reduce(bf16[192]{0:T(256)(128)(2,1)S(1)} %dynamic-slice.5, ...), channel_id=1, replica_groups=mesh['dp'=4,'expert'=8] {'expert'}, use_global_device_ids=true, to_apply=%region_49.51 | all-reduce | flops 2304 | bytes 9216 | tf_op jit(solution)/shard_map/psum | solution.py:312
  983.2 47.2 %reduce-scatter.17.cloned.1.call-done = bf16[1,768,768]{2,1,0:T(8,128)(2,1)} async-done(((bf16[1,3072,768]{2,1,0:T(8,128)(2,1)}), bf16[1,768,768]{2,1,0:T(8,128)(2,1)}) %reduce-scatter.17.cloned.1.call-update) | async-done | bytes 1179664 | tf_op jit(solution)/shard_map/reduce_scatter | solution.py:321
  1033.2 81.4 %all-reduce.20.cloned.1.call-done = (bf16[192,2304]{1,0:T(8,128)(2,1)}, bf16[192,768]{1,0:T(8,128)(2,1)}) async-done(((bf16[192,2304]{1,0:T(8,128)(2,1)}, bf16[192,768]{1,0:T(8,128)(2,1)}), (bf16[192,2304]{1,0:T(8,128)(2,1)}, bf16[192,768]{1,0:T(8,128)(2,1)})) %all-reduce.20.cloned.1.call-update) | async-done | bytes 1179664 | tf_op jit(solution)/shard_map/psum | solution.py:309
  (543 shorter events, 500.0 us)
Async XLA Ops:
  7.2 41.3 %all-gather.6.cloned.1.call-start = ((), (), s32[]{:S(2)}) async-start(), calls=%async_computation.14 | async-start | bytes 4423680 | tf_op jit(solution)/shard_map/all_gather | solution.py:95
  7.9 135.8 %all-gather.8.cloned.1.call-start = ((), (), s32[]{:S(2)}) async-start(), calls=%async_computation.15 | async-start | bytes 1474560 | tf_op jit(solution)/shard_map/all_gather | solution.py:96
  8.7 312.9 %all-gather.10.cloned.1.call-start = ((), (), s32[]{:S(2)}) async-start(), calls=%async_computation.16 | async-start | bytes 5898240 | tf_op jit(solution)/shard_map/all_gather | solution.py:106
  12.9 242.6 %copy-start.66 = (s32[591,2]{0,1:T(2,128)}, s32[591,2]{0,1:T(2,128)S(1)}, u32[]{:S(2)}) copy-start(s32[591,2]{0,1:T(2,128)S(1)} %reshape.498) | copy-start | bytes 14188
  36.8 111.8 %copy-start.71 = (f32[768]{0:T(1024)}, f32[768]{0:T(1024)S(1)}, u32[]{:S(2)}) copy-start(f32[768]{0:T(1024)S(1)} %convert_element_type.254) | copy-start | bytes 9220
  38.6 108.6 %copy-start.17 = (f32[591,768]{1,0:T(8,128)}, f32[591,768]{1,0:T(8,128)S(1)}, u32[]{:S(2)}) copy-start(f32[591,768]{1,0:T(8,128)S(1)} %reshape.493) | copy-start | bytes 5446660
  38.8 230.3 %copy-start.69 = (s32[591,2]{0,1:T(2,128)}, s32[591,2]{0,1:T(2,128)S(1)}, u32[]{:S(2)}) copy-start(s32[591,2]{0,1:T(2,128)S(1)} %reshape.486) | copy-start | bytes 14188
  149.5 139.1 %copy-start.4 = (bf16[591,768]{1,0:T(8,128)(2,1)}, bf16[591,768]{1,0:T(8,128)(2,1)S(1)}, u32[]{:S(2)}) copy-start(bf16[591,768]{1,0:T(8,128)(2,1)S(1)} %get-tuple-element.75) | copy-start | bytes 2723332
  158.4 56.2 %all-to-all-start.2 = ((bf16[8,184,768]{2,1,0:T(8,128)(2,1)}), bf16[8,184,768]{2,1,0:T(8,128)(2,1)}, u32[]{:S(2)}, u32[]{:S(2)}) async-start(bf16[8,184,768]{2,1,0:T(8,128)(2,1)} %broadcast_select_fusion), calls=%async_computation.2 | async-start | bytes 4521984 | tf_op jit(solution)/shard_map/all_to_all | solution.py:170
  164.2 274.4 %all-gather.12.cloned.1.call-start = ((), (), s32[]{:S(2)}) async-start(), calls=%async_computation.17 | async-start | bytes 5898240 | tf_op jit(solution)/shard_map/all_gather | solution.py:107
  214.5 120.7 %all-to-all-start = ((bf16[8,184,768]{2,1,0:T(8,128)(2,1)}), bf16[8,184,768]{2,1,0:T(8,128)(2,1)}, u32[]{:S(2)}, u32[]{:S(2)}) async-start(bf16[8,184,768]{2,1,0:T(8,128)(2,1)} %broadcast_select_fusion.1), calls=%async_computation | async-start | bytes 4521984 | tf_op jit(solution)/shard_map/all_to_all | solution.py:170
  335.2 96.9 %all-to-all-start.4 = ((bf16[8,184,768]{2,1,0:T(8,128)(2,1)}), bf16[8,184,768]{2,1,0:T(8,128)(2,1)}, u32[]{:S(2)}, u32[]{:S(2)}) async-start(bf16[8,184,768]{2,1,0:T(8,128)(2,1)} %bitcast.25), calls=%async_computation.4 | async-start | bytes 4521984 | tf_op jit(solution)/shard_map/all_to_all | solution.py:206
  432.1 58.0 %all-to-all-start.6 = ((bf16[8,184,768]{2,1,0:T(8,128)(2,1)}), bf16[8,184,768]{2,1,0:T(8,128)(2,1)S(1)}, u32[]{:S(2)}, u32[]{:S(2)}) async-start(bf16[8,184,768]{2,1,0:T(8,128)(2,1)} %bitcast.33), calls=%async_computation.6 | async-start | bytes 4521984 | tf_op jit(solution)/shard_map/all_to_all | solution.py:206
  491.6 55.6 %all-to-all-start.5 = ((bf16[8,184,768]{2,1,0:T(8,128)(2,1)}), bf16[8,184,768]{2,1,0:T(8,128)(2,1)S(1)}, u32[]{:S(2)}, u32[]{:S(2)}) async-start(bf16[8,184,768]{2,1,0:T(8,128)(2,1)} %bitcast.210), calls=%async_computation.5 | async-start | bytes 4521984 | tf_op jit(solution)/shard_map/all_to_all | solution.py:223
  547.2 55.9 %all-to-all-start.1 = ((bf16[8,184,768]{2,1,0:T(8,128)(2,1)}), bf16[8,184,768]{2,1,0:T(8,128)(2,1)}, u32[]{:S(2)}, u32[]{:S(2)}) async-start(bf16[8,184,768]{2,1,0:T(8,128)(2,1)} %bitcast.208), calls=%async_computation.1 | async-start | bytes 4521984 | tf_op jit(solution)/shard_map/all_to_all | solution.py:181
  603.0 55.7 %all-to-all-start.7 = ((bf16[8,184,768]{2,1,0:T(8,128)(2,1)}), bf16[8,184,768]{2,1,0:T(8,128)(2,1)}, u32[]{:S(2)}, u32[]{:S(2)}) async-start(bf16[8,184,768]{2,1,0:T(8,128)(2,1)} %bitcast.209), calls=%async_computation.7 | async-start | bytes 4521984 | tf_op jit(solution)/shard_map/all_to_all | solution.py:223
  658.7 69.3 %all-to-all-start.3 = ((bf16[8,184,768]{2,1,0:T(8,128)(2,1)}), bf16[8,184,768]{2,1,0:T(8,128)(2,1)}, u32[]{:S(2)}, u32[]{:S(2)}) async-start(bf16[8,184,768]{2,1,0:T(8,128)(2,1)} %bitcast.207), calls=%async_computation.3 | async-start | bytes 4521984 | tf_op jit(solution)/shard_map/all_to_all | solution.py:181
  663.1 256.7 %reduce-scatter.21.cloned.1.call-start = ((), (), s32[]{:S(2)}) async-start(), calls=%async_computation.23 | async-start | bytes 983040
  664.5 278.6 %reduce-scatter.13.cloned.1.call-start = ((), (), s32[]{:S(2)}) async-start(), calls=%async_computation.19 | async-start | bytes 1474560 | tf_op jit(solution)/shard_map/reduce_scatter | solution.py:280
  825.7 117.5 %reduce-scatter.11.cloned.1.call-start = ((), (), s32[]{:S(2)}) async-start(), calls=%async_computation.18 | async-start | bytes 4423680 | tf_op jit(solution)/shard_map/reduce_scatter | solution.py:277
  864.7 89.8 %reduce-scatter.19.cloned.1.call-start = ((), (), s32[]{:S(2)}) async-start(), calls=%async_computation.22 | async-start | bytes 245760
  879.7 100.7 %reduce-scatter.15.cloned.1.call-start = ((), (), s32[]{:S(2)}) async-start(), calls=%async_computation.20 | async-start | bytes 5898240 | tf_op jit(solution)/shard_map/reduce_scatter | solution.py:318
  893.5 136.9 %reduce-scatter.17.cloned.1.call-start = ((), (), s32[]{:S(2)}) async-start(), calls=%async_computation.21 | async-start | bytes 5898240 | tf_op jit(solution)/shard_map/reduce_scatter | solution.py:321
  918.7 196.0 %all-reduce.20.cloned.1.call-start = ((), (), s32[]{:S(2)}) async-start(), calls=%async_computation.24 | async-start | bytes 2359296 | tf_op jit(solution)/shard_map/psum | solution.py:309
  (123 other events, 1284.8 us)
Sparse Core Ops, SparseCore 0:
  9.6 33.7 all-gather.5
  44.9 17.4 all-gather.7
  64.0 37.4 all-gather.9
  166.3 37.9 all-gather.11
  666.1 24.6 reduce-scatter.20
  825.8 27.0 reduce-scatter.12
  864.8 41.7 reduce-scatter.10
  909.8 19.7 reduce-scatter.18
  932.2 47.8 reduce-scatter.14
  982.5 47.8 reduce-scatter.16
  1034.3 80.3 all-reduce.19
where the time goes:
time: 1140 us; the launch traced here: 1130 us
  matrix products  364 us (32%)
  waiting for transfers between devices  281 us (25%)
  local copies, waits for them, and re-layouts  257 us (23%)
  other arithmetic  119 us (10%)
  blocking collectives  47.4 us (4%)
  starting transfers between devices  40.5 us (4%)
  between operations  17.6 us (2%)
    dot_general x26, matrix products, contract(): jnp.einsum(formula, left_side, right_side, preferred_element_type=jnp.flo...  278 us
    psum x1, waiting for transfers between devices, per_device(): lax.psum(owned_attn_in.astype(jnp.bfloat16), 'expert').astype(jnp.float32)  81.4 us
    all_to_all x2, waiting for transfers between devices, per_device(): lax.all_to_all(grad_dispatched.reshape(experts, capacity, features), 'exp...  79.1 us
    dot_general x10, matrix products, matmul(): return jnp.dot(left_side, right_side, preferred_element_type=jnp.float32)  61.4 us
    reduce_scatter x1, waiting for transfers between devices, per_device(): lax.psum_scatter(total(acc_expert_out)[None].astype(jnp.bfloat16), 'dp',...  47.2 us
    all_to_all x2, waiting for transfers between devices, per_device(): lax.all_to_all(dispatched.reshape(experts, capacity, features), 'expert',...  40.4 us
    scatter x2, other arithmetic, per_device(): grad_slots = jnp.zeros((experts * capacity + 1, features), jnp.float32).a...  31.1 us
    gather x10, local copies, waits for them, and re-layouts, per_device(): gate_values = jnp.take_along_axis(router_probs, route_block, axis=1)  25.1 us
  transfers between devices with their start and end apart: 19, of which 7 were waited for; matrix products, arithmetic and copies ran while one was open for 65% of the time, Pallas kernels for 0%

commit v1 on v0

v1 whole, which is shorter than its diff:
```python
import functools

import jax
import jax.numpy as jnp
from jax import lax
from jax.experimental import pallas as pl
from jax.experimental.pallas import tpu as pltpu
from jax.sharding import PartitionSpec as P

HEADS = 12
HEAD_DIM = 64
SEQ = 197
MICRO = 2
IMG_MB = 3
TOP = 2
LANES = 128
VMEM_LIMIT = 60 * 1024 * 1024

epsilon = 1e-06
f32 = jnp.float32
bf16 = jnp.bfloat16


def params(semantics, **more):
    return pltpu.CompilerParams(
        dimension_semantics=semantics, vmem_limit_bytes=VMEM_LIMIT, **more
    )


def dot(left, right):
    return lax.dot_general(
        left, right, (((1,), (0,)), ((), ())), preferred_element_type=f32
    )


def dot_t(left, right):
    return lax.dot_general(
        left, right, (((1,), (1,)), ((), ())), preferred_element_type=f32
    )


def t_dot(left, right):
    return lax.dot_general(
        left, right, (((0,), (0,)), ((), ())), preferred_element_type=f32
    )


def norm_forward(values):
    row_mean = jnp.mean(values, axis=-1, keepdims=True)
    centred = values - row_mean
    row_var = jnp.mean(centred * centred, axis=-1, keepdims=True)
    inverse = lax.rsqrt(row_var + epsilon)
    return centred * inverse, inverse


def norm_backward(grad_normed, normed, inverse):
    mean_grad = jnp.mean(grad_normed, axis=-1, keepdims=True)
    mean_cross = jnp.mean(grad_normed * normed, axis=-1, keepdims=True)
    return inverse * (grad_normed - mean_grad - normed * mean_cross)


def softmax_lanes(logits, count):
    lane = lax.broadcasted_iota(jnp.int32, logits.shape, 1)
    masked = jnp.where(lane < count, logits, -1e30)
    top = jnp.max(masked, axis=-1, keepdims=True)
    raised = jnp.where(lane < count, jnp.exp(masked - top), 0.0)
    return raised / jnp.sum(raised, axis=-1, keepdims=True)


def gelu_both(values):
    size = jnp.abs(values)
    bell = jnp.exp(values * values * -0.5)
    t = 1.0 / (1.0 + (0.3275911 * 0.7071067811865476) * size)
    tail = t * (
        0.5 * 0.254829592
        + t
        * (
            0.5 * -0.284496736
            + t * (0.5 * 1.421413741 + t * (0.5 * -1.453152027 + t * (0.5 * 1.061405429)))
        )
    )
    tail = tail * bell
    phi = jnp.where(values >= 0, 1.0 - tail, tail)
    return values * phi, phi + values * (0.3989422804014327 * bell)


def route_kernel(experts, capacity, routes_ref, slots_ref):
    seq = routes_ref.shape[1]
    row = lax.broadcasted_iota(jnp.int32, (seq, seq), 0)
    col = lax.broadcasted_iota(jnp.int32, (seq, seq), 1)
    earlier = (col < row).astype(f32).astype(bf16)
    lane = lax.broadcasted_iota(jnp.int32, (seq, LANES), 1)
    groups = routes_ref.shape[0] // IMG_MB
    for group in range(groups):
        base = jnp.zeros((1, LANES), f32)
        for choice in range(TOP):
            for image in range(IMG_MB):
                index = group * IMG_MB + image
                named = routes_ref[index][:, choice : choice + 1]
                onehot = (lane == named).astype(f32)
                count = dot(earlier, onehot.astype(bf16)) + base
                position = jnp.sum(onehot * count, axis=1, keepdims=True).astype(jnp.int32)
                base = base + jnp.sum(onehot, axis=0, keepdims=True)
                slot = jnp.where(position < capacity, named * capacity + position, -1)
                slots_ref[index, :, choice : choice + 1] = slot


def route(routes, experts, capacity):
    return pl.pallas_call(
        functools.partial(route_kernel, experts, capacity),
        out_shape=jax.ShapeDtypeStruct(routes.shape, jnp.int32),
        compiler_params=pltpu.CompilerParams(vmem_limit_bytes=VMEM_LIMIT),
        cost_estimate=pl.CostEstimate(
            flops=10**8, bytes_accessed=2 * 10**6, transcendentals=0
        ),
        name="route",
    )(routes)


def dispatch_kernel(capacity, slots_ref, rows_ref, out_ref):
    first = pl.program_id(0) * capacity
    seq = rows_ref.shape[1]
    column = lax.broadcasted_iota(jnp.int32, (seq, capacity), 1) + first
    acc = jnp.zeros((capacity, rows_ref.shape[2]), f32)
    for image in range(IMG_MB):
        slots = slots_ref[image]
        holds = (slots[:, 0:1] == column) | (slots[:, 1:2] == column)
        acc = acc + t_dot(holds.astype(f32).astype(bf16), rows_ref[image])
    out_ref[0] = acc.astype(bf16)


def dispatch(slots, rows, group, experts, capacity):
    seq, features = rows.shape[1:]
    return pl.pallas_call(
        functools.partial(dispatch_kernel, capacity),
        grid=(experts,),
        in_specs=[
            pl.BlockSpec((IMG_MB, seq, TOP), lambda e: (group, 0, 0)),
            pl.BlockSpec((IMG_MB, seq, features), lambda e: (group, 0, 0)),
        ],
        out_specs=pl.BlockSpec((1, capacity, features), lambda e: (e, 0, 0)),
        out_shape=jax.ShapeDtypeStruct((experts, capacity, features), bf16),
        compiler_params=params(("arbitrary",)),
        cost_estimate=pl.CostEstimate(
            flops=2 * experts * capacity * IMG_MB * seq * features,
            bytes_accessed=2 * features * (experts * capacity + IMG_MB * seq),
            transcendentals=0,
        ),
        name="dispatch",
    )(slots, rows)


def attend_kernel(
    experts, x_ref, routes_ref, win_ref, wout_ref, small_ref,
    proj_ref, mixed_ref, residual_ref, hidden_ref, gates_ref,
):
    features = x_ref.shape[2]
    image = x_ref[0].astype(f32)
    vectors = small_ref[...].astype(f32)
    normed, _ = norm_forward(image)
    attn_input = (
        normed * vectors[experts : experts + 1] + vectors[experts + 1 : experts + 2]
    ).astype(bf16)
    proj_ref[0] = dot(attn_input, win_ref[...]).astype(bf16)
    low_half = lax.broadcasted_iota(jnp.int32, (1, LANES), 1) < HEAD_DIM
    for pair in range(features // LANES):
        first = pair * LANES
        queries = proj_ref[0, :, first : first + LANES]
        keys = proj_ref[0, :, features + first : features + first + LANES]
        values = proj_ref[0, :, 2 * features + first : 2 * features + first + LANES]
        out = None
        for half in range(2):
            keep = low_half if half == 0 else jnp.logical_not(low_half)
            scores = dot_t(
                jnp.where(keep, queries * HEAD_DIM ** (-0.5), 0).astype(bf16), keys
            )
            top = jnp.max(scores, axis=-1, keepdims=True)
            raised = jnp.exp(scores - top)
            share = 1.0 / jnp.sum(raised, axis=-1, keepdims=True)
            weights = (raised * share).astype(bf16)
            part = dot(weights, jnp.where(keep, values, 0).astype(bf16))
            out = part if out is None else out + part
        mixed_ref[0, :, first : first + LANES] = out.astype(bf16)
    residual = image + dot(mixed_ref[0], wout_ref[...])
    residual_ref[0] = residual
    normed, _ = norm_forward(residual)
    hidden = (
        normed * vectors[experts + 2 : experts + 3] + vectors[experts + 3 : experts + 4]
    ).astype(bf16)
    hidden_ref[0] = hidden
    probs = softmax_lanes(dot_t(hidden, small_ref[...]), experts)
    lane = lax.broadcasted_iota(jnp.int32, probs.shape, 1)
    routes = routes_ref[0]
    for choice in range(TOP):
        gates_ref[0, :, choice : choice + 1] = jnp.sum(
            jnp.where(lane == routes[:, choice : choice + 1], probs, 0.0),
            axis=1,
            keepdims=True,
        )


def attend(images, routes, attn_in, attn_out, small, experts, group):
    seq, features = images.shape[1:]
    wide = attn_in.shape[1]
    first = group * IMG_MB

    def rows(width):
        return pl.BlockSpec((1, seq, width), lambda i: (i, 0, 0))

    def source(width):
        return pl.BlockSpec((1, seq, width), lambda i: (first + i, 0, 0))

    def whole(array):
        return pl.BlockSpec(array.shape, lambda i: (0, 0))

    def out(width, dtype):
        return jax.ShapeDtypeStruct((IMG_MB, seq, width), dtype)

    return pl.pallas_call(
        functools.partial(attend_kernel, experts),
        grid=(IMG_MB,),
        in_specs=[
            source(features),
            source(TOP),
            whole(attn_in),
            whole(attn_out),
            whole(small),
        ],
        out_specs=[rows(wide), rows(features), rows(features), rows(features), rows(TOP)],
        out_shape=[
            out(wide, bf16),
            out(features, bf16),
            out(features, f32),
            out(features, bf16),
            out(TOP, f32),
        ],
        compiler_params=params(("arbitrary",)),
        cost_estimate=pl.CostEstimate(
            flops=IMG_MB * seq * 16 * features * features,
            bytes_accessed=4 * features * (4 * features + IMG_MB * seq * 8),
            transcendentals=IMG_MB * HEADS * seq * seq,
        ),
        name="attend",
    )(images, routes, attn_in, attn_out, small)


def expert_kernel(
    experts, chunk, add, mine_ref, x_ref, g_ref, w1_ref, w2_ref, bias_ref, small_ref, *refs
):
    if add:
        old_w1_ref, old_w2_ref, old_bias_ref, old_router_ref = refs[:4]
        refs = refs[4:]
    (
        result_ref, dx_ref, dw1_ref, dw2_ref, dbias_ref, drouter_ref,
        result_acc, dx_acc, dr_ref, probs_ref, act_ref, pre_ref,
    ) = refs
    step = pl.program_id(0)
    last = pl.num_programs(0) - 1
    rows = x_ref.shape[0]
    mine = mine_ref[0]
    chunks = rows // chunk

    @pl.when(step == 0)
    def _():
        for index in range(chunks):
            at = pl.ds(index * chunk, chunk)
            probs = softmax_lanes(dot_t(x_ref[at, :], small_ref[...]), experts)
            lane = lax.broadcasted_iota(jnp.int32, probs.shape, 1)
            probs_ref[at, :] = probs
            gate = jnp.sum(jnp.where(lane == mine, probs, 0.0), axis=1, keepdims=True)
            dr_ref[at, :] = (gate * g_ref[at, :].astype(f32)).astype(bf16)
            result_acc[at, :] = jnp.zeros((chunk, x_ref.shape[1]), f32)
            dx_acc[at, :] = jnp.zeros((chunk, x_ref.shape[1]), f32)

    w1 = w1_ref[...]
    w2 = w2_ref[...]
    bias = bias_ref[...].astype(f32)
    dbias = jnp.zeros(bias.shape, f32)
    for index in range(chunks):
        at = pl.ds(index * chunk, chunk)
        act, slope = gelu_both(dot_t(x_ref[at, :], w1) + bias)
        act = act.astype(bf16)
        act_ref[at, :] = act
        result_acc[at, :] += dot(act, w2)
        grad_pre = (dot_t(dr_ref[at, :], w2) * slope).astype(bf16)
        pre_ref[at, :] = grad_pre
        dbias = dbias + jnp.sum(grad_pre.astype(f32), axis=0, keepdims=True)
        dx_acc[at, :] += dot(grad_pre, w1)
    dw1 = t_dot(pre_ref[...], x_ref[...])
    dw2 = t_dot(act_ref[...], dr_ref[...])
    if add:
        dw1 = dw1 + old_w1_ref[...]
        dw2 = dw2 + old_w2_ref[...]
        dbias = dbias + old_bias_ref[...]
    dw1_ref[...] = dw1.astype(dw1_ref.dtype)
    dw2_ref[...] = dw2.astype(dw2_ref.dtype)
    dbias_ref[...] = dbias

    @pl.when(step == last)
    def _():
        drouter = jnp.zeros(drouter_ref.shape, f32)
        if add:
            drouter = old_router_ref[...]
        for index in range(chunks):
            at = pl.ds(index * chunk, chunk)
            result = result_acc[at, :].astype(bf16)
            result_ref[at, :] = result
            grad_gate = jnp.sum(
                g_ref[at, :].astype(f32) * result.astype(f32), axis=1, keepdims=True
            )
            probs = probs_ref[at, :]
            lane = lax.broadcasted_iota(jnp.int32, probs.shape, 1)
            chosen = lane == mine
            gate = jnp.sum(jnp.where(chosen, probs, 0.0), axis=1, keepdims=True)
            logits = (grad_gate * gate) * (chosen.astype(f32) - probs)
            high = logits.astype(bf16)
            low = (logits - high.astype(f32)).astype(bf16)
            dx_ref[at, :] = (
                dx_acc[at, :] + dot(high, small_ref[...]) + dot(low, small_ref[...])
            ).astype(bf16)
            drouter = drouter + t_dot(high, x_ref[at, :]) + t_dot(low, x_ref[at, :])
        drouter_ref[...] = drouter


def row_chunk(rows):
    best = rows
    for size in range(16, 513, 16):
        if rows % size == 0:
            best = size
    return best


def expert_block(mine, x, g, w1, w2, bias, small, experts, old):
    rows, features = x.shape
    hidden_units = w1.shape[0]
    block = 256
    steps = hidden_units // block
    chunk = row_chunk(rows)
    add = old is not None
    out_type = bf16 if add else f32

    def whole(shape):
        return pl.BlockSpec(shape, lambda s: (0,) * len(shape))

    units = pl.BlockSpec((block, features), lambda s: (s, 0))
    unit_row = pl.BlockSpec((1, block), lambda s: (0, s))
    in_specs = [
        pl.BlockSpec(memory_space=pltpu.SMEM),
        whole(x.shape),
        whole(g.shape),
        units,
        units,
        unit_row,
        whole(small.shape),
    ]
    operands = [mine, x, g, w1, w2, bias, small]
    if add:
        in_specs += [units, units, unit_row, whole(small.shape)]
        operands += list(old)
    return pl.pallas_call(
        functools.partial(expert_kernel, experts, chunk, add),
        grid=(steps,),
        in_specs=in_specs,
        out_specs=[
            whole(x.shape), whole(x.shape), units, units, unit_row, whole(small.shape)
        ],
        out_shape=[
            jax.ShapeDtypeStruct(x.shape, bf16),
            jax.ShapeDtypeStruct(x.shape, bf16),
            jax.ShapeDtypeStruct(w1.shape, out_type),
            jax.ShapeDtypeStruct(w2.shape, out_type),
            jax.ShapeDtypeStruct((1, hidden_units), f32),
            jax.ShapeDtypeStruct(small.shape, f32),
        ],
        scratch_shapes=[
            pltpu.VMEM((rows, features), f32),
            pltpu.VMEM((rows, features), f32),
            pltpu.VMEM((rows, features), bf16),
            pltpu.VMEM((rows, small.shape[0]), f32),
            pltpu.VMEM((rows, block), bf16),
            pltpu.VMEM((rows, block), bf16),
        ],
        compiler_params=params(("arbitrary",)),
        cost_estimate=pl.CostEstimate(
            flops=12 * rows * features * hidden_units,
            bytes_accessed=(8 * rows + 12 * hidden_units) * features,
            transcendentals=rows * hidden_units,
        ),
        name="expert_block",
    )(*operands)


def combine_kernel(slots_ref, gates_ref, residual_ref, returned_ref, out_ref):
    seq = slots_ref.shape[1]
    total = returned_ref.shape[0]
    column = lax.broadcasted_iota(jnp.int32, (seq, total), 1)
    slots = slots_ref[0]
    gates = gates_ref[0]
    value = residual_ref[0]
    mix = None
    for choice in range(TOP):
        holds = slots[:, choice : choice + 1] == column
        picked = dot(holds.astype(f32).astype(bf16), returned_ref[...])
        part = gates[:, choice : choice + 1] * picked
        mix = part if mix is None else mix + part
    out_ref[0] = (value + mix).astype(bf16)


def combine(slots, gates, residual, returned, group):
    seq, features = residual.shape[1:]
    first = group * IMG_MB
    return pl.pallas_call(
        combine_kernel,
        grid=(IMG_MB,),
        in_specs=[
            pl.BlockSpec((1, seq, TOP), lambda i: (first + i, 0, 0)),
            pl.BlockSpec((1, seq, TOP), lambda i: (i, 0, 0)),
            pl.BlockSpec((1, seq, features), lambda i: (i, 0, 0)),
            pl.BlockSpec(returned.shape, lambda i: (0, 0)),
        ],
        out_specs=pl.BlockSpec((1, seq, features), lambda i: (i, 0, 0)),
        out_shape=jax.ShapeDtypeStruct(residual.shape, bf16),
        compiler_params=params(("arbitrary",)),
        cost_estimate=pl.CostEstimate(
            flops=4 * IMG_MB * seq * returned.shape[0] * features,
            bytes_accessed=2 * features * (returned.shape[0] + 3 * IMG_MB * seq),
            transcendentals=0,
        ),
        name="combine",
    )(slots, gates, residual, returned)


def attend_back_kernel(
    experts, add, x_ref, top_ref, slots_ref, sent_ref, proj_ref, mixed_ref, residual_ref,
    win_ref, wout_ref, small_ref, *refs
):
    if add:
        old_in_ref, old_out_ref, old_small_ref = refs[:3]
        refs = refs[3:]
    (grad_x_ref, dwin_ref, dwout_ref, dsmall_ref, acc_in, acc_out, acc_small, dproj_ref) = refs
    features = x_ref.shape[2]
    seq = x_ref.shape[1]
    step = pl.program_id(0)
    vectors = small_ref[...].astype(f32)

    @pl.when(step == 0)
    def _():
        if add:
            acc_in[...] = old_in_ref[...]
            acc_out[...] = old_out_ref[...]
            acc_small[...] = old_small_ref[...]
        else:
            acc_in[...] = jnp.zeros(acc_in.shape, f32)
            acc_out[...] = jnp.zeros(acc_out.shape, f32)
            acc_small[...] = jnp.zeros(acc_small.shape, f32)

    column = lax.broadcasted_iota(jnp.int32, (seq, sent_ref.shape[0]), 1)
    slots = slots_ref[0]
    holds = (slots[:, 0:1] == column) | (slots[:, 1:2] == column)
    grad_hidden = dot(holds.astype(f32).astype(bf16), sent_ref[...])
    normed_two, inverse_two = norm_forward(residual_ref[0])
    acc_small[2:3, :] += jnp.sum(grad_hidden * normed_two, axis=0, keepdims=True)
    acc_small[3:4, :] += jnp.sum(grad_hidden, axis=0, keepdims=True)
    grad_residual = top_ref[0].astype(f32) + norm_backward(
        grad_hidden * vectors[experts + 2 : experts + 3], normed_two, inverse_two
    )
    grad_branch = grad_residual.astype(bf16)
    acc_out[...] += t_dot(mixed_ref[0], grad_branch)
    grad_mixed = dot_t(grad_branch, wout_ref[...]).astype(bf16)
    low_half = lax.broadcasted_iota(jnp.int32, (1, LANES), 1) < HEAD_DIM
    scale = HEAD_DIM ** (-0.5)
    for pair in range(features // LANES):
        first = pair * LANES
        queries = proj_ref[0, :, first : first + LANES]
        keys = proj_ref[0, :, features + first : features + first + LANES]
        values = proj_ref[0, :, 2 * features + first : 2 * features + first + LANES]
        grad_out = grad_mixed[:, first : first + LANES]
        sums = [None, None, None]
        for half in range(2):
            keep = low_half if half == 0 else jnp.logical_not(low_half)
            head_queries = jnp.where(keep, queries * scale, 0).astype(bf16)
            head_keys = jnp.where(keep, keys, 0).astype(bf16)
            head_grad = jnp.where(keep, grad_out, 0).astype(bf16)
            scores = dot_t(keys, head_queries)
            top = jnp.max(scores, axis=0, keepdims=True)
            raised = jnp.exp(scores - top)
            probs = raised * (1.0 / jnp.sum(raised, axis=0, keepdims=True))
            grad_values = dot(probs.astype(bf16), head_grad)
            grad_weights = dot_t(values, head_grad)
            inner = jnp.sum(grad_weights * probs, axis=0, keepdims=True)
            grad_scores = (probs * (grad_weights - inner)).astype(bf16)
            grad_keys = dot(grad_scores, head_queries)
            grad_queries = t_dot(grad_scores, head_keys)
            for place, part in enumerate((grad_queries, grad_keys, grad_values)):
                sums[place] = part if half == 0 else sums[place] + part
        dproj_ref[:, first : first + LANES] = (sums[0] * scale).astype(bf16)
        dproj_ref[:, features + first : features + first + LANES] = sums[1].astype(bf16)
        dproj_ref[:, 2 * features + first : 2 * features + first + LANES] = sums[2].astype(bf16)
    normed_one, inverse_one = norm_forward(x_ref[0].astype(f32))
    attn_input = (
        normed_one * vectors[experts : experts + 1] + vectors[experts + 1 : experts + 2]
    ).astype(bf16)
    acc_in[...] += t_dot(attn_input, dproj_ref[...])
    grad_input = dot_t(dproj_ref[...], win_ref[...])
    acc_small[0:1, :] += jnp.sum(grad_input * normed_one, axis=0, keepdims=True)
    acc_small[1:2, :] += jnp.sum(grad_input, axis=0, keepdims=True)
    grad_x_ref[0] = grad_residual + norm_backward(
        grad_input * vectors[experts : experts + 1], normed_one, inverse_one
    )

    @pl.when(step == pl.num_programs(0) - 1)
    def _():
        dwin_ref[...] = acc_in[...].astype(dwin_ref.dtype)
        dwout_ref[...] = acc_out[...].astype(dwout_ref.dtype)
        dsmall_ref[...] = acc_small[...]


def attend_back(
    images, out_grad, slots, sent, proj, mixed, residual, attn_in, attn_out, small,
    experts, group, old,
):
    seq, features = images.shape[1:]
    wide = attn_in.shape[1]
    first = group * IMG_MB
    add = old is not None
    out_type = bf16 if add else f32

    def rows(width):
        return pl.BlockSpec((1, seq, width), lambda i: (i, 0, 0))

    def source(width):
        return pl.BlockSpec((1, seq, width), lambda i: (first + i, 0, 0))

    def whole(shape):
        return pl.BlockSpec(shape, lambda i: (0, 0))

    small_grads = (8, features)
    in_specs = [
        source(features), source(features), source(TOP), whole(sent.shape),
        rows(wide), rows(features), rows(features),
        whole(attn_in.shape), whole(attn_out.shape), whole(small.shape),
    ]
    operands = [
        images, out_grad, slots, sent, proj, mixed, residual, attn_in, attn_out, small
    ]
    if add:
        in_specs += [whole(attn_in.shape), whole(attn_out.shape), whole(small_grads)]
        operands += list(old)
    return pl.pallas_call(
        functools.partial(attend_back_kernel, experts, add),
        grid=(IMG_MB,),
        in_specs=in_specs,
        out_specs=[
            rows(features), whole(attn_in.shape), whole(attn_out.shape), whole(small_grads)
        ],
        out_shape=[
            jax.ShapeDtypeStruct((IMG_MB, seq, features), f32),
            jax.ShapeDtypeStruct(attn_in.shape, out_type),
            jax.ShapeDtypeStruct(attn_out.shape, out_type),
            jax.ShapeDtypeStruct(small_grads, f32),
        ],
        scratch_shapes=[
            pltpu.VMEM(attn_in.shape, f32),
            pltpu.VMEM(attn_out.shape, f32),
            pltpu.VMEM(small_grads, f32),
            pltpu.VMEM((seq, wide), bf16),
        ],
        compiler_params=params(("arbitrary",)),
        cost_estimate=pl.CostEstimate(
            flops=IMG_MB * seq * 40 * features * features,
            bytes_accessed=8 * features * (4 * features + IMG_MB * seq * 4),
            transcendentals=IMG_MB * HEADS * seq * seq,
        ),
        name="attend_back",
    )(*operands)


def per_device(
    images, first_gain, first_shift, attn_in, attn_out, second_gain, second_shift, router,
    expert_in, expert_bias, expert_out, routes, out_grad,
):
    features = images.shape[2]
    experts = router.shape[1]
    tok_mb = IMG_MB * SEQ
    capacity = max(2, (5 * TOP * tok_mb // (4 * experts) + 7) // 8 * 8)
    slot_rows = experts * capacity
    micro = images.shape[0] // IMG_MB
    small_rows = (experts + 4 + 15) // 16 * 16

    small = jnp.concatenate(
        [
            router.T,
            first_gain[None],
            first_shift[None],
            second_gain[None],
            second_shift[None],
            jnp.zeros((small_rows - experts - 4, router.shape[0]), bf16),
        ],
        axis=0,
    )
    small = lax.all_gather(small, "dp", axis=1, tiled=True)
    attn_in_full = lax.all_gather(attn_in, "dp", axis=0, tiled=True)
    attn_out_full = lax.all_gather(attn_out, "dp", axis=0, tiled=True)
    weight_in = lax.all_gather(expert_in[0], "dp", axis=0, tiled=True)
    weight_out = lax.all_gather(expert_out[0], "dp", axis=0, tiled=True)
    bias_row = lax.all_gather(expert_bias, "dp", axis=1, tiled=True)
    mine = lax.axis_index("expert").astype(jnp.int32)[None]

    def exchange(rows):
        return lax.all_to_all(
            rows.reshape(experts, capacity, features),
            "expert",
            split_axis=0,
            concat_axis=0,
            tiled=True,
        )

    slots = route(routes, experts, capacity)
    grads = [
        exchange(dispatch(slots, out_grad, group, experts, capacity)).reshape(slot_rows, features)
        for group in range(micro)
    ]
    saved = []
    received = []
    for group in range(micro):
        proj, mixed, residual, hidden, gates = attend(
            images, routes, attn_in_full, attn_out_full, small, experts, group
        )
        saved.append((proj, mixed, residual, gates))
        rows = dispatch(slots[group * IMG_MB : (group + 1) * IMG_MB], hidden, 0, experts, capacity)
        received.append(exchange(rows).reshape(slot_rows, features))
    old = None
    returned = []
    sent = []
    for group in range(micro):
        result, dx, *old = expert_block(
            mine, received[group], grads[group], weight_in, weight_out, bias_row, small,
            experts, old,
        )
        sent.append(exchange(dx).reshape(slot_rows, features))
        returned.append(exchange(result).reshape(slot_rows, features))
    dw1, dw2, dbias, drouter = old
    old = None
    grad_blocks = []
    out_blocks = []
    for group in range(micro):
        proj, mixed, residual, gates = saved[group]
        grad_x, *old = attend_back(
            images, out_grad, slots, sent[group], proj, mixed, residual, attn_in_full,
            attn_out_full, small, experts, group, old,
        )
        grad_blocks.append(grad_x)
        out_blocks.append(combine(slots, gates, residual, returned[group], group))
    dwin, dwout, dsmall = old

    def scatter(value, axis):
        return lax.psum_scatter(value, "dp", scatter_dimension=axis, tiled=True)

    grad_expert_in = scatter(dw1, 0).astype(f32)[None]
    grad_expert_out = scatter(dw2, 0).astype(f32)[None]
    grad_expert_bias = scatter(dbias.astype(bf16), 1).astype(f32)
    little = scatter(jnp.concatenate([dsmall, drouter], axis=0).astype(bf16), 1)
    grad_attn_in = lax.psum(scatter(dwin, 0), "expert").astype(f32)
    grad_attn_out = lax.psum(scatter(dwout, 0), "expert").astype(f32)
    little = lax.psum(little, "expert").astype(f32)
    return (
        jnp.concatenate(out_blocks, axis=0),
        jnp.concatenate(grad_blocks, axis=0),
        little[0],
        little[1],
        grad_attn_in,
        grad_attn_out,
        little[2],
        little[3],
        little[8 : 8 + experts].T,
        grad_expert_in,
        grad_expert_bias,
        grad_expert_out,
    )


def solution(mesh):
    return jax.shard_map(
        per_device,
        mesh=mesh,
        in_specs=(
            P(("dp", "expert"), None, None),
            P("dp"),
            P("dp"),
            P("dp", None),
            P("dp", None),
            P("dp"),
            P("dp"),
            P("dp", None),
            P("expert", "dp", None),
            P("expert", "dp"),
            P("expert", "dp", None),
            P(("dp", "expert"), None, None),
            P(("dp", "expert"), None, None),
        ),
        out_specs=(
            P(("dp", "expert"), None, None),
            P(("dp", "expert"), None, None),
            P("dp"),
            P("dp"),
            P("dp", None),
            P("dp", None),
            P("dp"),
            P("dp"),
            P("dp", None),
            P("expert", "dp", None),
            P("expert", "dp"),
            P("expert", "dp", None),
        ),
        check_vma=False,
    )
```

time: 1140 us -> 742 us (0.65)
  matrix products: 364 us -> 0 us
  Pallas kernels: 0 us -> 287 us
  local copies, waits for them, and re-layouts: 257 us -> 11.8 us
  other arithmetic: 119 us -> 17.6 us
  blocking collectives: 47.4 us -> 102 us
  waiting for transfers between devices: 281 us -> 263 us
    dot_general x40 -> x0, matrix products: 349 us -> none  [the longest x26 278 us: contract(): jnp.einsum(formula, left_side, right_side, preferred_element_type=jnp.flo...]
    pallas_call x0 -> x13, Pallas kernels: none -> 287 us  [the longest x2 144 us: expert_block(): pl.pallas_call(functools.partial(expert_kernel, experts, chunk, add), gri...]
    reshape x38 -> x0, local copies, waits for them, and re-layouts: 117 us -> none  [the longest x4 16.8 us: per_device(): values = projected[:, 2 * features:].reshape(head_shape)]
    gather x16 -> x0, local copies, waits for them, and re-layouts: 69.4 us -> none  [the longest x10 25.1 us: per_device(): gate_values = jnp.take_along_axis(router_probs, route_block, axis=1)]
    all_to_all x0 -> x1, blocking collectives: none -> 55.6 us  [exchange(): lax.all_to_all(rows.reshape(experts, capacity, features), 'expert', split...]
    scatter x2 -> x0, other arithmetic: 31.1 us -> none  [per_device(): grad_slots = jnp.zeros((experts * capacity + 1, features), jnp.float32).a...]
    convert_element_type x23 -> x5, other arithmetic: 29.9 us -> 4.92 us  [the longest x1 2.49 us: per_device(): grad_attn_in = lax.psum(scatter(dwin, 0), 'expert').astype(f32)]
    reduce_scatter x4, waiting for transfers between devices: 47.2 us -> 25.7 us  [scatter(): return lax.psum_scatter(value, 'dp', scatter_dimension=axis, tiled=True)]
  transfers between devices with their start and end apart: 19 -> 18, of which waited for: 7 -> 7; matrix products, arithmetic and copies ran while one was open for 65% -> 3% of each run, Pallas kernels for 0% -> 39%
where the time goes in v1:
time: 742 us; the launch traced here: 733 us
  Pallas kernels  287 us (39%)
  waiting for transfers between devices  263 us (35%)
  blocking collectives  102 us (14%)
  starting transfers between devices  36 us (5%)
  other arithmetic  17.6 us (2%)
  between operations  14.7 us (2%)
  local copies, waits for them, and re-layouts  11.8 us (2%)
    all_to_all x7, waiting for transfers between devices, exchange(): lax.all_to_all(rows.reshape(experts, capacity, features), 'expert', split...  151 us
    pallas_call x2, Pallas kernels, expert_block(): pl.pallas_call(functools.partial(expert_kernel, experts, chunk, add), gri...  144 us
    psum x1, waiting for transfers between devices, per_device(): grad_attn_in = lax.psum(scatter(dwin, 0), 'expert').astype(f32)  81.5 us
    pallas_call x2, Pallas kernels, attend_back(): pl.pallas_call(functools.partial(attend_back_kernel, experts, add), grid=...  64.3 us
    all_to_all x1, blocking collectives, exchange(): lax.all_to_all(rows.reshape(experts, capacity, features), 'expert', split...  55.6 us
    all_to_all x7, starting transfers between devices, exchange(): lax.all_to_all(rows.reshape(experts, capacity, features), 'expert', split...  35.4 us
    psum x1, blocking collectives, per_device(): little = lax.psum(little, 'expert').astype(f32)  35.2 us
    pallas_call x4, Pallas kernels, dispatch(): pl.pallas_call(functools.partial(dispatch_kernel, capacity), grid=(expert...  33.2 us
  transfers between devices with their start and end apart: 18, of which 7 were waited for; matrix products, arithmetic and copies ran while one was open for 3% of the time, Pallas kernels for 39%

profile of v1, /device:TPU:0, one launch (start us, length us, event | category | flops | bytes accessed | tf_op | source)
XLA Modules:
  0.0 732.7 jit_solution(2045544056697988757)
XLA Ops:
  14.4 8.2 %dispatch.7 = bf16[8,184,768]{2,1,0:T(8,128)(2,1)} custom-call(s32[6,197,2]{2,1,0:T(8,128)} %route.1.slots_ref, bf16[6,197,768]{2,1,0:T(8,128)(2,1)} %top_ref.3), custom_call_target="tpu_custom_call" | custom-call | flops 1336246272 | bytes 3168768 | tf_op jit(solution)/shard_map/dispatch/pallas_call | solution.py:134
  22.6 7.3 all-to-all-start.4
  29.9 8.3 %dispatch.5 = bf16[8,184,768]{2,1,0:T(8,128)(2,1)} custom-call(s32[6,197,2]{2,1,0:T(8,128)} %route.1.slots_ref, bf16[6,197,768]{2,1,0:T(8,128)(2,1)} %top_ref.3), custom_call_target="tpu_custom_call" | custom-call | flops 1336246272 | bytes 3168768 | tf_op jit(solution)/shard_map/dispatch/pallas_call | solution.py:134
  38.2 43.4 %all-to-all-done.4 = bf16[8,184,768]{2,1,0:T(8,128)(2,1)S(1)} async-done(((bf16[8,184,768]{2,1,0:T(8,128)(2,1)}), bf16[8,184,768]{2,1,0:T(8,128)(2,1)S(1)}, u32[]{:S(2)}, u32[]{:S(2)}) %all-to-all-start.4) | async-done | bytes 2261024 | tf_op jit(solution)/shard_map/all_to_all | solution.py:610
  93.7 14.4 %attend.2 = (bf16[3,197,2304]{2,1,0:T(8,128)(2,1)}, bf16[3,197,768]{2,1,0:T(8,128)(2,1)}, f32[3,197,768]{2,1,0:T(8,128)}, bf16[3,197,768]{2,1,0:T(8,128)(2,1)}, f32[3,197,2]{2,1,0:T(8,128)}) custom-call(bf16[6,197,768]{2,1,0:T(8,128)(2,1)} %x_ref.7, s32[6,197,2]{2,1,0:T(8,128)} %copy.29.routes_ref, bf16[768,2304]{1,0:T(8,128)(2,1)} %all-gather.8.cloned.1.call-done.win_ref, ...), custom_call_target="tpu_custom_call" | custom-call | flops 5577375744 | bytes 23961600 | tf_op jit(solution)/shard_map/attend/pallas_call | solution.py:219
  108.1 8.4 %dispatch.4 = bf16[8,184,768]{2,1,0:T(8,128)(2,1)} custom-call(s32[3,197,2]{2,1,0:T(8,128)} %get-tuple-element.74.slots_ref, bf16[3,197,768]{2,1,0:T(8,128)(2,1)} %get-tuple-element.44.rows_ref), custom_call_target="tpu_custom_call" | custom-call | flops 1336246272 | bytes 3168768 | tf_op jit(solution)/shard_map/dispatch/pallas_call | solution.py:134
  116.4 20.9 %all-to-all-done.1 = bf16[8,184,768]{2,1,0:T(8,128)(2,1)} async-done(((bf16[8,184,768]{2,1,0:T(8,128)(2,1)}), bf16[8,184,768]{2,1,0:T(8,128)(2,1)}, u32[]{:S(2)}, u32[]{:S(2)}) %all-to-all-start.1) | async-done | bytes 2261024 | tf_op jit(solution)/shard_map/all_to_all | solution.py:610
  141.0 14.3 %attend.3 = (bf16[3,197,2304]{2,1,0:T(8,128)(2,1)}, bf16[3,197,768]{2,1,0:T(8,128)(2,1)}, f32[3,197,768]{2,1,0:T(8,128)}, bf16[3,197,768]{2,1,0:T(8,128)(2,1)}, f32[3,197,2]{2,1,0:T(8,128)}) custom-call(bf16[6,197,768]{2,1,0:T(8,128)(2,1)} %x_ref.7, s32[6,197,2]{2,1,0:T(8,128)} %copy.29.routes_ref, bf16[768,2304]{1,0:T(8,128)(2,1)} %all-gather.8.cloned.1.call-done.win_ref, ...), custom_call_target="tpu_custom_call" | custom-call | flops 5577375744 | bytes 23961600 | tf_op jit(solution)/shard_map/attend/pallas_call | solution.py:219
  155.3 8.3 %dispatch.6 = bf16[8,184,768]{2,1,0:T(8,128)(2,1)} custom-call(s32[3,197,2]{2,1,0:T(8,128)} %get-tuple-element.75.slots_ref, bf16[3,197,768]{2,1,0:T(8,128)(2,1)} %get-tuple-element.48.rows_ref), custom_call_target="tpu_custom_call" | custom-call | flops 1336246272 | bytes 3168768 | tf_op jit(solution)/shard_map/dispatch/pallas_call | solution.py:134
  163.6 29.3 %all-to-all-done = bf16[8,184,768]{2,1,0:T(8,128)(2,1)S(1)} async-done(((bf16[8,184,768]{2,1,0:T(8,128)(2,1)}), bf16[8,184,768]{2,1,0:T(8,128)(2,1)S(1)}, u32[]{:S(2)}, u32[]{:S(2)}) %all-to-all-start) | async-done | bytes 2261024 | tf_op jit(solution)/shard_map/all_to_all | solution.py:610
  197.3 6.1 all_gather.23.bias_ref
  203.4 71.8 %expert_block.2 = (bf16[1472,768]{1,0:T(8,128)(2,1)}, bf16[1472,768]{1,0:T(8,128)(2,1)}, f32[3072,768]{1,0:T(8,128)}, f32[3072,768]{1,0:T(8,128)}, f32[1,3072]{1,0:T(1,128)}, /*index=5*/f32[16,768]{1,0:T(8,128)}) custom-call(s32[1]{0:T(128)} %bitcast.8.mine_ref, bf16[1472,768]{1,0:T(8,128)(2,1)} %bitcast.43, bf16[1472,768]{1,0:T(8,128)(2,1)} %bitcast.10.g_ref, ...), custom_call_target="tpu_custom_call" | custom-call | flops 41674604544 | bytes 37355520 | tf_op jit(solution)/shard_map/expert_block/pallas_call | solution.py:360
  275.1 6.1 all-to-all-start.6
  281.3 72.6 %expert_block.3 = (bf16[1472,768]{1,0:T(8,128)(2,1)}, bf16[1472,768]{1,0:T(8,128)(2,1)}, bf16[3072,768]{1,0:T(8,128)(2,1)}, bf16[3072,768]{1,0:T(8,128)(2,1)}, f32[1,3072]{1,0:T(1,128)}, /*index=5*/f32[16,768]{1,0:T(8,128)}) custom-call(s32[1]{0:T(128)} %bitcast.8.mine_ref, bf16[1472,768]{1,0:T(8,128)(2,1)} %bitcast.15.x_ref, bf16[1472,768]{1,0:T(8,128)(2,1)} %bitcast.40, ...), custom_call_target="tpu_custom_call" | custom-call | flops 41674604544 | bytes 37355520 | tf_op jit(solution)/shard_map/expert_block/pallas_call | solution.py:360
  362.9 31.5 %attend_back.2 = (f32[3,197,768]{2,1,0:T(8,128)}, f32[768,2304]{1,0:T(8,128)}, f32[768,768]{1,0:T(8,128)}, f32[8,768]{1,0:T(8,128)}) custom-call(bf16[6,197,768]{2,1,0:T(8,128)(2,1)} %x_ref.7, bf16[6,197,768]{2,1,0:T(8,128)(2,1)} %top_ref.3, s32[6,197,2]{2,1,0:T(8,128)} %route.1.slots_ref, bf16[1472,768]{1,0:T(8,128)(2,1)} %bitcast.41, ...), custom_call_target="tpu_custom_call" | custom-call | flops 13943439360 | bytes 33398784 | tf_op jit(solution)/shard_map/attend_back/pallas_call | solution.py:549
  394.4 18.7 %all-to-all-done.7 = bf16[8,184,768]{2,1,0:T(8,128)(2,1)} async-done(((bf16[8,184,768]{2,1,0:T(8,128)(2,1)}), bf16[8,184,768]{2,1,0:T(8,128)(2,1)}, u32[]{:S(2)}, u32[]{:S(2)}) %all-to-all-start.7) | async-done | bytes 2261024 | tf_op jit(solution)/shard_map/all_to_all | solution.py:610
  413.0 32.8 %attend_back.3 = (f32[3,197,768]{2,1,0:T(8,128)}, bf16[768,2304]{1,0:T(8,128)(2,1)}, bf16[768,768]{1,0:T(8,128)(2,1)}, f32[8,768]{1,0:T(8,128)}) custom-call(bf16[6,197,768]{2,1,0:T(8,128)(2,1)} %x_ref.7, bf16[6,197,768]{2,1,0:T(8,128)(2,1)} %top_ref.3, s32[6,197,2]{2,1,0:T(8,128)} %route.1.slots_ref, bf16[1472,768]{1,0:T(8,128)(2,1)} %bitcast.22.sent_ref, ...), custom_call_target="tpu_custom_call" | custom-call | flops 13943439360 | bytes 33398784 | tf_op jit(solution)/shard_map/attend_back/pallas_call | solution.py:549
  450.0 55.6 %all_to_all.40 = bf16[8,184,768]{2,1,0:T(8,128)(2,1)} all-to-all(bf16[8,184,768]{2,1,0:T(8,128)(2,1)S(1)} %bitcast.39), channel_id=1, replica_groups=mesh['dp'=4,'expert'=8] {'expert'}, dimensions={0} | all-to-all | bytes 4521984 | tf_op jit(solution)/shard_map/all_to_all | solution.py:610
  515.2 6.5 combine.2
  521.7 38.9 %all-to-all-done.5 = bf16[8,184,768]{2,1,0:T(8,128)(2,1)S(1)} async-done(((bf16[8,184,768]{2,1,0:T(8,128)(2,1)}), bf16[8,184,768]{2,1,0:T(8,128)(2,1)S(1)}, u32[]{:S(2)}, u32[]{:S(2)}) %all-to-all-start.5) | async-done | bytes 2261024 | tf_op jit(solution)/shard_map/all_to_all | solution.py:610
  562.0 6.5 combine.3
  572.0 35.2 %psum.21 = bf16[24,192]{1,0:T(8,128)(2,1)S(1)} all-reduce(bf16[24,192]{1,0:T(8,128)(2,1)S(1)} %copy.34), channel_id=1, replica_groups=mesh['dp'=4,'expert'=8] {'expert'}, use_global_device_ids=true, to_apply=%region_1.0 | all-reduce | flops 4608 | bytes 18432 | tf_op jit(solution)/shard_map/psum | solution.py:665
  611.4 25.7 %reduce-scatter.15.cloned.1.call-done = bf16[768,768]{1,0:T(8,128)(2,1)} async-done(((bf16[3072,768]{1,0:T(8,128)(2,1)}), bf16[768,768]{1,0:T(8,128)(2,1)}) %reduce-scatter.15.cloned.1.call-update) | async-done | bytes 1179664 | tf_op jit(solution)/shard_map/reduce_scatter | solution.py:657
  640.0 81.5 %all-reduce.3.cloned.1.call-done = (bf16[192,2304]{1,0:T(8,128)(2,1)}, bf16[192,768]{1,0:T(8,128)(2,1)}) async-done(((bf16[192,2304]{1,0:T(8,128)(2,1)}, bf16[192,768]{1,0:T(8,128)(2,1)}), (bf16[192,2304]{1,0:T(8,128)(2,1)}, bf16[192,768]{1,0:T(8,128)(2,1)})) %all-reduce.3.cloned.1.call-update) | async-done | bytes 1179664 | tf_op jit(solution)/shard_map/psum | solution.py:663
  (102 shorter events, 65.8 us)
Async XLA Ops:
  7.2 86.5 %all-gather.10.cloned.1.call-start = ((), (), s32[]{:S(2)}) async-start(), calls=%async_computation.15 | async-start | bytes 1474560 | tf_op jit(solution)/shard_map/all_gather | solution.py:603
  7.9 85.8 %all-gather.8.cloned.1.call-start = ((), (), s32[]{:S(2)}) async-start(), calls=%async_computation.14 | async-start | bytes 4423680 | tf_op jit(solution)/shard_map/all_gather | solution.py:602
  8.7 194.7 %all-gather.12.cloned.1.call-start = ((), (), s32[]{:S(2)}) async-start(), calls=%async_computation.20 | async-start | bytes 5898240 | tf_op jit(solution)/shard_map/all_gather | solution.py:604
  22.6 59.0 %all-to-all-start.4 = ((bf16[8,184,768]{2,1,0:T(8,128)(2,1)}), bf16[8,184,768]{2,1,0:T(8,128)(2,1)S(1)}, u32[]{:S(2)}, u32[]{:S(2)}) async-start(bf16[8,184,768]{2,1,0:T(8,128)(2,1)} %dispatch.7), calls=%async_computation.4 | async-start | bytes 4521984 | tf_op jit(solution)/shard_map/all_to_all | solution.py:610
  38.2 48.4 %copy-start.13 = (bf16[192]{0:T(256)(128)(2,1)S(1)}, bf16[192]{0:T(256)(128)(2,1)}, u32[]{:S(2)}) copy-start(bf16[192]{0:T(256)(128)(2,1)} %param.14) | copy-start | bytes 1156
  38.2 48.5 %copy-start.14 = (bf16[192]{0:T(256)(128)(2,1)S(1)}, bf16[192]{0:T(256)(128)(2,1)}, u32[]{:S(2)}) copy-start(bf16[192]{0:T(256)(128)(2,1)} %param.15) | copy-start | bytes 1156
  38.2 48.5 %copy-start.15 = (bf16[192]{0:T(256)(128)(2,1)S(1)}, bf16[192]{0:T(256)(128)(2,1)}, u32[]{:S(2)}) copy-start(bf16[192]{0:T(256)(128)(2,1)} %param.18) | copy-start | bytes 1156
  38.2 48.5 %copy-start.16 = (bf16[192]{0:T(256)(128)(2,1)S(1)}, bf16[192]{0:T(256)(128)(2,1)}, u32[]{:S(2)}) copy-start(bf16[192]{0:T(256)(128)(2,1)} %param.19) | copy-start | bytes 1156
  38.2 48.5 %copy-start.11 = (bf16[192,8]{0,1:T(8,128)(2,1)S(1)}, bf16[192,8]{0,1:T(8,128)(2,1)}, u32[]{:S(2)}) copy-start(bf16[192,8]{0,1:T(8,128)(2,1)} %param.20) | copy-start | bytes 9220
  38.2 54.6 %copy-start = (s32[6,197,2]{2,1,0:T(8,128)S(1)}, s32[6,197,2]{2,1,0:T(8,128)}, u32[]{:S(2)}) copy-start(s32[6,197,2]{2,1,0:T(8,128)} %route.1.slots_ref) | copy-start | bytes 28372
  81.6 55.7 %all-to-all-start.1 = ((bf16[8,184,768]{2,1,0:T(8,128)(2,1)}), bf16[8,184,768]{2,1,0:T(8,128)(2,1)}, u32[]{:S(2)}, u32[]{:S(2)}) async-start(bf16[8,184,768]{2,1,0:T(8,128)(2,1)} %dispatch.5), calls=%async_computation.1 | async-start | bytes 4521984 | tf_op jit(solution)/shard_map/all_to_all | solution.py:610
  86.0 117.3 %all-gather.14.cloned.1.call-start = ((), (), s32[]{:S(2)}) async-start(), calls=%async_computation.21 | async-start | bytes 5898240 | tf_op jit(solution)/shard_map/all_gather | solution.py:605
  137.3 55.6 %all-to-all-start = ((bf16[8,184,768]{2,1,0:T(8,128)(2,1)}), bf16[8,184,768]{2,1,0:T(8,128)(2,1)S(1)}, u32[]{:S(2)}, u32[]{:S(2)}) async-start(bf16[8,184,768]{2,1,0:T(8,128)(2,1)} %dispatch.4), calls=%async_computation | async-start | bytes 4521984 | tf_op jit(solution)/shard_map/all_to_all | solution.py:610
  192.9 82.2 %all-to-all-start.3 = ((bf16[8,184,768]{2,1,0:T(8,128)(2,1)}), bf16[8,184,768]{2,1,0:T(8,128)(2,1)}, u32[]{:S(2)}, u32[]{:S(2)}) async-start(bf16[8,184,768]{2,1,0:T(8,128)(2,1)} %dispatch.6), calls=%async_computation.3 | async-start | bytes 4521984 | tf_op jit(solution)/shard_map/all_to_all | solution.py:610
  275.1 78.7 %all-to-all-start.6 = ((bf16[8,184,768]{2,1,0:T(8,128)(2,1)}), bf16[8,184,768]{2,1,0:T(8,128)(2,1)S(1)}, u32[]{:S(2)}, u32[]{:S(2)}) async-start(bf16[8,184,768]{2,1,0:T(8,128)(2,1)} %bitcast.45), calls=%async_computation.6 | async-start | bytes 4521984 | tf_op jit(solution)/shard_map/all_to_all | solution.py:610
  355.2 57.8 %all-to-all-start.7 = ((bf16[8,184,768]{2,1,0:T(8,128)(2,1)}), bf16[8,184,768]{2,1,0:T(8,128)(2,1)}, u32[]{:S(2)}, u32[]{:S(2)}) async-start(bf16[8,184,768]{2,1,0:T(8,128)(2,1)} %bitcast.42), calls=%async_computation.7 | async-start | bytes 4521984 | tf_op jit(solution)/shard_map/all_to_all | solution.py:610
  361.2 148.1 %reduce-scatter.21.cloned.1.call-start = ((), (), s32[]{:S(2)}) async-start(), calls=%async_computation.23 | async-start | bytes 983040
  362.6 205.9 %reduce-scatter.13.cloned.1.call-start = ((), (), s32[]{:S(2)}) async-start(), calls=%async_computation.17 | async-start | bytes 1474560 | tf_op jit(solution)/shard_map/reduce_scatter | solution.py:657
  445.9 122.6 %reduce-scatter.11.cloned.1.call-start = ((), (), s32[]{:S(2)}) async-start(), calls=%async_computation.16 | async-start | bytes 4423680 | tf_op jit(solution)/shard_map/reduce_scatter | solution.py:657
  446.7 124.4 %reduce-scatter.19.cloned.1.call-start = ((), (), s32[]{:S(2)}) async-start(), calls=%async_computation.22 | async-start | bytes 245760
  447.6 160.7 %reduce-scatter.17.cloned.1.call-start = ((), (), s32[]{:S(2)}) async-start(), calls=%async_computation.19 | async-start | bytes 5898240 | tf_op jit(solution)/shard_map/reduce_scatter | solution.py:657
  448.3 188.8 %reduce-scatter.15.cloned.1.call-start = ((), (), s32[]{:S(2)}) async-start(), calls=%async_computation.18 | async-start | bytes 5898240 | tf_op jit(solution)/shard_map/reduce_scatter | solution.py:657
  505.7 54.9 %all-to-all-start.5 = ((bf16[8,184,768]{2,1,0:T(8,128)(2,1)}), bf16[8,184,768]{2,1,0:T(8,128)(2,1)S(1)}, u32[]{:S(2)}, u32[]{:S(2)}) async-start(bf16[8,184,768]{2,1,0:T(8,128)(2,1)} %bitcast.17), calls=%async_computation.5 | async-start | bytes 4521984 | tf_op jit(solution)/shard_map/all_to_all | solution.py:610
  509.3 212.2 %all-reduce.3.cloned.1.call-start = ((), (), s32[]{:S(2)}) async-start(), calls=%async_computation.24 | async-start | bytes 2359296 | tf_op jit(solution)/shard_map/psum | solution.py:663
  (11 other events, 65.3 us)
Sparse Core Ops, SparseCore 0:
  9.6 20.1 all-gather.9
  31.4 30.7 all-gather.7
  63.7 37.6 all-gather.11
  102.8 37.4 all-gather.13
  364.3 24.6 reduce-scatter.20
  446.0 24.8 reduce-scatter.12
  473.5 40.4 reduce-scatter.10
  516.5 19.7 reduce-scatter.18
  539.0 47.8 reduce-scatter.16
  589.2 47.8 reduce-scatter.14
  641.0 80.3 all-reduce.2

commit v2 on v1

--- a/solution.py
+++ b/solution.py
@@ -84,7 +84,80 @@
     return values * phi, phi + values * (0.3989422804014327 * bell)
 
 
-def route_kernel(experts, capacity, routes_ref, slots_ref):
+class Rides:
+    def __init__(self, arrays):
+        self.arrays = list(arrays)
+        self.parts = arrays[0].shape[0]
+        self.in_specs = [pl.BlockSpec(memory_space=pl.ANY)] * len(arrays)
+        self.out_shape = [jax.ShapeDtypeStruct(a.shape, a.dtype) for a in arrays]
+        self.scratch = [
+            pltpu.SemaphoreType.DMA((self.parts,)),
+            pltpu.SemaphoreType.DMA((self.parts,)),
+            pltpu.SemaphoreType.DMA,
+        ] * len(arrays)
+
+    def copies(self, refs, offset):
+        me = lax.axis_index("expert")
+        peer = lax.rem(me + offset, self.parts)
+        sources, targets, sems = refs
+        return [
+            pltpu.make_async_remote_copy(
+                src_ref=source.at[peer],
+                dst_ref=target.at[me],
+                send_sem=sems[3 * index].at[offset],
+                recv_sem=sems[3 * index + 1].at[offset],
+                device_id={"expert": peer},
+                device_id_type=pl.DeviceIdType.MESH,
+            )
+            for index, (source, target) in enumerate(zip(sources, targets))
+        ]
+
+    def own(self, refs):
+        me = lax.axis_index("expert")
+        sources, targets, sems = refs
+        return [
+            pltpu.make_async_copy(source.at[me], target.at[me], sems[3 * index + 2])
+            for index, (source, target) in enumerate(zip(sources, targets))
+        ]
+
+    def start(self, refs, more=()):
+        me = lax.axis_index("expert")
+        barrier = pltpu.get_barrier_semaphore()
+        for peer in more:
+            pl.semaphore_signal(
+                barrier, inc=1, device_id=peer, device_id_type=pl.DeviceIdType.MESH
+            )
+
+        @pl.loop(1, self.parts)
+        def _(offset):
+            pl.semaphore_signal(
+                barrier,
+                inc=1,
+                device_id={"expert": lax.rem(me + offset, self.parts)},
+                device_id_type=pl.DeviceIdType.MESH,
+            )
+
+        pl.semaphore_wait(barrier, self.parts - 1 + len(more))
+
+        @pl.loop(1, self.parts)
+        def _(offset):
+            for copy in self.copies(refs, offset):
+                copy.start()
+
+        for copy in self.own(refs):
+            copy.start()
+
+    def finish(self, refs):
+        for copy in self.own(refs):
+            copy.wait()
+
+        @pl.loop(1, self.parts)
+        def _(offset):
+            for copy in self.copies(refs, offset):
+                copy.wait()
+
+
+def route_kernel(experts, capacity, routes_ref, slots_ref, lines_ref):
     seq = routes_ref.shape[1]
     row = lax.broadcasted_iota(jnp.int32, (seq, seq), 0)
     col = lax.broadcasted_iota(jnp.int32, (seq, seq), 1)
@@ -93,6 +166,7 @@
     groups = routes_ref.shape[0] // IMG_MB
     for group in range(groups):
         base = jnp.zeros((1, LANES), f32)
+        table = jnp.full((seq, LANES), -1.0, f32)
         for choice in range(TOP):
             for image in range(IMG_MB):
                 index = group * IMG_MB + image
@@ -103,12 +177,17 @@
                 base = base + jnp.sum(onehot, axis=0, keepdims=True)
                 slot = jnp.where(position < capacity, named * capacity + position, -1)
                 slots_ref[index, :, choice : choice + 1] = slot
+                table = jnp.where(lane == image * TOP + choice, slot.astype(f32), table)
+        lines_ref[group] = table.T[: lines_ref.shape[1]].astype(jnp.int32)
 
 
 def route(routes, experts, capacity):
     return pl.pallas_call(
         functools.partial(route_kernel, experts, capacity),
-        out_shape=jax.ShapeDtypeStruct(routes.shape, jnp.int32),
+        out_shape=[
+            jax.ShapeDtypeStruct(routes.shape, jnp.int32),
+            jax.ShapeDtypeStruct((routes.shape[0] // IMG_MB, 8, routes.shape[1]), jnp.int32),
+        ],
         compiler_params=pltpu.CompilerParams(vmem_limit_bytes=VMEM_LIMIT),
         cost_estimate=pl.CostEstimate(
             flops=10**8, bytes_accessed=2 * 10**6, transcendentals=0
@@ -117,26 +196,28 @@
     )(routes)
 
 
-def dispatch_kernel(capacity, slots_ref, rows_ref, out_ref):
+def dispatch_kernel(capacity, lines_ref, rows_ref, out_ref):
     first = pl.program_id(0) * capacity
     seq = rows_ref.shape[1]
-    column = lax.broadcasted_iota(jnp.int32, (seq, capacity), 1) + first
+    slot = lax.broadcasted_iota(jnp.int32, (capacity, seq), 0) + first
+    lines = lines_ref[0]
     acc = jnp.zeros((capacity, rows_ref.shape[2]), f32)
     for image in range(IMG_MB):
-        slots = slots_ref[image]
-        holds = (slots[:, 0:1] == column) | (slots[:, 1:2] == column)
-        acc = acc + t_dot(holds.astype(f32).astype(bf16), rows_ref[image])
+        at = image * TOP
+        holds = (lines[at : at + 1] == slot) | (lines[at + 1 : at + 2] == slot)
+        acc = acc + dot(holds.astype(f32).astype(bf16), rows_ref[image])
     out_ref[0] = acc.astype(bf16)
 
 
-def dispatch(slots, rows, group, experts, capacity):
+def dispatch(lines, rows, group, experts, capacity):
     seq, features = rows.shape[1:]
+    block = group if rows.shape[0] > IMG_MB else 0
     return pl.pallas_call(
         functools.partial(dispatch_kernel, capacity),
         grid=(experts,),
         in_specs=[
-            pl.BlockSpec((IMG_MB, seq, TOP), lambda e: (group, 0, 0)),
-            pl.BlockSpec((IMG_MB, seq, features), lambda e: (group, 0, 0)),
+            pl.BlockSpec((1, 8, seq), lambda e: (group, 0, 0)),
+            pl.BlockSpec((IMG_MB, seq, features), lambda e: (block, 0, 0)),
         ],
         out_specs=pl.BlockSpec((1, capacity, features), lambda e: (e, 0, 0)),
         out_shape=jax.ShapeDtypeStruct((experts, capacity, features), bf16),
@@ -147,11 +228,11 @@
             transcendentals=0,
         ),
         name="dispatch",
-    )(slots, rows)
+    )(lines, rows)
 
 
 def attend_kernel(
-    experts, x_ref, routes_ref, win_ref, wout_ref, small_ref,
+    experts, x_ref, routes_ref, dense_ref, small_ref,
     proj_ref, mixed_ref, residual_ref, hidden_ref, gates_ref,
 ):
     features = x_ref.shape[2]
@@ -161,7 +242,7 @@
     attn_input = (
         normed * vectors[experts : experts + 1] + vectors[experts + 1 : experts + 2]
     ).astype(bf16)
-    proj_ref[0] = dot(attn_input, win_ref[...]).astype(bf16)
+    proj_ref[0] = dot(attn_input, dense_ref[:, : 3 * features]).astype(bf16)
     low_half = lax.broadcasted_iota(jnp.int32, (1, LANES), 1) < HEAD_DIM
     for pair in range(features // LANES):
         first = pair * LANES
@@ -181,7 +262,7 @@
             part = dot(weights, jnp.where(keep, values, 0).astype(bf16))
             out = part if out is None else out + part
         mixed_ref[0, :, first : first + LANES] = out.astype(bf16)
-    residual = image + dot(mixed_ref[0], wout_ref[...])
+    residual = image + dot(mixed_ref[0], dense_ref[:, 3 * features :])
     residual_ref[0] = residual
     normed, _ = norm_forward(residual)
     hidden = (
@@ -199,9 +280,9 @@
         )
 
 
-def attend(images, routes, attn_in, attn_out, small, experts, group):
+def attend(images, routes, dense, small, experts, group):
     seq, features = images.shape[1:]
-    wide = attn_in.shape[1]
+    wide = 3 * features
     first = group * IMG_MB
 
     def rows(width):
@@ -222,8 +303,7 @@
         in_specs=[
             source(features),
             source(TOP),
-            whole(attn_in),
-            whole(attn_out),
+            whole(dense),
             whole(small),
         ],
         out_specs=[rows(wide), rows(features), rows(features), rows(features), rows(TOP)],
@@ -241,24 +321,31 @@
             transcendentals=IMG_MB * HEADS * seq * seq,
         ),
         name="attend",
-    )(images, routes, attn_in, attn_out, small)
+    )(images, routes, dense, small)
 
 
 def expert_kernel(
-    experts, chunk, add, mine_ref, x_ref, g_ref, w1_ref, w2_ref, bias_ref, small_ref, *refs
+    experts, chunk, add, rides, x_ref, g_ref, w1_ref, w2_ref, bias_ref, small_ref, *refs
 ):
     if add:
-        old_w1_ref, old_w2_ref, old_bias_ref, old_router_ref = refs[:4]
-        refs = refs[4:]
+        old_w_ref, old_router_ref = refs[:2]
+        refs = refs[2:]
+    count = len(rides.arrays)
+    ride_refs = (refs[:count], refs[count + 4 : 2 * count + 4], refs[2 * count + 10 :])
+    refs = refs[count : count + 4] + refs[2 * count + 4 : 2 * count + 10]
     (
-        result_ref, dx_ref, dw1_ref, dw2_ref, dbias_ref, drouter_ref,
+        result_ref, dx_ref, dw_ref, drouter_ref,
         result_acc, dx_acc, dr_ref, probs_ref, act_ref, pre_ref,
     ) = refs
     step = pl.program_id(0)
     last = pl.num_programs(0) - 1
     rows = x_ref.shape[0]
-    mine = mine_ref[0]
+    mine = lax.axis_index("expert")
     chunks = rows // chunk
+
+    @pl.when(step == 0)
+    def _():
+        rides.start(ride_refs)
 
     @pl.when(step == 0)
     def _():
@@ -288,13 +375,14 @@
         dx_acc[at, :] += dot(grad_pre, w1)
     dw1 = t_dot(pre_ref[...], x_ref[...])
     dw2 = t_dot(act_ref[...], dr_ref[...])
-    if add:
-        dw1 = dw1 + old_w1_ref[...]
-        dw2 = dw2 + old_w2_ref[...]
-        dbias = dbias + old_bias_ref[...]
-    dw1_ref[...] = dw1.astype(dw1_ref.dtype)
-    dw2_ref[...] = dw2.astype(dw2_ref.dtype)
-    dbias_ref[...] = dbias
+    dbias = jnp.broadcast_to(dbias, (LANES, dbias.shape[1])).T
+    first = 0
+    for part in (dw1, dw2, dbias):
+        at = pl.ds(first, part.shape[1])
+        if add:
+            part = part + old_w_ref[:, at]
+        dw_ref[:, at] = part.astype(dw_ref.dtype)
+        first += part.shape[1]
 
     @pl.when(step == last)
     def _():
@@ -320,6 +408,7 @@
             ).astype(bf16)
             drouter = drouter + t_dot(high, x_ref[at, :]) + t_dot(low, x_ref[at, :])
         drouter_ref[...] = drouter
+        rides.finish(ride_refs)
 
 
 def row_chunk(rows):
@@ -330,22 +419,26 @@
     return best
 
 
-def expert_block(mine, x, g, w1, w2, bias, small, experts, old):
+def expert_block(x, g, w1, w2, bias, small, experts, old, arrays, collective):
     rows, features = x.shape
     hidden_units = w1.shape[0]
-    block = 256
+    block = 512 if hidden_units % 512 == 0 else 256
     steps = hidden_units // block
     chunk = row_chunk(rows)
     add = old is not None
     out_type = bf16 if add else f32
+    rides = Rides(arrays)
 
     def whole(shape):
-        return pl.BlockSpec(shape, lambda s: (0,) * len(shape))
-
+        return pl.BlockSpec(
+            shape, lambda s: (0,) * len(shape), pipeline_mode=pl.Buffered(1)
+        )
+
+    packed = 2 * features + LANES
+    unit_grads = pl.BlockSpec((block, packed), lambda s: (s, 0))
     units = pl.BlockSpec((block, features), lambda s: (s, 0))
     unit_row = pl.BlockSpec((1, block), lambda s: (0, s))
     in_specs = [
-        pl.BlockSpec(memory_space=pltpu.SMEM),
         whole(x.shape),
         whole(g.shape),
         units,
@@ -353,25 +446,25 @@
         unit_row,
         whole(small.shape),
     ]
-    operands = [mine, x, g, w1, w2, bias, small]
+    operands = [x, g, w1, w2, bias, small]
     if add:
-        in_specs += [units, units, unit_row, whole(small.shape)]
+        in_specs += [unit_grads, whole(small.shape)]
         operands += list(old)
     return pl.pallas_call(
-        functools.partial(expert_kernel, experts, chunk, add),
+        functools.partial(expert_kernel, experts, chunk, add, rides),
         grid=(steps,),
-        in_specs=in_specs,
+        in_specs=in_specs + rides.in_specs,
         out_specs=[
-            whole(x.shape), whole(x.shape), units, units, unit_row, whole(small.shape)
-        ],
+            whole(x.shape), whole(x.shape), unit_grads, whole(small.shape)
+        ]
+        + rides.in_specs,
         out_shape=[
             jax.ShapeDtypeStruct(x.shape, bf16),
             jax.ShapeDtypeStruct(x.shape, bf16),
-            jax.ShapeDtypeStruct(w1.shape, out_type),
-            jax.ShapeDtypeStruct(w2.shape, out_type),
-            jax.ShapeDtypeStruct((1, hidden_units), f32),
+            jax.ShapeDtypeStruct((hidden_units, packed), out_type),
             jax.ShapeDtypeStruct(small.shape, f32),
-        ],
+        ]
+        + rides.out_shape,
         scratch_shapes=[
             pltpu.VMEM((rows, features), f32),
             pltpu.VMEM((rows, features), f32),
@@ -379,15 +472,18 @@
             pltpu.VMEM((rows, small.shape[0]), f32),
             pltpu.VMEM((rows, block), bf16),
             pltpu.VMEM((rows, block), bf16),
-        ],
-        compiler_params=params(("arbitrary",)),
+        ]
+        + rides.scratch,
+        compiler_params=params(
+            ("arbitrary",), collective_id=collective, has_side_effects=True
+        ),
         cost_estimate=pl.CostEstimate(
             flops=12 * rows * features * hidden_units,
             bytes_accessed=(8 * rows + 12 * hidden_units) * features,
             transcendentals=rows * hidden_units,
         ),
         name="expert_block",
-    )(*operands)
+    )(*operands, *rides.arrays)
 
 
 def combine_kernel(slots_ref, gates_ref, residual_ref, returned_ref, out_ref):
@@ -431,13 +527,32 @@
 
 
 def attend_back_kernel(
-    experts, add, x_ref, top_ref, slots_ref, sent_ref, proj_ref, mixed_ref, residual_ref,
-    win_ref, wout_ref, small_ref, *refs
+    experts, add, rides, ranks, x_ref, top_ref, slots_ref, sent_ref, proj_ref, mixed_ref, residual_ref,
+    dense_ref, small_ref, *refs
 ):
     if add:
-        old_in_ref, old_out_ref, old_small_ref = refs[:3]
+        old_dense_ref, old_small_ref, drouter_ref = refs[:3]
         refs = refs[3:]
-    (grad_x_ref, dwin_ref, dwout_ref, dsmall_ref, acc_in, acc_out, acc_small, dproj_ref) = refs
+    count = len(rides.arrays)
+    outs = 2 if add else 3
+    sources, refs = refs[:count], refs[count:]
+    grad_x_ref, ddense_ref = refs[:2]
+    if not add:
+        dsmall_ref = refs[2]
+    targets, refs = refs[outs : outs + count], refs[outs + count :]
+    acc_in, acc_out, acc_small, dproj_ref = refs[:4]
+    refs = refs[4:]
+    more = ()
+    if add:
+        pack_ref, first_ref, second_ref, first_sems, second_sems = refs[:5]
+        refs = refs[5:]
+        rank = lax.axis_index("dp")
+        core = lax.rem(rank, 2)
+        pairs = ranks // 2
+        partner = {"dp": rank + 1 - 2 * core}
+        others = [{"dp": lax.rem(rank + 2 * hop, ranks)} for hop in range(1, pairs)]
+        more = [partner] + others
+    ride_refs = (sources, targets, refs)
     features = x_ref.shape[2]
     seq = x_ref.shape[1]
     step = pl.program_id(0)
@@ -445,9 +560,10 @@
 
     @pl.when(step == 0)
     def _():
+        rides.start(ride_refs, more)
         if add:
-            acc_in[...] = old_in_ref[...]
-            acc_out[...] = old_out_ref[...]
+            acc_in[...] = old_dense_ref[:, : 3 * features]
+            acc_out[...] = old_dense_ref[:, 3 * features :]
             acc_small[...] = old_small_ref[...]
         else:
             acc_in[...] = jnp.zeros(acc_in.shape, f32)
@@ -466,7 +582,7 @@
     )
     grad_branch = grad_residual.astype(bf16)
     acc_out[...] += t_dot(mixed_ref[0], grad_branch)
-    grad_mixed = dot_t(grad_branch, wout_ref[...]).astype(bf16)
+    grad_mixed = dot_t(grad_branch, dense_ref[:, 3 * features :]).astype(bf16)
     low_half = lax.broadcasted_iota(jnp.int32, (1, LANES), 1) < HEAD_DIM
     scale = HEAD_DIM ** (-0.5)
     for pair in range(features // LANES):
@@ -501,7 +617,7 @@
         normed_one * vectors[experts : experts + 1] + vectors[experts + 1 : experts + 2]
     ).astype(bf16)
     acc_in[...] += t_dot(attn_input, dproj_ref[...])
-    grad_input = dot_t(dproj_ref[...], win_ref[...])
+    grad_input = dot_t(dproj_ref[...], dense_ref[:, : 3 * features])
     acc_small[0:1, :] += jnp.sum(grad_input * normed_one, axis=0, keepdims=True)
     acc_small[1:2, :] += jnp.sum(grad_input, axis=0, keepdims=True)
     grad_x_ref[0] = grad_residual + norm_backward(
@@ -510,20 +626,69 @@
 
     @pl.when(step == pl.num_programs(0) - 1)
     def _():
-        dwin_ref[...] = acc_in[...].astype(dwin_ref.dtype)
-        dwout_ref[...] = acc_out[...].astype(dwout_ref.dtype)
-        dsmall_ref[...] = acc_small[...]
+        if not add:
+            ddense_ref[:, : 3 * features] = acc_in[...]
+            ddense_ref[:, 3 * features :] = acc_out[...]
+            dsmall_ref[...] = acc_small[...]
+        else:
+            used = acc_small.shape[0] + drouter_ref.shape[0]
+            rest = jnp.zeros((LANES - used, features), f32)
+            column = jnp.concatenate([acc_small[...], drouter_ref[...], rest], axis=0).T
+            share = features // ranks
+            for shard in range(ranks):
+                at = slice(shard * share, (shard + 1) * share)
+                place = (shard % 2, shard // 2)
+                pack_ref[place[0], place[1], :, : 3 * features] = acc_in[at].astype(bf16)
+                pack_ref[place[0], place[1], :, 3 * features : 4 * features] = acc_out[
+                    at
+                ].astype(bf16)
+                pack_ref[place[0], place[1], :, 4 * features :] = column[at].astype(bf16)
+            copy = pltpu.make_async_remote_copy(
+                src_ref=pack_ref.at[1 - core],
+                dst_ref=first_ref,
+                send_sem=first_sems.at[0],
+                recv_sem=first_sems.at[1],
+                device_id=partner,
+                device_id_type=pl.DeviceIdType.MESH,
+            )
+            copy.start()
+            copy.wait()
+            for pair in range(pairs):
+                first_ref[pair] = (
+                    first_ref[pair].astype(f32) + pack_ref[core, pair].astype(f32)
+                ).astype(bf16)
+            mine = rank // 2
+            copies = [
+                pltpu.make_async_remote_copy(
+                    src_ref=first_ref.at[lax.rem(mine + hop, pairs)],
+                    dst_ref=second_ref.at[hop - 1],
+                    send_sem=second_sems.at[0, hop - 1],
+                    recv_sem=second_sems.at[1, hop - 1],
+                    device_id=others[hop - 1],
+                    device_id_type=pl.DeviceIdType.MESH,
+                )
+                for hop in range(1, pairs)
+            ]
+            for copy in copies:
+                copy.start()
+            total = first_ref[mine].astype(f32)
+            for copy in copies:
+                copy.wait()
+            for hop in range(1, pairs):
+                total = total + second_ref[hop - 1].astype(f32)
+            ddense_ref[...] = total.astype(bf16)
+        rides.finish(ride_refs)
 
 
 def attend_back(
-    images, out_grad, slots, sent, proj, mixed, residual, attn_in, attn_out, small,
-    experts, group, old,
+    images, out_grad, slots, sent, proj, mixed, residual, dense, small, experts, group, old,
+    arrays, collective, ranks,
 ):
     seq, features = images.shape[1:]
-    wide = attn_in.shape[1]
+    wide = 3 * features
     first = group * IMG_MB
     add = old is not None
-    out_type = bf16 if add else f32
+    rides = Rides(arrays)
 
     def rows(width):
         return pl.BlockSpec((1, seq, width), lambda i: (i, 0, 0))
@@ -532,47 +697,61 @@
         return pl.BlockSpec((1, seq, width), lambda i: (first + i, 0, 0))
 
     def whole(shape):
-        return pl.BlockSpec(shape, lambda i: (0, 0))
+        return pl.BlockSpec(shape, lambda i: (0, 0), pipeline_mode=pl.Buffered(1))
 
     small_grads = (8, features)
     in_specs = [
         source(features), source(features), source(TOP), whole(sent.shape),
         rows(wide), rows(features), rows(features),
-        whole(attn_in.shape), whole(attn_out.shape), whole(small.shape),
+        whole(dense.shape), whole(small.shape),
     ]
-    operands = [
-        images, out_grad, slots, sent, proj, mixed, residual, attn_in, attn_out, small
+    operands = [images, out_grad, slots, sent, proj, mixed, residual, dense, small]
+    out_specs = [rows(features), whole((features, 4 * features))]
+    out_shape = [
+        jax.ShapeDtypeStruct((IMG_MB, seq, features), f32),
+        jax.ShapeDtypeStruct((features, 4 * features), f32),
     ]
     if add:
-        in_specs += [whole(attn_in.shape), whole(attn_out.shape), whole(small_grads)]
+        in_specs += [whole(array.shape) for array in old]
         operands += list(old)
+        shard = (features // ranks, 4 * features + LANES)
+        out_specs[1] = whole(shard)
+        out_shape[1] = jax.ShapeDtypeStruct(shard, bf16)
+        reduce_scratch = [
+            pltpu.VMEM((2, ranks // 2, *shard), bf16),
+            pltpu.VMEM((ranks // 2, *shard), bf16),
+            pltpu.VMEM((ranks // 2 - 1, *shard), bf16),
+            pltpu.SemaphoreType.DMA((2,)),
+            pltpu.SemaphoreType.DMA((2, ranks // 2 - 1)),
+        ]
+    else:
+        out_specs.append(whole(small_grads))
+        out_shape.append(jax.ShapeDtypeStruct(small_grads, f32))
+        reduce_scratch = []
     return pl.pallas_call(
-        functools.partial(attend_back_kernel, experts, add),
+        functools.partial(attend_back_kernel, experts, add, rides, ranks),
         grid=(IMG_MB,),
-        in_specs=in_specs,
-        out_specs=[
-            rows(features), whole(attn_in.shape), whole(attn_out.shape), whole(small_grads)
-        ],
-        out_shape=[
-            jax.ShapeDtypeStruct((IMG_MB, seq, features), f32),
-            jax.ShapeDtypeStruct(attn_in.shape, out_type),
-            jax.ShapeDtypeStruct(attn_out.shape, out_type),
-            jax.ShapeDtypeStruct(small_grads, f32),
-        ],
+        in_specs=in_specs + rides.in_specs,
+        out_specs=out_specs + rides.in_specs,
+        out_shape=out_shape + rides.out_shape,
         scratch_shapes=[
-            pltpu.VMEM(attn_in.shape, f32),
-            pltpu.VMEM(attn_out.shape, f32),
+            pltpu.VMEM((features, 3 * features), f32),
+            pltpu.VMEM((features, features), f32),
             pltpu.VMEM(small_grads, f32),
             pltpu.VMEM((seq, wide), bf16),
-        ],
-        compiler_params=params(("arbitrary",)),
+        ]
+        + reduce_scratch
+        + rides.scratch,
+        compiler_params=params(
+            ("arbitrary",), collective_id=collective, has_side_effects=True
+        ),
         cost_estimate=pl.CostEstimate(
             flops=IMG_MB * seq * 40 * features * features,
             bytes_accessed=8 * features * (4 * features + IMG_MB * seq * 4),
             transcendentals=IMG_MB * HEADS * seq * seq,
         ),
         name="attend_back",
-    )(*operands)
+    )(*operands, *rides.arrays)
 
 
 def per_device(
@@ -587,6 +766,9 @@
     micro = images.shape[0] // IMG_MB
     small_rows = (experts + 4 + 15) // 16 * 16
 
+    own = router.shape[0]
+    ranks = features // own
+    bias_rows = expert_bias.shape[1] // own
     small = jnp.concatenate(
         [
             router.T,
@@ -594,88 +776,89 @@
             first_shift[None],
             second_gain[None],
             second_shift[None],
-            jnp.zeros((small_rows - experts - 4, router.shape[0]), bf16),
+            jnp.zeros((small_rows - experts - 4, own), bf16),
+            expert_bias.reshape(bias_rows, own),
         ],
         axis=0,
     )
+    dense = lax.all_gather(
+        jnp.concatenate([attn_in, attn_out], axis=1), "dp", axis=0, tiled=True
+    )
     small = lax.all_gather(small, "dp", axis=1, tiled=True)
-    attn_in_full = lax.all_gather(attn_in, "dp", axis=0, tiled=True)
-    attn_out_full = lax.all_gather(attn_out, "dp", axis=0, tiled=True)
+    bias_row = small[small_rows:].reshape(bias_rows, -1, own).transpose(1, 0, 2).reshape(1, -1)
+    small = small[:small_rows]
     weight_in = lax.all_gather(expert_in[0], "dp", axis=0, tiled=True)
     weight_out = lax.all_gather(expert_out[0], "dp", axis=0, tiled=True)
-    bias_row = lax.all_gather(expert_bias, "dp", axis=1, tiled=True)
-    mine = lax.axis_index("expert").astype(jnp.int32)[None]
+    last = None
 
     def exchange(rows):
-        return lax.all_to_all(
-            rows.reshape(experts, capacity, features),
-            "expert",
-            split_axis=0,
-            concat_axis=0,
-            tiled=True,
-        )
-
-    slots = route(routes, experts, capacity)
-    grads = [
-        exchange(dispatch(slots, out_grad, group, experts, capacity)).reshape(slot_rows, features)
-        for group in range(micro)
-    ]
+        nonlocal last
+        if last is not None:
+            rows, _ = lax.optimization_barrier((rows, last))
+        last = lax.all_to_all(rows, "expert", split_axis=0, concat_axis=0, tiled=True)
+        return last
+
+    def flat(blocks):
+        return blocks.reshape(slot_rows, features)
+
+    def blocks(rows):
+        return rows.reshape(experts, capacity, features)
+
+    slots, lines = route(routes, experts, capacity)
+    grad_rows = [dispatch(lines, out_grad, group, experts, capacity) for group in range(micro)]
     saved = []
-    received = []
+    token_rows = []
     for group in range(micro):
         proj, mixed, residual, hidden, gates = attend(
-            images, routes, attn_in_full, attn_out_full, small, experts, group
+            images, routes, dense, small, experts, group
         )
         saved.append((proj, mixed, residual, gates))
-        rows = dispatch(slots[group * IMG_MB : (group + 1) * IMG_MB], hidden, 0, experts, capacity)
-        received.append(exchange(rows).reshape(slot_rows, features))
-    old = None
-    returned = []
-    sent = []
-    for group in range(micro):
-        result, dx, *old = expert_block(
-            mine, received[group], grads[group], weight_in, weight_out, bias_row, small,
-            experts, old,
-        )
-        sent.append(exchange(dx).reshape(slot_rows, features))
-        returned.append(exchange(result).reshape(slot_rows, features))
-    dw1, dw2, dbias, drouter = old
-    old = None
-    grad_blocks = []
-    out_blocks = []
-    for group in range(micro):
-        proj, mixed, residual, gates = saved[group]
-        grad_x, *old = attend_back(
-            images, out_grad, slots, sent[group], proj, mixed, residual, attn_in_full,
-            attn_out_full, small, experts, group, old,
-        )
-        grad_blocks.append(grad_x)
-        out_blocks.append(combine(slots, gates, residual, returned[group], group))
-    dwin, dwout, dsmall = old
-
-    def scatter(value, axis):
-        return lax.psum_scatter(value, "dp", scatter_dimension=axis, tiled=True)
-
-    grad_expert_in = scatter(dw1, 0).astype(f32)[None]
-    grad_expert_out = scatter(dw2, 0).astype(f32)[None]
-    grad_expert_bias = scatter(dbias.astype(bf16), 1).astype(f32)
-    little = scatter(jnp.concatenate([dsmall, drouter], axis=0).astype(bf16), 1)
-    grad_attn_in = lax.psum(scatter(dwin, 0), "expert").astype(f32)
-    grad_attn_out = lax.psum(scatter(dwout, 0), "expert").astype(f32)
-    little = lax.psum(little, "expert").astype(f32)
+        token_rows.append(dispatch(lines, hidden, group, experts, capacity))
+    grads = exchange(grad_rows[0])
+    received = exchange(token_rows[0])
+    result_0, dx_0, *old, grads_1, received_1 = expert_block(
+        flat(received), flat(grads), weight_in, weight_out, bias_row, small, experts, None,
+        [grad_rows[1], token_rows[1]], 0,
+    )
+    result_1, dx_1, dweights, drouter, sent = expert_block(
+        flat(received_1), flat(grads_1), weight_in, weight_out, bias_row, small, experts, old,
+        [blocks(dx_0)], 1,
+    )
+    dweights = lax.psum_scatter(dweights, "dp", scatter_dimension=0, tiled=True)
+    proj, mixed, residual, _ = saved[0]
+    grad_x_0, *old, sent_1 = attend_back(
+        images, out_grad, slots, flat(sent), proj, mixed, residual, dense, small,
+        experts, 0, None, [blocks(dx_1)], 2, ranks,
+    )
+    proj, mixed, residual, _ = saved[1]
+    grad_x_1, ddense, returned_0, returned_1 = attend_back(
+        images, out_grad, slots, flat(sent_1), proj, mixed, residual, dense, small,
+        experts, 1, old + [drouter], [blocks(result_0), blocks(result_1)], 3, ranks,
+    )
+    grad_blocks = [grad_x_0, grad_x_1]
+    out_blocks = [
+        combine(slots, saved[group][3], saved[group][2], flat(returned), group)
+        for group, returned in enumerate((returned_0, returned_1))
+    ]
+    share = ddense.shape[0] // experts
+    shares = exchange(ddense.reshape(experts, share, ddense.shape[1]))
+    total = jnp.sum(shares.astype(f32), axis=0, keepdims=True).astype(bf16)
+    ddense = exchange(jnp.broadcast_to(total, shares.shape)).reshape(ddense.shape).astype(f32)
+    little = ddense[:, 4 * features :].T
+    dweights = dweights.astype(f32)
     return (
         jnp.concatenate(out_blocks, axis=0),
         jnp.concatenate(grad_blocks, axis=0),
         little[0],
         little[1],
-        grad_attn_in,
-        grad_attn_out,
+        ddense[:, : 3 * features],
+        ddense[:, 3 * features : 4 * features],
         little[2],
         little[3],
         little[8 : 8 + experts].T,
-        grad_expert_in,
-        grad_expert_bias,
-        grad_expert_out,
+        dweights[None, :, :features],
+        dweights[None, :, 2 * features],
+        dweights[None, :, features : 2 * features],
     )
 
 

time: 742 us -> 577 us (0.78)
  waiting for transfers between devices: 263 us -> 61.3 us
  Pallas kernels: 287 us -> 391 us
  blocking collectives: 102 us -> 63.8 us
  starting transfers between devices: 36 us -> 15.8 us
  other arithmetic: 17.6 us -> 9.81 us
    all_to_all x7 -> x3, waiting for transfers between devices: 151 us -> 32.7 us  [exchange(): lax.all_to_all(rows, 'expert', split_axis=0, concat_axis=0, tiled=True)]
    pallas_call x4, Pallas kernels: 209 us -> 320 us  [the longest x2 178 us: expert_block(): pl.pallas_call(functools.partial(expert_kernel, experts, chunk, add, ride...]
    psum x1 -> x0, waiting for transfers between devices: 81.5 us -> none  [per_device(): grad_attn_in = lax.psum(scatter(dwin, 0), 'expert').astype(f32)]
    psum x1 -> x0, blocking collectives: 35.2 us -> none  [per_device(): little = lax.psum(little, 'expert').astype(f32)]
    reduce_scatter x4 -> x1, waiting for transfers between devices: 25.7 us -> 0.01 us  [per_device(): dweights = lax.psum_scatter(dweights, 'dp', scatter_dimension=0, tiled=True)]
    all_to_all x7 -> x3, starting transfers between devices: 35.4 us -> 15.6 us  [exchange(): lax.all_to_all(rows, 'expert', split_axis=0, concat_axis=0, tiled=True)]
    all_gather x1, waiting for transfers between devices: 0.01 us -> 13.9 us  [per_device(): weight_out = lax.all_gather(expert_out[0], 'dp', axis=0, tiled=True)]
    all_gather x2 -> x1, waiting for transfers between devices: 0.01 us -> 13.3 us  [per_device(): lax.all_gather(jnp.concatenate([attn_in, attn_out], axis=1), 'dp', axis=0...]
  transfers between devices with their start and end apart: 18 -> 7, of which waited for: 7 -> 5; matrix products, arithmetic and copies ran while one was open for 3% -> 2% of each run, Pallas kernels for 39% -> 37%
where the time goes in v2:
time: 577 us; the launch traced here: 568 us
  Pallas kernels  391 us (68%)
  blocking collectives  63.8 us (11%)
  waiting for transfers between devices  61.3 us (11%)
  starting transfers between devices  15.8 us (3%)
  between operations  14.2 us (2%)
  local copies, waits for them, and re-layouts  12.5 us (2%)
  other arithmetic  9.81 us (2%)
    pallas_call x2, Pallas kernels, expert_block(): pl.pallas_call(functools.partial(expert_kernel, experts, chunk, add, ride...  178 us
    pallas_call x2, Pallas kernels, attend_back(): pl.pallas_call(functools.partial(attend_back_kernel, experts, add, rides,...  142 us
    all_to_all x1, blocking collectives, exchange(): lax.all_to_all(rows, 'expert', split_axis=0, concat_axis=0, tiled=True)  58.4 us
    all_to_all x3, waiting for transfers between devices, exchange(): lax.all_to_all(rows, 'expert', split_axis=0, concat_axis=0, tiled=True)  32.7 us
    pallas_call x2, Pallas kernels, attend(): pl.pallas_call(functools.partial(attend_kernel, experts), grid=(IMG_MB,),...  28.3 us
    pallas_call x4, Pallas kernels, dispatch(): pl.pallas_call(functools.partial(dispatch_kernel, capacity), grid=(expert...  24.1 us
    all_to_all x3, starting transfers between devices, exchange(): lax.all_to_all(rows, 'expert', split_axis=0, concat_axis=0, tiled=True)  15.6 us
    all_gather x1, waiting for transfers between devices, per_device(): weight_out = lax.all_gather(expert_out[0], 'dp', axis=0, tiled=True)  13.9 us
  transfers between devices with their start and end apart: 7, of which 5 were waited for; matrix products, arithmetic and copies ran while one was open for 2% of the time, Pallas kernels for 37%

profile of v2, /device:TPU:0, one launch (start us, length us, event | category | flops | bytes accessed | tf_op | source)
XLA Modules:
  0.0 568.1 jit_solution(15448086343135690886)
XLA Ops:
  11.5 5.1 route.1
  16.6 6.0 %dispatch.5 = bf16[8,184,768]{2,1,0:T(8,128)(2,1)} custom-call(s32[2,8,197]{2,1,0:T(8,128)} %get-tuple-element.49.lines_ref, bf16[6,197,768]{2,1,0:T(8,128)(2,1)} %top_ref.3), custom_call_target="tpu_custom_call" | custom-call | flops 1336246272 | bytes 3168768 | tf_op jit(solution)/shard_map/dispatch/pallas_call | solution.py:215
  22.7 7.5 %all-to-all-start = ((bf16[8,184,768]{2,1,0:T(8,128)(2,1)}), bf16[8,184,768]{2,1,0:T(8,128)(2,1)S(1)}, u32[]{:S(2)}, u32[]{:S(2)}) async-start(bf16[8,184,768]{2,1,0:T(8,128)(2,1)} %dispatch.5), calls=%async_computation | async-start | bytes 4521984 | tf_op jit(solution)/shard_map/all_to_all | solution.py:798
  31.1 5.4 all-gather.2
  37.3 13.3 %all-gather.7.cloned.1.call-done.dense_ref = bf16[768,3072]{1,0:T(8,128)(2,1)} async-done(((bf16[192,3072]{1,0:T(8,128)(2,1)}), bf16[768,3072]{1,0:T(8,128)(2,1)}) %all-gather.7.cloned.1.call-update) | async-done | bytes 4718608 | tf_op jit(solution)/shard_map/all_gather | solution.py:784
  50.6 14.0 %attend.2 = (bf16[3,197,2304]{2,1,0:T(8,128)(2,1)}, bf16[3,197,768]{2,1,0:T(8,128)(2,1)}, f32[3,197,768]{2,1,0:T(8,128)}, bf16[3,197,768]{2,1,0:T(8,128)(2,1)}, f32[3,197,2]{2,1,0:T(8,128)}) custom-call(bf16[6,197,768]{2,1,0:T(8,128)(2,1)} %x_ref.7, s32[6,197,2]{2,1,0:T(8,128)} %copy.44.routes_ref, bf16[768,3072]{1,0:T(8,128)(2,1)} %all-gather.7.cloned.1.call-done.dense_ref, ...), custom_call_target="tpu_custom_call" | custom-call | flops 5577375744 | bytes 23961600 | tf_op jit(solution)/shard_map/attend/pallas_call | solution.py:300
  64.7 6.0 %dispatch.4 = bf16[8,184,768]{2,1,0:T(8,128)(2,1)} custom-call(s32[2,8,197]{2,1,0:T(8,128)} %get-tuple-element.49.lines_ref, bf16[3,197,768]{2,1,0:T(8,128)(2,1)} %get-tuple-element.50.rows_ref), custom_call_target="tpu_custom_call" | custom-call | flops 1336246272 | bytes 3168768 | tf_op jit(solution)/shard_map/dispatch/pallas_call | solution.py:215
  70.7 11.2 %all-to-all-done = bf16[8,184,768]{2,1,0:T(8,128)(2,1)S(1)} async-done(((bf16[8,184,768]{2,1,0:T(8,128)(2,1)}), bf16[8,184,768]{2,1,0:T(8,128)(2,1)S(1)}, u32[]{:S(2)}, u32[]{:S(2)}) %all-to-all-start) | async-done | bytes 2261024 | tf_op jit(solution)/shard_map/all_to_all | solution.py:798
  83.3 4.4 all-to-all-start.1
  88.5 6.1 %dispatch.6.refs_0_ = bf16[8,184,768]{2,1,0:T(8,128)(2,1)} custom-call(s32[2,8,197]{2,1,0:T(8,128)} %get-tuple-element.49.lines_ref, bf16[6,197,768]{2,1,0:T(8,128)(2,1)} %top_ref.3), custom_call_target="tpu_custom_call" | custom-call | flops 1336246272 | bytes 3168768 | tf_op jit(solution)/shard_map/dispatch/pallas_call | solution.py:215
  94.6 14.3 %attend.3 = (bf16[3,197,2304]{2,1,0:T(8,128)(2,1)}, bf16[3,197,768]{2,1,0:T(8,128)(2,1)}, f32[3,197,768]{2,1,0:T(8,128)}, bf16[3,197,768]{2,1,0:T(8,128)(2,1)}, f32[3,197,2]{2,1,0:T(8,128)}) custom-call(bf16[6,197,768]{2,1,0:T(8,128)(2,1)} %x_ref.7, s32[6,197,2]{2,1,0:T(8,128)} %copy.44.routes_ref, bf16[768,3072]{1,0:T(8,128)(2,1)} %all-gather.7.cloned.1.call-done.dense_ref, ...), custom_call_target="tpu_custom_call" | custom-call | flops 5577375744 | bytes 23961600 | tf_op jit(solution)/shard_map/attend/pallas_call | solution.py:300
  108.8 6.0 %dispatch.7.refs_1_ = bf16[8,184,768]{2,1,0:T(8,128)(2,1)} custom-call(s32[2,8,197]{2,1,0:T(8,128)} %get-tuple-element.49.lines_ref, bf16[3,197,768]{2,1,0:T(8,128)(2,1)} %get-tuple-element.52.rows_ref), custom_call_target="tpu_custom_call" | custom-call | flops 1336246272 | bytes 3168768 | tf_op jit(solution)/shard_map/dispatch/pallas_call | solution.py:215
  114.9 13.9 %all-gather.11.cloned.1.call-done = bf16[1,3072,768]{2,1,0:T(8,128)(2,1)} async-done(((bf16[1,768,768]{2,1,0:T(8,128)(2,1)}), bf16[1,3072,768]{2,1,0:T(8,128)(2,1)}) %all-gather.11.cloned.1.call-update) | async-done | bytes 4718608 | tf_op jit(solution)/shard_map/all_gather | solution.py:791
  128.7 10.2 %all-to-all-done.1 = bf16[8,184,768]{2,1,0:T(8,128)(2,1)} async-done(((bf16[8,184,768]{2,1,0:T(8,128)(2,1)}), bf16[8,184,768]{2,1,0:T(8,128)(2,1)}, u32[]{:S(2)}, u32[]{:S(2)}) %all-to-all-start.1) | async-done | bytes 2261024 | tf_op jit(solution)/shard_map/all_to_all | solution.py:798
  138.9 82.3 %expert_block.2 = (bf16[1472,768]{1,0:T(8,128)(2,1)}, bf16[1472,768]{1,0:T(8,128)(2,1)}, f32[3072,1664]{1,0:T(8,128)}, f32[16,768]{1,0:T(8,128)}, bf16[8,184,768...) custom-call(bf16[1472,768]{1,0:T(8,128)(2,1)} %bitcast.4.x_ref, bf16[1472,768]{1,0:T(8,128)(2,1)} %bitcast.34, ...), custom_call_target="tpu_custom_call" | custom-call | flops 41674604544 | bytes 37355520 | tf_op jit(solution)/shard_map/expert_block/pallas_call | solution.py:453
  221.3 96.0 %expert_block.3 = (bf16[1472,768]{1,0:T(8,128)(2,1)}, bf16[1472,768]{1,0:T(8,128)(2,1)}, bf16[3072,1664]{1,0:T(8,128)(2,1)}, f32[16,768]{1,0:T(8,128)}, bf16[8,184,768]{2,1,0:T(8,128)(2,1)}) custom-call(bf16[1472,768]{1,0:T(8,128)(2,1)} %bitcast.54, bf16[1472,768]{1,0:T(8,128)(2,1)} %bitcast.53, bf16[3072,768]{1,0:T(8,128)(2,1)} %bitcast.42, ...), custom_call_target="tpu_custom_call" | custom-call | flops 41674604544 | bytes 37355520 | tf_op jit(solution)/shard_map/expert_block/pallas_call | solution.py:453
  317.3 45.3 %attend_back.2 = (f32[3,197,768]{2,1,0:T(8,128)}, f32[768,3072]{1,0:T(8,128)}, f32[8,768]{1,0:T(8,128)}, bf16[8,184,768]{2,1,0:T(8,128)(2,1)}) custom-call(bf16[6,197,768]{2,1,0:T(8,128)(2,1)} %x_ref.7, bf16[6,197,768]{2,1,0:T(8,128)(2,1)} %top_ref.3, s32[6,197,2]{2,1,0:T(8,128)} %get-tuple-element.46.slots_ref, bf16[1472,768]{1,0:T(8,128)(2,1)} %bitcast.49, ...), custom_call_target="tpu_custom_call" | custom-call | flops 13943439360 | bytes 33398784 | tf_op jit(solution)/shard_map/attend_back/pallas_call | solution.py:731
  362.6 96.6 %attend_back.3 = (f32[3,197,768]{2,1,0:T(8,128)}, bf16[192,3200]{1,0:T(8,128)(2,1)}, bf16[8,184,768]{2,1,0:T(8,128)(2,1)}, bf16[8,184,768]{2,1,0:T(8,128)(2,1)}) custom-call(bf16[6,197,768]{2,1,0:T(8,128)(2,1)} %x_ref.7, bf16[6,197,768]{2,1,0:T(8,128)(2,1)} %top_ref.3, s32[6,197,2]{2,1,0:T(8,128)} %get-tuple-element.46.slots_ref, ...), custom_call_target="tpu_custom_call" | custom-call | flops 13943439360 | bytes 33398784 | tf_op jit(solution)/shard_map/attend_back/pallas_call | solution.py:731
  459.2 58.4 %all_to_all.20 = bf16[8,24,3200]{2,1,0:T(8,128)(2,1)S(1)} all-to-all(bf16[8,24,3200]{2,1,0:T(8,128)(2,1)} %bitcast.35), channel_id=1, replica_groups=mesh['dp'=4,'expert'=8] {'expert'}, dimensions={0} | all-to-all | bytes 2457600 | tf_op jit(solution)/shard_map/all_to_all | solution.py:798
  518.9 3.8 all-to-all-start.3
  522.7 6.5 %combine.2 = bf16[3,197,768]{2,1,0:T(8,128)(2,1)} custom-call(s32[6,197,2]{2,1,0:T(8,128)} %get-tuple-element.46.slots_ref, f32[3,197,2]{2,1,0:T(8,128)} %get-tuple-element.47.gates_ref, f32[3,197,768]{2,1,0:T(8,128)} %get-tuple-element.48.residual_ref, bf16[1472,768]{1,0:T(8,128)(2,1)} %bitcast.50), custom_call_target="tpu_custom_call" | custom-call | flops 2672492544 | bytes 4984320 | tf_op jit(solution)/shard_map/combine/pallas_call | solution.py:508
  529.2 6.5 %combine.3 = bf16[3,197,768]{2,1,0:T(8,128)(2,1)} custom-call(s32[6,197,2]{2,1,0:T(8,128)} %get-tuple-element.46.slots_ref, f32[3,197,2]{2,1,0:T(8,128)} %get-tuple-element.72.gates_ref, f32[3,197,768]{2,1,0:T(8,128)} %get-tuple-element.65.residual_ref, bf16[1472,768]{1,0:T(8,128)(2,1)} %bitcast.47), custom_call_target="tpu_custom_call" | custom-call | flops 2672492544 | bytes 4984320 | tf_op jit(solution)/shard_map/combine/pallas_call | solution.py:508
  535.7 2.7 pad_maximum_fusion.1
  540.6 11.2 %all-to-all-done.3 = bf16[8,24,3200]{2,1,0:T(8,128)(2,1)S(1)} async-done(((bf16[8,24,3200]{2,1,0:T(8,128)(2,1)}), bf16[8,24,3200]{2,1,0:T(8,128)(2,1)S(1)}, u32[]{:S(2)}, u32[]{:S(2)}) %all-to-all-start.3) | async-done | bytes 1228832 | tf_op jit(solution)/shard_map/all_to_all | solution.py:798
  (63 shorter events, 21.1 us)
Async XLA Ops:
  7.2 3.2 copy-start.4
  7.2 43.4 %all-gather.7.cloned.1.call-start = ((), (), s32[]{:S(2)}) async-start(), calls=%async_computation.5 | async-start | bytes 5898240 | tf_op jit(solution)/shard_map/all_gather | solution.py:784
  9.7 105.2 %all-gather.9.cloned.1.call-start = ((), (), s32[]{:S(2)}) async-start(), calls=%async_computation.7 | async-start | bytes 5898240 | tf_op jit(solution)/shard_map/all_gather | solution.py:790
  22.6 8.3 %copy-start.7 = (bf16[192]{0:T(256)(128)(2,1)S(1)}, bf16[192]{0:T(256)(128)(2,1)}, u32[]{:S(2)}) copy-start(bf16[192]{0:T(256)(128)(2,1)} %param.14) | copy-start | bytes 1156
  22.6 8.3 %copy-start.8 = (bf16[192]{0:T(256)(128)(2,1)S(1)}, bf16[192]{0:T(256)(128)(2,1)}, u32[]{:S(2)}) copy-start(bf16[192]{0:T(256)(128)(2,1)} %param.15) | copy-start | bytes 1156
  22.6 8.3 %copy-start.9 = (bf16[192]{0:T(256)(128)(2,1)S(1)}, bf16[192]{0:T(256)(128)(2,1)}, u32[]{:S(2)}) copy-start(bf16[192]{0:T(256)(128)(2,1)} %param.18) | copy-start | bytes 1156
  22.6 8.3 %copy-start.10 = (bf16[192]{0:T(256)(128)(2,1)S(1)}, bf16[192]{0:T(256)(128)(2,1)}, u32[]{:S(2)}) copy-start(bf16[192]{0:T(256)(128)(2,1)} %param.19) | copy-start | bytes 1156
  22.6 8.3 %copy-start.6 = (bf16[1,768]{1,0:T(2,128)(2,1)S(1)}, bf16[1,768]{1,0:T(2,128)(2,1)}, u32[]{:S(2)}) copy-start(bf16[1,768]{1,0:T(2,128)(2,1)} %param.22) | copy-start | bytes 4612
  22.6 8.4 %copy-start.5 = (bf16[192,8]{0,1:T(8,128)(2,1)S(1)}, bf16[192,8]{0,1:T(8,128)(2,1)}, u32[]{:S(2)}) copy-start(bf16[192,8]{0,1:T(8,128)(2,1)} %param.20) | copy-start | bytes 9220
  22.7 59.2 %all-to-all-start = ((bf16[8,184,768]{2,1,0:T(8,128)(2,1)}), bf16[8,184,768]{2,1,0:T(8,128)(2,1)S(1)}, u32[]{:S(2)}, u32[]{:S(2)}) async-start(bf16[8,184,768]{2,1,0:T(8,128)(2,1)} %dispatch.5), calls=%async_computation | async-start | bytes 4521984 | tf_op jit(solution)/shard_map/all_to_all | solution.py:798
  30.1 98.6 %all-gather.11.cloned.1.call-start = ((), (), s32[]{:S(2)}) async-start(), calls=%async_computation.8 | async-start | bytes 5898240 | tf_op jit(solution)/shard_map/all_gather | solution.py:791
  81.9 1.4 copy-start
  83.3 55.7 %all-to-all-start.1 = ((bf16[8,184,768]{2,1,0:T(8,128)(2,1)}), bf16[8,184,768]{2,1,0:T(8,128)(2,1)}, u32[]{:S(2)}, u32[]{:S(2)}) async-start(bf16[8,184,768]{2,1,0:T(8,128)(2,1)} %dispatch.4), calls=%async_computation.1 | async-start | bytes 4521984 | tf_op jit(solution)/shard_map/all_to_all | solution.py:798
  87.6 468.3 %reduce-scatter.2.cloned.1.call-start = ((), (), s32[]{:S(2)}) async-start(), calls=%async_computation.6 | async-start | bytes 12779520 | tf_op jit(solution)/shard_map/reduce_scatter | solution.py:827
  518.9 32.9 %all-to-all-start.3 = ((bf16[8,24,3200]{2,1,0:T(8,128)(2,1)}), bf16[8,24,3200]{2,1,0:T(8,128)(2,1)S(1)}, u32[]{:S(2)}, u32[]{:S(2)}) async-start(bf16[8,24,3200]{2,1,0:T(8,128)(2,1)} %broadcast_in_dim.32), calls=%async_computation.3 | async-start | bytes 2457600 | tf_op jit(solution)/shard_map/all_to_all | solution.py:798
  529.2 6.5 %copy-start.3 = (bf16[3,197,768]{2,1,0:T(8,128)(2,1)S(1)}, bf16[3,197,768]{2,1,0:T(8,128)(2,1)}, u32[]{:S(2)}) copy-start(bf16[3,197,768]{2,1,0:T(8,128)(2,1)} %combine.2) | copy-start | bytes 2723332
  535.7 2.7 copy-start.1
  535.7 2.7 copy-start.2
Sparse Core Ops, SparseCore 0:
  10.2 40.4 all-gather.6
  52.2 37.4 all-gather.8
  91.2 37.4 all-gather.10
  317.4 80.8 reduce-scatter.1

commit v3 on v2

--- a/solution.py
+++ b/solution.py
@@ -85,10 +85,16 @@
 
 
 class Rides:
-    def __init__(self, arrays):
-        self.arrays = list(arrays)
+    def __init__(self, entries):
+        self.arrays = [entry[0] for entry in entries]
+        self.rows = [pl.ds(entry[1], entry[2] - entry[1]) for entry in entries]
+        self.before = [entry[3] for entry in entries if entry[3] is not None]
+        self.filled = [index for index, entry in enumerate(entries) if entry[3] is not None]
+        arrays = self.arrays
         self.parts = arrays[0].shape[0]
-        self.in_specs = [pl.BlockSpec(memory_space=pl.ANY)] * len(arrays)
+        self.operands = self.arrays + self.before
+        self.in_specs = [pl.BlockSpec(memory_space=pl.ANY)] * len(self.operands)
+        self.out_specs = [pl.BlockSpec(memory_space=pl.ANY)] * len(arrays)
         self.out_shape = [jax.ShapeDtypeStruct(a.shape, a.dtype) for a in arrays]
         self.scratch = [
             pltpu.SemaphoreType.DMA((self.parts,)),
@@ -96,28 +102,33 @@
             pltpu.SemaphoreType.DMA,
         ] * len(arrays)
 
-    def copies(self, refs, offset):
+    def aliases(self, inputs, outputs):
+        first = inputs + len(self.arrays)
+        return {first + place: outputs + index for place, index in enumerate(self.filled)}
+
+    def copy(self, refs, index, offset):
         me = lax.axis_index("expert")
         peer = lax.rem(me + offset, self.parts)
         sources, targets, sems = refs
-        return [
-            pltpu.make_async_remote_copy(
-                src_ref=source.at[peer],
-                dst_ref=target.at[me],
-                send_sem=sems[3 * index].at[offset],
-                recv_sem=sems[3 * index + 1].at[offset],
-                device_id={"expert": peer},
-                device_id_type=pl.DeviceIdType.MESH,
-            )
-            for index, (source, target) in enumerate(zip(sources, targets))
-        ]
+        return pltpu.make_async_remote_copy(
+            src_ref=sources[index].at[peer, self.rows[index]],
+            dst_ref=targets[index].at[me, self.rows[index]],
+            send_sem=sems[3 * index].at[offset],
+            recv_sem=sems[3 * index + 1].at[offset],
+            device_id={"expert": peer},
+            device_id_type=pl.DeviceIdType.MESH,
+        )
 
     def own(self, refs):
         me = lax.axis_index("expert")
         sources, targets, sems = refs
         return [
-            pltpu.make_async_copy(source.at[me], target.at[me], sems[3 * index + 2])
-            for index, (source, target) in enumerate(zip(sources, targets))
+            pltpu.make_async_copy(
+                sources[index].at[me, self.rows[index]],
+                targets[index].at[me, self.rows[index]],
+                sems[3 * index + 2],
+            )
+            for index in range(len(sources))
         ]
 
     def start(self, refs, more=()):
@@ -138,11 +149,11 @@
             )
 
         pl.semaphore_wait(barrier, self.parts - 1 + len(more))
-
-        @pl.loop(1, self.parts)
-        def _(offset):
-            for copy in self.copies(refs, offset):
-                copy.start()
+        for index in range(len(self.rows)):
+
+            @pl.loop(1, self.parts)
+            def _(offset):
+                self.copy(refs, index, offset).start()
 
         for copy in self.own(refs):
             copy.start()
@@ -150,47 +161,51 @@
     def finish(self, refs):
         for copy in self.own(refs):
             copy.wait()
-
-        @pl.loop(1, self.parts)
-        def _(offset):
-            for copy in self.copies(refs, offset):
-                copy.wait()
-
-
-def route_kernel(experts, capacity, routes_ref, slots_ref, lines_ref):
+        for index in range(len(self.rows)):
+
+            @pl.loop(1, self.parts)
+            def _(offset):
+                self.copy(refs, index, offset).wait()
+
+
+def route_kernel(capacity, routes_ref, slots_ref, lines_ref):
     seq = routes_ref.shape[1]
     row = lax.broadcasted_iota(jnp.int32, (seq, seq), 0)
     col = lax.broadcasted_iota(jnp.int32, (seq, seq), 1)
     earlier = (col < row).astype(f32).astype(bf16)
     lane = lax.broadcasted_iota(jnp.int32, (seq, LANES), 1)
-    groups = routes_ref.shape[0] // IMG_MB
-    for group in range(groups):
-        base = jnp.zeros((1, LANES), f32)
-        table = jnp.full((seq, LANES), -1.0, f32)
-        for choice in range(TOP):
-            for image in range(IMG_MB):
-                index = group * IMG_MB + image
-                named = routes_ref[index][:, choice : choice + 1]
-                onehot = (lane == named).astype(f32)
-                count = dot(earlier, onehot.astype(bf16)) + base
-                position = jnp.sum(onehot * count, axis=1, keepdims=True).astype(jnp.int32)
-                base = base + jnp.sum(onehot, axis=0, keepdims=True)
-                slot = jnp.where(position < capacity, named * capacity + position, -1)
-                slots_ref[index, :, choice : choice + 1] = slot
-                table = jnp.where(lane == image * TOP + choice, slot.astype(f32), table)
-        lines_ref[group] = table.T[: lines_ref.shape[1]].astype(jnp.int32)
-
-
-def route(routes, experts, capacity):
+    base = jnp.zeros((1, LANES), f32)
+    table = jnp.full((seq, LANES), -1.0, f32)
+    for choice in range(TOP):
+        for image in range(IMG_MB):
+            named = routes_ref[image][:, choice : choice + 1]
+            onehot = (lane == named).astype(f32)
+            count = dot(earlier, onehot.astype(bf16)) + base
+            position = jnp.sum(onehot * count, axis=1, keepdims=True).astype(jnp.int32)
+            base = base + jnp.sum(onehot, axis=0, keepdims=True)
+            slot = jnp.where(position < capacity, named * capacity + position, -1)
+            slots_ref[image, :, choice : choice + 1] = slot
+            table = jnp.where(lane == image * TOP + choice, slot.astype(f32), table)
+    lines_ref[...] = table.T[: lines_ref.shape[0]].astype(jnp.int32)
+
+
+def route(routes, group, capacity):
+    seq = routes.shape[1]
     return pl.pallas_call(
-        functools.partial(route_kernel, experts, capacity),
+        functools.partial(route_kernel, capacity),
+        grid=(1,),
+        in_specs=[pl.BlockSpec((IMG_MB, seq, TOP), lambda i: (group, 0, 0))],
+        out_specs=[
+            pl.BlockSpec((IMG_MB, seq, TOP), lambda i: (0, 0, 0)),
+            pl.BlockSpec((8, seq), lambda i: (0, 0)),
+        ],
         out_shape=[
-            jax.ShapeDtypeStruct(routes.shape, jnp.int32),
-            jax.ShapeDtypeStruct((routes.shape[0] // IMG_MB, 8, routes.shape[1]), jnp.int32),
+            jax.ShapeDtypeStruct((IMG_MB, seq, TOP), jnp.int32),
+            jax.ShapeDtypeStruct((8, seq), jnp.int32),
         ],
-        compiler_params=pltpu.CompilerParams(vmem_limit_bytes=VMEM_LIMIT),
+        compiler_params=params(("arbitrary",)),
         cost_estimate=pl.CostEstimate(
-            flops=10**8, bytes_accessed=2 * 10**6, transcendentals=0
+            flops=10**8, bytes_accessed=10**6, transcendentals=0
         ),
         name="route",
     )(routes)
@@ -200,7 +215,7 @@
     first = pl.program_id(0) * capacity
     seq = rows_ref.shape[1]
     slot = lax.broadcasted_iota(jnp.int32, (capacity, seq), 0) + first
-    lines = lines_ref[0]
+    lines = lines_ref[...]
     acc = jnp.zeros((capacity, rows_ref.shape[2]), f32)
     for image in range(IMG_MB):
         at = image * TOP
@@ -211,13 +226,12 @@
 
 def dispatch(lines, rows, group, experts, capacity):
     seq, features = rows.shape[1:]
-    block = group if rows.shape[0] > IMG_MB else 0
     return pl.pallas_call(
         functools.partial(dispatch_kernel, capacity),
         grid=(experts,),
         in_specs=[
-            pl.BlockSpec((1, 8, seq), lambda e: (group, 0, 0)),
-            pl.BlockSpec((IMG_MB, seq, features), lambda e: (block, 0, 0)),
+            pl.BlockSpec((8, seq), lambda e: (0, 0)),
+            pl.BlockSpec((IMG_MB, seq, features), lambda e: (group, 0, 0)),
         ],
         out_specs=pl.BlockSpec((1, capacity, features), lambda e: (e, 0, 0)),
         out_shape=jax.ShapeDtypeStruct((experts, capacity, features), bf16),
@@ -232,9 +246,19 @@
 
 
 def attend_kernel(
-    experts, x_ref, routes_ref, dense_ref, small_ref,
-    proj_ref, mixed_ref, residual_ref, hidden_ref, gates_ref,
+    experts, rides, x_ref, routes_ref, lines_ref, dense_ref, small_ref, *refs
 ):
+    count = len(rides.arrays) if rides else 0
+    sources, refs = refs[:count], refs[count:]
+    proj_ref, mixed_ref, residual_ref, gates_ref, rows_ref = refs[:5]
+    targets, (hidden_ref, *sems) = refs[5 : 5 + count], refs[5 + count :]
+    step = pl.program_id(0)
+    if rides:
+
+        @pl.when(step == 0)
+        def _():
+            rides.start((sources, targets, sems))
+
     features = x_ref.shape[2]
     image = x_ref[0].astype(f32)
     vectors = small_ref[...].astype(f32)
@@ -268,7 +292,7 @@
     hidden = (
         normed * vectors[experts + 2 : experts + 3] + vectors[experts + 3 : experts + 4]
     ).astype(bf16)
-    hidden_ref[0] = hidden
+    hidden_ref[step] = hidden
     probs = softmax_lanes(dot_t(hidden, small_ref[...]), experts)
     lane = lax.broadcasted_iota(jnp.int32, probs.shape, 1)
     routes = routes_ref[0]
@@ -279,11 +303,37 @@
             keepdims=True,
         )
 
-
-def attend(images, routes, dense, small, experts, group):
+    @pl.when(step == pl.num_programs(0) - 1)
+    def _():
+        seq = x_ref.shape[1]
+        capacity = rows_ref.shape[1]
+        lines = lines_ref[...]
+        slot = lax.broadcasted_iota(jnp.int32, (capacity, seq), 0)
+
+        @pl.loop(0, experts)
+        def _(expert):
+            here = slot + expert * capacity
+            total = None
+            for index in range(IMG_MB):
+                at = index * TOP
+                holds = (lines[at : at + 1] == here) | (lines[at + 1 : at + 2] == here)
+                part = dot(holds.astype(f32).astype(bf16), hidden_ref[index])
+                total = part if total is None else total + part
+            rows_ref[expert] = total.astype(bf16)
+
+        if rides:
+            rides.finish((sources, targets, sems))
+
+
+def attend(
+    images, routes, lines, dense, small, experts, capacity, group, entries=(), collective=None
+):
     seq, features = images.shape[1:]
     wide = 3 * features
     first = group * IMG_MB
+    rides = Rides(entries) if entries else None
+    more = {"collective_id": collective, "has_side_effects": True} if entries else {}
+    slot_rows = (experts, capacity, features)
 
     def rows(width):
         return pl.BlockSpec((1, seq, width), lambda i: (i, 0, 0))
@@ -291,37 +341,45 @@
     def source(width):
         return pl.BlockSpec((1, seq, width), lambda i: (first + i, 0, 0))
 
-    def whole(array):
-        return pl.BlockSpec(array.shape, lambda i: (0, 0))
+    def whole(shape):
+        return pl.BlockSpec(
+            shape, lambda i: (0,) * len(shape), pipeline_mode=pl.Buffered(1)
+        )
 
     def out(width, dtype):
         return jax.ShapeDtypeStruct((IMG_MB, seq, width), dtype)
 
     return pl.pallas_call(
-        functools.partial(attend_kernel, experts),
+        functools.partial(attend_kernel, experts, rides),
         grid=(IMG_MB,),
         in_specs=[
             source(features),
             source(TOP),
-            whole(dense),
-            whole(small),
-        ],
-        out_specs=[rows(wide), rows(features), rows(features), rows(features), rows(TOP)],
+            whole(lines.shape),
+            whole(dense.shape),
+            whole(small.shape),
+        ]
+        + (rides.in_specs if rides else []),
+        out_specs=[rows(wide), rows(features), rows(features), rows(TOP), whole(slot_rows)]
+        + (rides.out_specs if rides else []),
         out_shape=[
             out(wide, bf16),
             out(features, bf16),
             out(features, f32),
-            out(features, bf16),
             out(TOP, f32),
-        ],
-        compiler_params=params(("arbitrary",)),
+            jax.ShapeDtypeStruct(slot_rows, bf16),
+        ]
+        + (rides.out_shape if rides else []),
+        scratch_shapes=[pltpu.VMEM((IMG_MB, seq, features), bf16)]
+        + (rides.scratch if rides else []),
+        compiler_params=params(("arbitrary",), **more),
         cost_estimate=pl.CostEstimate(
             flops=IMG_MB * seq * 16 * features * features,
             bytes_accessed=4 * features * (4 * features + IMG_MB * seq * 8),
             transcendentals=IMG_MB * HEADS * seq * seq,
         ),
         name="attend",
-    )(images, routes, dense, small)
+    )(images, routes, lines, dense, small, *(rides.operands if rides else []))
 
 
 def expert_kernel(
@@ -331,8 +389,9 @@
         old_w_ref, old_router_ref = refs[:2]
         refs = refs[2:]
     count = len(rides.arrays)
-    ride_refs = (refs[:count], refs[count + 4 : 2 * count + 4], refs[2 * count + 10 :])
-    refs = refs[count : count + 4] + refs[2 * count + 4 : 2 * count + 10]
+    sources, refs = refs[:count], refs[len(rides.operands) :]
+    ride_refs = (sources, refs[4 : count + 4], refs[count + 10 :])
+    refs = refs[:4] + refs[count + 4 : count + 10]
     (
         result_ref, dx_ref, dw_ref, drouter_ref,
         result_acc, dx_acc, dr_ref, probs_ref, act_ref, pre_ref,
@@ -419,7 +478,7 @@
     return best
 
 
-def expert_block(x, g, w1, w2, bias, small, experts, old, arrays, collective):
+def expert_block(x, g, w1, w2, bias, small, experts, old, entries, collective):
     rows, features = x.shape
     hidden_units = w1.shape[0]
     block = 512 if hidden_units % 512 == 0 else 256
@@ -427,7 +486,7 @@
     chunk = row_chunk(rows)
     add = old is not None
     out_type = bf16 if add else f32
-    rides = Rides(arrays)
+    rides = Rides(entries)
 
     def whole(shape):
         return pl.BlockSpec(
@@ -457,7 +516,7 @@
         out_specs=[
             whole(x.shape), whole(x.shape), unit_grads, whole(small.shape)
         ]
-        + rides.in_specs,
+        + rides.out_specs,
         out_shape=[
             jax.ShapeDtypeStruct(x.shape, bf16),
             jax.ShapeDtypeStruct(x.shape, bf16),
@@ -483,47 +542,205 @@
             transcendentals=rows * hidden_units,
         ),
         name="expert_block",
-    )(*operands, *rides.arrays)
-
-
-def combine_kernel(slots_ref, gates_ref, residual_ref, returned_ref, out_ref):
-    seq = slots_ref.shape[1]
-    total = returned_ref.shape[0]
-    column = lax.broadcasted_iota(jnp.int32, (seq, total), 1)
-    slots = slots_ref[0]
-    gates = gates_ref[0]
-    value = residual_ref[0]
-    mix = None
-    for choice in range(TOP):
-        holds = slots[:, choice : choice + 1] == column
-        picked = dot(holds.astype(f32).astype(bf16), returned_ref[...])
-        part = gates[:, choice : choice + 1] * picked
-        mix = part if mix is None else mix + part
-    out_ref[0] = (value + mix).astype(bf16)
-
-
-def combine(slots, gates, residual, returned, group):
-    seq, features = residual.shape[1:]
-    first = group * IMG_MB
+    )(*operands, *rides.operands)
+
+
+def inner_size(parts):
+    size = 1
+    while parts % (2 * size) == 0 and 4 * size * size <= parts:
+        size *= 2
+    return size
+
+
+def finish_kernel(
+    inner, outer, slots0_ref, slots1_ref, gates0_ref, gates1_ref, residual0_ref, residual1_ref,
+    returned0_ref, returned1_ref, part_ref, out_ref, din_ref, dout_ref, little_ref,
+    second_ref, full_ref, sems2, sems3, sems4,
+):
+    step = pl.program_id(0)
+    seq = slots0_ref.shape[1]
+    features = out_ref.shape[2]
+    width = part_ref.shape[2]
+    tiles = width // LANES
+    chunks = 3
+    edges = [LANES * (tiles * c // chunks) for c in range(chunks + 1)]
+    cuts = [pl.ds(edges[c], edges[c + 1] - edges[c]) for c in range(chunks)]
+    me = lax.axis_index("expert")
+    row = lax.rem(me, inner)
+    line = me // inner
+
+    def row_peer(hop):
+        return lax.rem(row + hop, inner)
+
+    def line_peer(hop):
+        return lax.rem(line + hop, outer)
+
+    def copy(source, target, sems, chunk, hop, peer):
+        return pltpu.make_async_remote_copy(
+            src_ref=source,
+            dst_ref=target,
+            send_sem=sems.at[0, chunk, hop - 1],
+            recv_sem=sems.at[1, chunk, hop - 1],
+            device_id={"expert": peer},
+            device_id_type=pl.DeviceIdType.MESH,
+        )
+
+    def reduce_lines(chunk):
+        at = cuts[chunk]
+        return [
+            copy(
+                part_ref.at[line_peer(hop), :, at], second_ref.at[hop - 1, :, at],
+                sems2, chunk, hop, line_peer(hop) * inner + row,
+            )
+            for hop in range(1, outer)
+        ]
+
+    def gather_lines(chunk):
+        at = cuts[chunk]
+        return [
+            copy(
+                full_ref.at[row, line, :, at], full_ref.at[row, line, :, at],
+                sems3, chunk, hop, line_peer(hop) * inner + row,
+            )
+            for hop in range(1, outer)
+        ]
+
+    def gather_rows(chunk):
+        at = cuts[chunk]
+        return [
+            copy(
+                full_ref.at[row, :, :, at], full_ref.at[row, :, :, at],
+                sems4, chunk, hop, line * inner + row_peer(hop),
+            )
+            for hop in range(1, inner)
+        ]
+
+    def start(copies):
+        for item in copies:
+            item.start()
+
+    def wait(copies):
+        for item in copies:
+            item.wait()
+
+    @pl.when(step == 0)
+    def _():
+        barrier = pltpu.get_barrier_semaphore()
+        peers = [line * inner + row_peer(hop) for hop in range(1, inner)]
+        peers += [line_peer(hop) * inner + row for hop in range(1, outer)]
+        for peer in peers:
+            pl.semaphore_signal(
+                barrier,
+                inc=1,
+                device_id={"expert": peer},
+                device_id_type=pl.DeviceIdType.MESH,
+            )
+        pl.semaphore_wait(barrier, len(peers))
+        for chunk in range(chunks):
+            start(reduce_lines(chunk))
+
+    column = lax.broadcasted_iota(jnp.int32, (seq, returned0_ref.shape[0]), 1)
+
+    def mix(slots_ref, gates_ref, residual_ref, returned_ref):
+        slots = slots_ref[0]
+        gates = gates_ref[0]
+        total = residual_ref[0]
+        for choice in range(TOP):
+            holds = slots[:, choice : choice + 1] == column
+            picked = dot(holds.astype(f32).astype(bf16), returned_ref[...])
+            total = total + gates[:, choice : choice + 1] * picked
+        out_ref[0] = total.astype(bf16)
+
+    @pl.when(step < IMG_MB)
+    def _():
+        mix(slots0_ref, gates0_ref, residual0_ref, returned0_ref)
+
+    @pl.when(step >= IMG_MB)
+    def _():
+        mix(slots1_ref, gates1_ref, residual1_ref, returned1_ref)
+
+    @pl.when(step == 1)
+    def _():
+        for chunk in range(chunks):
+            at = cuts[chunk]
+            wait(reduce_lines(chunk))
+            total = part_ref[line, :, at].astype(f32)
+            for hop in range(1, outer):
+                total = total + second_ref[hop - 1, :, at].astype(f32)
+            full_ref[row, line, :, at] = total.astype(bf16)
+            start(gather_lines(chunk))
+
+    @pl.when(step == 3)
+    def _():
+        for chunk in range(chunks):
+            wait(gather_lines(chunk))
+            start(gather_rows(chunk))
+
+    @pl.when(step == 2 * IMG_MB - 1)
+    def _():
+        for chunk in range(chunks):
+            wait(gather_rows(chunk))
+        for part in range(inner):
+            for place in range(outer):
+                block = part * outer + place
+                din_ref[block] = full_ref[part, place, :, : 3 * features].astype(f32)
+                dout_ref[block] = full_ref[part, place, :, 3 * features : 4 * features].astype(
+                    f32
+                )
+                little_ref[block] = full_ref[part, place, :, 4 * features :].astype(f32)
+
+
+def finish(slots, gates, residuals, returned, part, parts, collective):
+    outer, share, width = part.shape
+    inner = inner_size(parts)
+    seq = slots[0].shape[1]
+    images = IMG_MB * len(slots)
+    features = residuals[0].shape[2]
+    chunks = 3
+
+    def whole(shape):
+        return pl.BlockSpec(
+            shape, lambda i: (0,) * len(shape), pipeline_mode=pl.Buffered(1)
+        )
+
+    def early(width):
+        return pl.BlockSpec((1, seq, width), lambda i: (jnp.minimum(i, IMG_MB - 1), 0, 0))
+
+    def late(width):
+        return pl.BlockSpec((1, seq, width), lambda i: (jnp.maximum(i - IMG_MB, 0), 0, 0))
+
+    def each(width):
+        return pl.BlockSpec((1, seq, width), lambda i: (i, 0, 0))
+
+    outs = [3 * features, features, width - 4 * features]
     return pl.pallas_call(
-        combine_kernel,
-        grid=(IMG_MB,),
+        functools.partial(finish_kernel, inner, outer),
+        grid=(images,),
         in_specs=[
-            pl.BlockSpec((1, seq, TOP), lambda i: (first + i, 0, 0)),
-            pl.BlockSpec((1, seq, TOP), lambda i: (i, 0, 0)),
-            pl.BlockSpec((1, seq, features), lambda i: (i, 0, 0)),
-            pl.BlockSpec(returned.shape, lambda i: (0, 0)),
+            early(TOP), late(TOP), early(TOP), late(TOP), early(features), late(features),
+            whole(returned[0].shape), whole(returned[1].shape),
+            whole(part.shape),
         ],
-        out_specs=pl.BlockSpec((1, seq, features), lambda i: (i, 0, 0)),
-        out_shape=jax.ShapeDtypeStruct(residual.shape, bf16),
-        compiler_params=params(("arbitrary",)),
+        out_specs=[each(features)] + [whole((parts, share, size)) for size in outs],
+        out_shape=[jax.ShapeDtypeStruct((images, seq, features), bf16)]
+        + [jax.ShapeDtypeStruct((parts, share, size), f32) for size in outs],
+        scratch_shapes=[
+            pltpu.VMEM((outer - 1, share, width), bf16),
+            pltpu.VMEM((inner, outer, share, width), bf16),
+            pltpu.SemaphoreType.DMA((2, chunks, outer - 1)),
+            pltpu.SemaphoreType.DMA((2, chunks, outer - 1)),
+            pltpu.SemaphoreType.DMA((2, chunks, inner - 1)),
+        ],
+        compiler_params=params(
+            ("arbitrary",), collective_id=collective, has_side_effects=True
+        ),
         cost_estimate=pl.CostEstimate(
-            flops=4 * IMG_MB * seq * returned.shape[0] * features,
-            bytes_accessed=2 * features * (returned.shape[0] + 3 * IMG_MB * seq),
+            flops=4 * images * seq * returned[0].shape[0] * features,
+            bytes_accessed=2 * features * (2 * returned[0].shape[0] + 3 * images * seq),
             transcendentals=0,
         ),
-        name="combine",
-    )(slots, gates, residual, returned)
+        name="finish",
+    )(*slots, *gates, *residuals, *returned, part)
 
 
 def attend_back_kernel(
@@ -535,7 +752,7 @@
         refs = refs[3:]
     count = len(rides.arrays)
     outs = 2 if add else 3
-    sources, refs = refs[:count], refs[count:]
+    sources, refs = refs[:count], refs[len(rides.operands) :]
     grad_x_ref, ddense_ref = refs[:2]
     if not add:
         dsmall_ref = refs[2]
@@ -544,8 +761,9 @@
     refs = refs[4:]
     more = ()
     if add:
-        pack_ref, first_ref, second_ref, first_sems, second_sems = refs[:5]
-        refs = refs[5:]
+        pack_ref, first_ref, second_ref, part_ref, third_ref = refs[:5]
+        first_sems, second_sems, third_sems = refs[5:8]
+        refs = refs[8:]
         rank = lax.axis_index("dp")
         core = lax.rem(rank, 2)
         pairs = ranks // 2
@@ -676,19 +894,45 @@
                 copy.wait()
             for hop in range(1, pairs):
                 total = total + second_ref[hop - 1].astype(f32)
+            total = total.astype(bf16)
+            inner, outer, rows = part_ref.shape[:3]
+            for block in range(inner * outer):
+                part_ref[block // outer, block % outer] = total[block * rows : (block + 1) * rows]
+            me = lax.axis_index("expert")
+            row = lax.rem(me, inner)
+            copies = []
+            for hop in range(1, inner):
+                peer = lax.rem(row + hop, inner)
+                copies.append(
+                    pltpu.make_async_remote_copy(
+                        src_ref=part_ref.at[peer],
+                        dst_ref=third_ref.at[hop - 1],
+                        send_sem=third_sems.at[0, hop - 1],
+                        recv_sem=third_sems.at[1, hop - 1],
+                        device_id={"expert": me - row + peer},
+                        device_id_type=pl.DeviceIdType.MESH,
+                    )
+                )
+            for copy in copies:
+                copy.start()
+            for copy in copies:
+                copy.wait()
+            total = part_ref[row].astype(f32)
+            for hop in range(1, inner):
+                total = total + third_ref[hop - 1].astype(f32)
             ddense_ref[...] = total.astype(bf16)
         rides.finish(ride_refs)
 
 
 def attend_back(
     images, out_grad, slots, sent, proj, mixed, residual, dense, small, experts, group, old,
-    arrays, collective, ranks,
+    entries, collective, ranks,
 ):
     seq, features = images.shape[1:]
     wide = 3 * features
     first = group * IMG_MB
     add = old is not None
-    rides = Rides(arrays)
+    rides = Rides(entries)
 
     def rows(width):
         return pl.BlockSpec((1, seq, width), lambda i: (i, 0, 0))
@@ -701,7 +945,7 @@
 
     small_grads = (8, features)
     in_specs = [
-        source(features), source(features), source(TOP), whole(sent.shape),
+        source(features), source(features), rows(TOP), whole(sent.shape),
         rows(wide), rows(features), rows(features),
         whole(dense.shape), whole(small.shape),
     ]
@@ -715,14 +959,21 @@
         in_specs += [whole(array.shape) for array in old]
         operands += list(old)
         shard = (features // ranks, 4 * features + LANES)
-        out_specs[1] = whole(shard)
-        out_shape[1] = jax.ShapeDtypeStruct(shard, bf16)
+        inner = inner_size(experts)
+        part = (experts // inner, shard[0] // experts, shard[1])
+        out_specs[1] = pl.BlockSpec(
+            part, lambda i: (0, 0, 0), pipeline_mode=pl.Buffered(1)
+        )
+        out_shape[1] = jax.ShapeDtypeStruct(part, bf16)
         reduce_scratch = [
             pltpu.VMEM((2, ranks // 2, *shard), bf16),
             pltpu.VMEM((ranks // 2, *shard), bf16),
             pltpu.VMEM((ranks // 2 - 1, *shard), bf16),
+            pltpu.VMEM((inner, *part), bf16),
+            pltpu.VMEM((inner - 1, *part), bf16),
             pltpu.SemaphoreType.DMA((2,)),
             pltpu.SemaphoreType.DMA((2, ranks // 2 - 1)),
+            pltpu.SemaphoreType.DMA((2, inner - 1)),
         ]
     else:
         out_specs.append(whole(small_grads))
@@ -732,7 +983,7 @@
         functools.partial(attend_back_kernel, experts, add, rides, ranks),
         grid=(IMG_MB,),
         in_specs=in_specs + rides.in_specs,
-        out_specs=out_specs + rides.in_specs,
+        out_specs=out_specs + rides.out_specs,
         out_shape=out_shape + rides.out_shape,
         scratch_shapes=[
             pltpu.VMEM((features, 3 * features), f32),
@@ -742,6 +993,7 @@
         ]
         + reduce_scratch
         + rides.scratch,
+        input_output_aliases=rides.aliases(len(operands), len(out_specs)),
         compiler_params=params(
             ("arbitrary",), collective_id=collective, has_side_effects=True
         ),
@@ -751,7 +1003,7 @@
             transcendentals=IMG_MB * HEADS * seq * seq,
         ),
         name="attend_back",
-    )(*operands, *rides.arrays)
+    )(*operands, *rides.operands)
 
 
 def per_device(
@@ -789,14 +1041,6 @@
     small = small[:small_rows]
     weight_in = lax.all_gather(expert_in[0], "dp", axis=0, tiled=True)
     weight_out = lax.all_gather(expert_out[0], "dp", axis=0, tiled=True)
-    last = None
-
-    def exchange(rows):
-        nonlocal last
-        if last is not None:
-            rows, _ = lax.optimization_barrier((rows, last))
-        last = lax.all_to_all(rows, "expert", split_axis=0, concat_axis=0, tiled=True)
-        return last
 
     def flat(blocks):
         return blocks.reshape(slot_rows, features)
@@ -804,55 +1048,58 @@
     def blocks(rows):
         return rows.reshape(experts, capacity, features)
 
-    slots, lines = route(routes, experts, capacity)
-    grad_rows = [dispatch(lines, out_grad, group, experts, capacity) for group in range(micro)]
-    saved = []
-    token_rows = []
-    for group in range(micro):
-        proj, mixed, residual, hidden, gates = attend(
-            images, routes, dense, small, experts, group
-        )
-        saved.append((proj, mixed, residual, gates))
-        token_rows.append(dispatch(lines, hidden, group, experts, capacity))
-    grads = exchange(grad_rows[0])
-    received = exchange(token_rows[0])
+    routed = [route(routes, group, capacity) for group in range(micro)]
+    slots = [item[0] for item in routed]
+    lines = [item[1] for item in routed]
+    grad_rows = [
+        dispatch(lines[group], out_grad, group, experts, capacity) for group in range(micro)
+    ]
+    grads_0 = lax.all_to_all(grad_rows[0], "expert", split_axis=0, concat_axis=0, tiled=True)
+    *kept_0, token_rows_0 = attend(
+        images, routes, lines[0], dense, small, experts, capacity, 0
+    )
+    *kept_1, token_rows_1, received_0 = attend(
+        images, routes, lines[1], dense, small, experts, capacity, 1,
+        [(token_rows_0, 0, capacity, None)], 5,
+    )
+    saved = [kept_0, kept_1]
     result_0, dx_0, *old, grads_1, received_1 = expert_block(
-        flat(received), flat(grads), weight_in, weight_out, bias_row, small, experts, None,
-        [grad_rows[1], token_rows[1]], 0,
-    )
-    result_1, dx_1, dweights, drouter, sent = expert_block(
+        flat(received_0), flat(grads_0), weight_in, weight_out, bias_row, small, experts, None,
+        [(grad_rows[1], 0, capacity, None), (token_rows_1, 0, capacity, None)], 0,
+    )
+    early = max(8, capacity * 3 // 8 // 8 * 8)
+    result_1, dx_1, dweights, drouter, sent_0, returned_0 = expert_block(
         flat(received_1), flat(grads_1), weight_in, weight_out, bias_row, small, experts, old,
-        [blocks(dx_0)], 1,
+        [(blocks(dx_0), 0, capacity, None), (blocks(result_0), 0, early, None)], 1,
     )
     dweights = lax.psum_scatter(dweights, "dp", scatter_dimension=0, tiled=True)
     proj, mixed, residual, _ = saved[0]
     grad_x_0, *old, sent_1 = attend_back(
-        images, out_grad, slots, flat(sent), proj, mixed, residual, dense, small,
-        experts, 0, None, [blocks(dx_1)], 2, ranks,
+        images, out_grad, slots[0], flat(sent_0), proj, mixed, residual, dense, small,
+        experts, 0, None, [(blocks(dx_1), 0, capacity, None)], 2, ranks,
     )
     proj, mixed, residual, _ = saved[1]
     grad_x_1, ddense, returned_0, returned_1 = attend_back(
-        images, out_grad, slots, flat(sent_1), proj, mixed, residual, dense, small,
-        experts, 1, old + [drouter], [blocks(result_0), blocks(result_1)], 3, ranks,
+        images, out_grad, slots[1], flat(sent_1), proj, mixed, residual, dense, small,
+        experts, 1, old + [drouter],
+        [(blocks(result_0), early, capacity, returned_0), (blocks(result_1), 0, capacity, None)],
+        3, ranks,
     )
     grad_blocks = [grad_x_0, grad_x_1]
-    out_blocks = [
-        combine(slots, saved[group][3], saved[group][2], flat(returned), group)
-        for group, returned in enumerate((returned_0, returned_1))
-    ]
-    share = ddense.shape[0] // experts
-    shares = exchange(ddense.reshape(experts, share, ddense.shape[1]))
-    total = jnp.sum(shares.astype(f32), axis=0, keepdims=True).astype(bf16)
-    ddense = exchange(jnp.broadcast_to(total, shares.shape)).reshape(ddense.shape).astype(f32)
-    little = ddense[:, 4 * features :].T
+    block_out, grad_attn_in, grad_attn_out, little = finish(
+        slots, [item[3] for item in saved], [item[2] for item in saved],
+        [flat(returned_0), flat(returned_1)],
+        ddense, experts, 4,
+    )
+    little = little.reshape(own, -1).T
     dweights = dweights.astype(f32)
     return (
-        jnp.concatenate(out_blocks, axis=0),
+        block_out,
         jnp.concatenate(grad_blocks, axis=0),
         little[0],
         little[1],
-        ddense[:, : 3 * features],
-        ddense[:, 3 * features : 4 * features],
+        grad_attn_in.reshape(own, -1),
+        grad_attn_out.reshape(own, -1),
         little[2],
         little[3],
         little[8 : 8 + experts].T,

time: 577 us -> 540 us (0.936)
  Pallas kernels: 391 us -> 464 us
  blocking collectives: 63.8 us -> 5.42 us
  waiting for transfers between devices: 61.3 us -> 21 us
  starting transfers between devices: 15.8 us -> 7.55 us
    pallas_call x5, Pallas kernels: 46.4 us -> 114 us  [the longest x2 64.6 us: attend(): pl.pallas_call(functools.partial(attend_kernel, experts, rides), grid=(IM...]
    all_to_all x1 -> x0, blocking collectives: 58.4 us -> none  [exchange(): lax.all_to_all(rows, 'expert', split_axis=0, concat_axis=0, tiled=True)]
    all_to_all x3 -> x1, waiting for transfers between devices: 32.7 us -> 0.01 us  [per_device(): lax.all_to_all(grad_rows[0], 'expert', split_axis=0, concat_axis=0, tiled...]
    pallas_call x4 -> x2, Pallas kernels: 24.1 us -> 12 us  [dispatch(): pl.pallas_call(functools.partial(dispatch_kernel, capacity), grid=(expert...]
    pallas_call x2, Pallas kernels: 142 us -> 154 us  [attend_back(): pl.pallas_call(functools.partial(attend_back_kernel, experts, add, rides,...]
    all_to_all x3 -> x1, starting transfers between devices: 15.6 us -> 7.39 us  [per_device(): lax.all_to_all(grad_rows[0], 'expert', split_axis=0, concat_axis=0, tiled...]
    all_gather x1, waiting for transfers between devices: 13.3 us -> 6.15 us  [per_device(): lax.all_gather(jnp.concatenate([attn_in, attn_out], axis=1), 'dp', axis=0...]
  transfers between devices with their start and end apart: 7 -> 5, of which waited for: 5 -> 2; matrix products, arithmetic and copies ran while one was open for 2% -> 2% of each run, Pallas kernels for 37% -> 53%
where the time goes in v3:
time: 540 us; the launch traced here: 532 us
  Pallas kernels  464 us (86%)
  waiting for transfers between devices  21 us (4%)
  between operations  14.2 us (3%)
  local copies, waits for them, and re-layouts  11.8 us (2%)
  other arithmetic  8.15 us (2%)
  starting transfers between devices  7.55 us (1%)
  blocking collectives  5.42 us (1%)
    pallas_call x2, Pallas kernels, expert_block(): pl.pallas_call(functools.partial(expert_kernel, experts, chunk, add, ride...  184 us
    pallas_call x2, Pallas kernels, attend_back(): pl.pallas_call(functools.partial(attend_back_kernel, experts, add, rides,...  154 us
    pallas_call x2, Pallas kernels, attend(): pl.pallas_call(functools.partial(attend_kernel, experts, rides), grid=(IM...  64.6 us
    pallas_call x1, Pallas kernels, finish(): pl.pallas_call(functools.partial(finish_kernel, inner, outer), grid=(imag...  44.3 us
    all_gather x1, waiting for transfers between devices, per_device(): weight_out = lax.all_gather(expert_out[0], 'dp', axis=0, tiled=True)  13.4 us
    pallas_call x2, Pallas kernels, dispatch(): pl.pallas_call(functools.partial(dispatch_kernel, capacity), grid=(expert...  12 us
  transfers between devices with their start and end apart: 5, of which 2 were waited for; matrix products, arithmetic and copies ran while one was open for 2% of the time, Pallas kernels for 53%

profile of v3, /device:TPU:0, one launch (start us, length us, event | category | flops | bytes accessed | tf_op | source)
XLA Modules:
  0.0 532.2 jit_solution(1610701928452263460)
XLA Ops:
  7.2 2.4 pad_maximum_fusion.1
  11.2 1.1 copy.40.routes_ref
  12.3 2.8 route.2
  15.0 6.0 %dispatch.2 = bf16[8,184,768]{2,1,0:T(8,128)(2,1)} custom-call(s32[8,197]{1,0:T(8,128)} %get-tuple-element.53.lines_ref, bf16[6,197,768]{2,1,0:T(8,128)(2,1)} %top_ref.3), custom_call_target="tpu_custom_call" | custom-call | flops 1336246272 | bytes 3168768 | tf_op jit(solution)/shard_map/dispatch/pallas_call | solution.py:229
  21.1 7.4 %all-to-all-start = ((bf16[8,184,768]{2,1,0:T(8,128)(2,1)}), bf16[8,184,768]{2,1,0:T(8,128)(2,1)S(1)}, u32[]{:S(2)}, u32[]{:S(2)}) async-start(bf16[8,184,768]{2,1,0:T(8,128)(2,1)} %dispatch.2), calls=%async_computation | async-start | bytes 4521984 | tf_op jit(solution)/shard_map/all_to_all | solution.py:1057
  28.8 5.4 %all-gather.2 = bf16[4,192,20]{1,2,0:T(8,128)(2,1)S(1)} all-gather(bf16[1,192,20]{1,2,0:T(8,128)(2,1)S(1)} %bitcast.44), channel_id=1, replica_groups=mesh['dp'=4,'expert'=8] {'dp'}, dimensions={0}, use_global_device_ids=true | all-gather | bytes 38400 | tf_op jit(solution)/shard_map/all_gather | solution.py:1039
  35.7 2.8 route.3
  38.5 6.0 %dispatch.3.refs_0_ = bf16[8,184,768]{2,1,0:T(8,128)(2,1)} custom-call(s32[8,197]{1,0:T(8,128)} %get-tuple-element.55.lines_ref, bf16[6,197,768]{2,1,0:T(8,128)(2,1)} %top_ref.3), custom_call_target="tpu_custom_call" | custom-call | flops 1336246272 | bytes 3168768 | tf_op jit(solution)/shard_map/dispatch/pallas_call | solution.py:229
  44.5 6.2 %all-gather.7.cloned.1.call-done.dense_ref = bf16[768,3072]{1,0:T(8,128)(2,1)} async-done(((bf16[192,3072]{1,0:T(8,128)(2,1)}), bf16[768,3072]{1,0:T(8,128)(2,1)}) %all-gather.7.cloned.1.call-update) | async-done | bytes 4718608 | tf_op jit(solution)/shard_map/all_gather | solution.py:1036
  50.7 18.6 %attend.2 = (bf16[3,197,2304]{2,1,0:T(8,128)(2,1)}, bf16[3,197,768]{2,1,0:T(8,128)(2,1)}, f32[3,197,768]{2,1,0:T(8,128)}, f32[3,197,2]{2,1,0:T(8,128)}, bf16[8,184,768]{2,1,0:T(8,128)(2,1)}) custom-call(bf16[6,197,768]{2,1,0:T(8,128)(2,1)} %x_ref.7, s32[6,197,2]{2,1,0:T(8,128)} %copy.40.routes_ref, s32[8,197]{1,0:T(8,128)} %get-tuple-element.53.lines_ref, ...), custom_call_target="tpu_custom_call" | custom-call | flops 5577375744 | bytes 23961600 | tf_op jit(solution)/shard_map/attend/pallas_call | solution.py:352
  69.2 46.1 %attend.3 = (bf16[3,197,2304]{2,1,0:T(8,128)(2,1)}, bf16[3,197,768]{2,1,0:T(8,128)(2,1)}, f32[3,197,768]{2,1,0:T(8,128)}, f32[3,197,2]{2,1,0:T(8,128)}, bf16[8,1...) custom-call(bf16[6,197,768]{2,1,0:T(8,128)(2,1)} %x_ref.7, s32[6,197,2]{2,1,0:T(8,128)} %copy.40.routes_ref, ...), custom_call_target="tpu_custom_call" | custom-call | flops 5577375744 | bytes 23961600 | tf_op jit(solution)/shard_map/attend/pallas_call | solution.py:352
  115.3 13.4 %all-gather.11.cloned.1.call-done = bf16[1,3072,768]{2,1,0:T(8,128)(2,1)} async-done(((bf16[1,768,768]{2,1,0:T(8,128)(2,1)}), bf16[1,3072,768]{2,1,0:T(8,128)(2,1)}) %all-gather.11.cloned.1.call-update) | async-done | bytes 4718608 | tf_op jit(solution)/shard_map/all_gather | solution.py:1043
  128.7 94.0 %expert_block.2 = (bf16[1472,768]{1,0:T(8,128)(2,1)}, bf16[1472,768]{1,0:T(8,128)(2,1)}, f32[3072,1664]{1,0:T(8,128)}, f32[16,768]{1,0:T(8,128)}, bf16[8,184,768...) custom-call(bf16[1472,768]{1,0:T(8,128)(2,1)} %bitcast.61, bf16[1472,768]{1,0:T(8,128)(2,1)} %bitcast.36, ...), custom_call_target="tpu_custom_call" | custom-call | flops 41674604544 | bytes 37355520 | tf_op jit(solution)/shard_map/expert_block/pallas_call | solution.py:512
  222.7 89.7 %expert_block.3 = (bf16[1472,768]{1,0:T(8,128)(2,1)}, bf16[1472,768]{1,0:T(8,128)(2,1)}, bf16[3072,1664]{1,0:T(8,128)(2,1)}, f32[16,768]{1,0:T(8,128)}, bf16[8,1...) custom-call(bf16[1472,768]{1,0:T(8,128)(2,1)} %bitcast.66, bf16[1472,768]{1,0:T(8,128)(2,1)} %bitcast.65, ...), custom_call_target="tpu_custom_call" | custom-call | flops 41674604544 | bytes 37355520 | tf_op jit(solution)/shard_map/expert_block/pallas_call | solution.py:512
  312.5 51.4 %attend_back.2 = (f32[3,197,768]{2,1,0:T(8,128)}, f32[768,3072]{1,0:T(8,128)}, f32[8,768]{1,0:T(8,128)}, bf16[8,184,768]{2,1,0:T(8,128)(2,1)}) custom-call(bf16[6,197,768]{2,1,0:T(8,128)(2,1)} %x_ref.7, bf16[6,197,768]{2,1,0:T(8,128)(2,1)} %top_ref.3, s32[3,197,2]{2,1,0:T(8,128)} %get-tuple-element.51.slots_ref.slots0_ref, bf16[1472,768]{1,0:T(8,128)(2,1)} %bitcast.60, ...), custom_call_target="tpu_custom_call" | custom-call | flops 13943439360 | bytes 33398784 | tf_op jit(solution)/shard_map/attend_back/pallas_call | solution.py:982
  363.9 102.5 %attend_back.3 = (f32[3,197,768]{2,1,0:T(8,128)}, bf16[4,24,3200]{2,1,0:T(8,128)(2,1)}, bf16[8,184,768]{2,1,0:T(8,128)(2,1)}, bf16[8,184,768]{2,1,0:T(8,128)(2,1)}) custom-call(bf16[6,197,768]{2,1,0:T(8,128)(2,1)} %x_ref.7, bf16[6,197,768]{2,1,0:T(8,128)(2,1)} %top_ref.3, ...), custom_call_target="tpu_custom_call", output_to_operand_aliasing={{2}: (14, {})} | custom-call | flops 13943439360 | bytes 33398784 | tf_op jit(solution)/shard_map/attend_back/pallas_call | solution.py:982
  466.5 44.3 %finish.1 = (bf16[6,197,768]{2,1,0:T(8,128)(2,1)}, f32[8,24,2304]{2,1,0:T(8,128)}, f32[8,24,768]{2,1,0:T(8,128)}, f32[8,24,128]{2,1,0:T(8,128)}) custom-call(s32[3,197,2]{2,1,0:T(8,128)} %get-tuple-element.51.slots_ref.slots0_ref, s32[3,197,2]{2,1,0:T(8,128)} %get-tuple-element.52.slots_ref.slots1_ref, f32[3,197,2]{2,1,0:T(8,128)} %get-tuple-element.54.gates0_ref, ...), custom_call_target="tpu_custom_call" | custom-call | flops 5344985088 | bytes 9968640 | tf_op jit(solution)/shard_map/finish/pallas_call | solution.py:716
  510.8 1.0 copy.46
  511.8 3.7 pad_maximum_fusion
  516.6 2.1 convert_element_type.3
  518.9 2.5 slice_bitcast_fusion
  522.0 1.2 copy.51
  523.2 1.2 copy.52
  524.7 0.8 copy.53
  (54 shorter events, 5.5 us)
Async XLA Ops:
  7.2 43.5 %all-gather.7.cloned.1.call-start = ((), (), s32[]{:S(2)}) async-start(), calls=%async_computation.2 | async-start | bytes 5898240 | tf_op jit(solution)/shard_map/all_gather | solution.py:1036
  9.6 1.5 copy-start.5
  9.7 105.7 %all-gather.9.cloned.1.call-start = ((), (), s32[]{:S(2)}) async-start(), calls=%async_computation.4 | async-start | bytes 5898240 | tf_op jit(solution)/shard_map/all_gather | solution.py:1042
  10.4 118.3 %all-gather.11.cloned.1.call-start = ((), (), s32[]{:S(2)}) async-start(), calls=%async_computation.5 | async-start | bytes 5898240 | tf_op jit(solution)/shard_map/all_gather | solution.py:1043
  21.0 7.5 %copy-start.8 = (bf16[192]{0:T(256)(128)(2,1)S(1)}, bf16[192]{0:T(256)(128)(2,1)}, u32[]{:S(2)}) copy-start(bf16[192]{0:T(256)(128)(2,1)} %param.14) | copy-start | bytes 1156
  21.0 7.5 %copy-start.9 = (bf16[192]{0:T(256)(128)(2,1)S(1)}, bf16[192]{0:T(256)(128)(2,1)}, u32[]{:S(2)}) copy-start(bf16[192]{0:T(256)(128)(2,1)} %param.15) | copy-start | bytes 1156
  21.0 7.5 %copy-start.10 = (bf16[192]{0:T(256)(128)(2,1)S(1)}, bf16[192]{0:T(256)(128)(2,1)}, u32[]{:S(2)}) copy-start(bf16[192]{0:T(256)(128)(2,1)} %param.18) | copy-start | bytes 1156
  21.0 7.5 %copy-start.11 = (bf16[192]{0:T(256)(128)(2,1)S(1)}, bf16[192]{0:T(256)(128)(2,1)}, u32[]{:S(2)}) copy-start(bf16[192]{0:T(256)(128)(2,1)} %param.19) | copy-start | bytes 1156
  21.0 7.6 %copy-start.7 = (bf16[1,768]{1,0:T(2,128)(2,1)S(1)}, bf16[1,768]{1,0:T(2,128)(2,1)}, u32[]{:S(2)}) copy-start(bf16[1,768]{1,0:T(2,128)(2,1)} %param.22) | copy-start | bytes 4612
  21.1 7.7 %copy-start.6 = (bf16[192,8]{0,1:T(8,128)(2,1)S(1)}, bf16[192,8]{0,1:T(8,128)(2,1)}, u32[]{:S(2)}) copy-start(bf16[192,8]{0,1:T(8,128)(2,1)} %param.20) | copy-start | bytes 9220
  21.1 94.2 %all-to-all-start = ((bf16[8,184,768]{2,1,0:T(8,128)(2,1)}), bf16[8,184,768]{2,1,0:T(8,128)(2,1)S(1)}, u32[]{:S(2)}, u32[]{:S(2)}) async-start(bf16[8,184,768]{2,1,0:T(8,128)(2,1)} %dispatch.2), calls=%async_computation | async-start | bytes 4521984 | tf_op jit(solution)/shard_map/all_to_all | solution.py:1057
  28.5 488.2 %reduce-scatter.2.cloned.1.call-start = ((), (), s32[]{:S(2)}) async-start(), calls=%async_computation.3 | async-start | bytes 12779520 | tf_op jit(solution)/shard_map/reduce_scatter | solution.py:1075
  115.3 13.5 %copy-start = (bf16[8,184,768]{2,1,0:T(8,128)(2,1)}, bf16[8,184,768]{2,1,0:T(8,128)(2,1)S(1)}, u32[]{:S(2)}) copy-start(bf16[8,184,768]{2,1,0:T(8,128)(2,1)S(1)} %all-to-all-done) | copy-start | bytes 6782980
  466.5 45.3 %copy-start.1 = (f32[3,197,768]{2,1,0:T(8,128)S(1)}, f32[3,197,768]{2,1,0:T(8,128)}, u32[]{:S(2)}) copy-start(f32[3,197,768]{2,1,0:T(8,128)} %get-tuple-element.84) | copy-start | bytes 5446660
  518.9 3.1 copy-start.2
  521.4 1.8 copy-start.3
  523.2 1.5 copy-start.4
Sparse Core Ops, SparseCore 0:
  10.1 40.4 all-gather.6
  52.2 37.4 all-gather.8
  91.2 37.4 all-gather.10
  312.6 88.6 reduce-scatter.1

commit v4 on v3

--- a/solution.py
+++ b/solution.py
@@ -166,6 +166,14 @@
             @pl.loop(1, self.parts)
             def _(offset):
                 self.copy(refs, index, offset).wait()
+
+
+HBM = pl.BlockSpec(memory_space=pl.ANY)
+
+
+def staged(*arrays):
+    buffers = [pltpu.VMEM(array.shape, array.dtype) for array in arrays]
+    return buffers + [pltpu.SemaphoreType.DMA((4,))]
 
 
 def route_kernel(capacity, routes_ref, slots_ref, lines_ref):
@@ -246,18 +254,21 @@
 
 
 def attend_kernel(
-    experts, rides, x_ref, routes_ref, lines_ref, dense_ref, small_ref, *refs
+    experts, rides, x_ref, routes_ref, lines_ref, dense_hbm, small_ref, *refs
 ):
     count = len(rides.arrays) if rides else 0
     sources, refs = refs[:count], refs[count:]
     proj_ref, mixed_ref, residual_ref, gates_ref, rows_ref = refs[:5]
-    targets, (hidden_ref, *sems) = refs[5 : 5 + count], refs[5 + count :]
+    targets, (hidden_ref, dense_ref, load_sem, *sems) = refs[5 : 5 + count], refs[5 + count :]
     step = pl.program_id(0)
-    if rides:
-
-        @pl.when(step == 0)
-        def _():
+    load = pltpu.make_async_copy(dense_hbm, dense_ref, load_sem.at[0])
+
+    @pl.when(step == 0)
+    def _():
+        if rides:
             rides.start((sources, targets, sems))
+        load.start()
+        load.wait()
 
     features = x_ref.shape[2]
     image = x_ref[0].astype(f32)
@@ -356,7 +367,7 @@
             source(features),
             source(TOP),
             whole(lines.shape),
-            whole(dense.shape),
+            HBM,
             whole(small.shape),
         ]
         + (rides.in_specs if rides else []),
@@ -370,7 +381,7 @@
             jax.ShapeDtypeStruct(slot_rows, bf16),
         ]
         + (rides.out_shape if rides else []),
-        scratch_shapes=[pltpu.VMEM((IMG_MB, seq, features), bf16)]
+        scratch_shapes=[pltpu.VMEM((IMG_MB, seq, features), bf16), *staged(dense)]
         + (rides.scratch if rides else []),
         compiler_params=params(("arbitrary",), **more),
         cost_estimate=pl.CostEstimate(
@@ -383,19 +394,28 @@
 
 
 def expert_kernel(
-    experts, chunk, add, rides, x_ref, g_ref, w1_ref, w2_ref, bias_ref, small_ref, *refs
+    experts, chunk, add, rides, x_hbm, g_hbm, w1_ref, w2_ref, bias_ref, small_ref, *refs
 ):
     if add:
         old_w_ref, old_router_ref = refs[:2]
         refs = refs[2:]
     count = len(rides.arrays)
     sources, refs = refs[:count], refs[len(rides.operands) :]
-    ride_refs = (sources, refs[4 : count + 4], refs[count + 10 :])
-    refs = refs[:4] + refs[count + 4 : count + 10]
+    ride_refs = (sources, refs[4 : count + 4], refs[count + 15 :])
+    refs = refs[:4] + refs[count + 4 : count + 15]
     (
-        result_ref, dx_ref, dw_ref, drouter_ref,
+        result_hbm, dx_hbm, dw_ref, drouter_ref,
         result_acc, dx_acc, dr_ref, probs_ref, act_ref, pre_ref,
+        x_ref, g_ref, result_ref, dx_ref, copy_sems,
     ) = refs
+    loads = [
+        pltpu.make_async_copy(x_hbm, x_ref, copy_sems.at[0]),
+        pltpu.make_async_copy(g_hbm, g_ref, copy_sems.at[1]),
+    ]
+    stores = [
+        pltpu.make_async_copy(result_ref, result_hbm, copy_sems.at[2]),
+        pltpu.make_async_copy(dx_ref, dx_hbm, copy_sems.at[3]),
+    ]
     step = pl.program_id(0)
     last = pl.num_programs(0) - 1
     rows = x_ref.shape[0]
@@ -405,9 +425,10 @@
     @pl.when(step == 0)
     def _():
         rides.start(ride_refs)
-
-    @pl.when(step == 0)
-    def _():
+        for load in loads:
+            load.start()
+        for load in loads:
+            load.wait()
         for index in range(chunks):
             at = pl.ds(index * chunk, chunk)
             probs = softmax_lanes(dot_t(x_ref[at, :], small_ref[...]), experts)
@@ -467,7 +488,11 @@
             ).astype(bf16)
             drouter = drouter + t_dot(high, x_ref[at, :]) + t_dot(low, x_ref[at, :])
         drouter_ref[...] = drouter
+        for store in stores:
+            store.start()
         rides.finish(ride_refs)
+        for store in stores:
+            store.wait()
 
 
 def row_chunk(rows):
@@ -498,8 +523,8 @@
     units = pl.BlockSpec((block, features), lambda s: (s, 0))
     unit_row = pl.BlockSpec((1, block), lambda s: (0, s))
     in_specs = [
-        whole(x.shape),
-        whole(g.shape),
+        HBM,
+        HBM,
         units,
         units,
         unit_row,
@@ -514,7 +539,7 @@
         grid=(steps,),
         in_specs=in_specs + rides.in_specs,
         out_specs=[
-            whole(x.shape), whole(x.shape), unit_grads, whole(small.shape)
+            HBM, HBM, unit_grads, whole(small.shape)
         ]
         + rides.out_specs,
         out_shape=[
@@ -531,6 +556,7 @@
             pltpu.VMEM((rows, small.shape[0]), f32),
             pltpu.VMEM((rows, block), bf16),
             pltpu.VMEM((rows, block), bf16),
+            *staged(x, g, x, x),
         ]
         + rides.scratch,
         compiler_params=params(
@@ -554,8 +580,8 @@
 
 def finish_kernel(
     inner, outer, slots0_ref, slots1_ref, gates0_ref, gates1_ref, residual0_ref, residual1_ref,
-    returned0_ref, returned1_ref, part_ref, out_ref, din_ref, dout_ref, little_ref,
-    second_ref, full_ref, sems2, sems3, sems4,
+    returned0_hbm, returned1_hbm, part_ref, out_ref, din_ref, dout_ref, little_ref,
+    returned0_ref, returned1_ref, load_sems, second_ref, full_ref, sems2, sems3, sems4,
 ):
     step = pl.program_id(0)
     seq = slots0_ref.shape[1]
@@ -614,6 +640,11 @@
             )
             for hop in range(1, inner)
         ]
+
+    loads = [
+        pltpu.make_async_copy(returned0_hbm, returned0_ref, load_sems.at[0]),
+        pltpu.make_async_copy(returned1_hbm, returned1_ref, load_sems.at[1]),
+    ]
 
     def start(copies):
         for item in copies:
@@ -638,6 +669,12 @@
         pl.semaphore_wait(barrier, len(peers))
         for chunk in range(chunks):
             start(reduce_lines(chunk))
+        start(loads)
+        wait(loads[:1])
+
+    @pl.when(step == IMG_MB)
+    def _():
+        wait(loads[1:])
 
     column = lax.broadcasted_iota(jnp.int32, (seq, returned0_ref.shape[0]), 1)
 
@@ -718,13 +755,13 @@
         grid=(images,),
         in_specs=[
             early(TOP), late(TOP), early(TOP), late(TOP), early(features), late(features),
-            whole(returned[0].shape), whole(returned[1].shape),
-            whole(part.shape),
+            HBM, HBM, whole(part.shape),
         ],
         out_specs=[each(features)] + [whole((parts, share, size)) for size in outs],
         out_shape=[jax.ShapeDtypeStruct((images, seq, features), bf16)]
         + [jax.ShapeDtypeStruct((parts, share, size), f32) for size in outs],
         scratch_shapes=[
+            *staged(*returned),
             pltpu.VMEM((outer - 1, share, width), bf16),
             pltpu.VMEM((inner, outer, share, width), bf16),
             pltpu.SemaphoreType.DMA((2, chunks, outer - 1)),
@@ -744,8 +781,8 @@
 
 
 def attend_back_kernel(
-    experts, add, rides, ranks, x_ref, top_ref, slots_ref, sent_ref, proj_ref, mixed_ref, residual_ref,
-    dense_ref, small_ref, *refs
+    experts, add, rides, ranks, x_ref, top_ref, slots_ref, sent_hbm, proj_ref, mixed_ref, residual_ref,
+    dense_hbm, small_ref, *refs
 ):
     if add:
         old_dense_ref, old_small_ref, drouter_ref = refs[:3]
@@ -758,7 +795,8 @@
         dsmall_ref = refs[2]
     targets, refs = refs[outs : outs + count], refs[outs + count :]
     acc_in, acc_out, acc_small, dproj_ref = refs[:4]
-    refs = refs[4:]
+    sent_ref, dense_ref, copy_sems = refs[4:7]
+    refs = refs[7:]
     more = ()
     if add:
         pack_ref, first_ref, second_ref, part_ref, third_ref = refs[:5]
@@ -775,18 +813,35 @@
     seq = x_ref.shape[1]
     step = pl.program_id(0)
     vectors = small_ref[...].astype(f32)
+    loads = [
+        pltpu.make_async_copy(sent_hbm, sent_ref, copy_sems.at[0]),
+        pltpu.make_async_copy(dense_hbm, dense_ref, copy_sems.at[1]),
+    ]
+    sums_hbm = old_dense_ref if add else ddense_ref
+    halves = [
+        (acc_in, sums_hbm.at[:, pl.ds(0, 3 * features)], copy_sems.at[2]),
+        (acc_out, sums_hbm.at[:, pl.ds(3 * features, features)], copy_sems.at[3]),
+    ]
+    if add:
+        moves = [pltpu.make_async_copy(far, near, sem) for near, far, sem in halves]
+    else:
+        moves = [pltpu.make_async_copy(near, far, sem) for near, far, sem in halves]
 
     @pl.when(step == 0)
     def _():
         rides.start(ride_refs, more)
+        for load in loads:
+            load.start()
         if add:
-            acc_in[...] = old_dense_ref[:, : 3 * features]
-            acc_out[...] = old_dense_ref[:, 3 * features :]
+            for move in moves:
+                move.start()
             acc_small[...] = old_small_ref[...]
         else:
             acc_in[...] = jnp.zeros(acc_in.shape, f32)
             acc_out[...] = jnp.zeros(acc_out.shape, f32)
             acc_small[...] = jnp.zeros(acc_small.shape, f32)
+        for load in loads:
+            load.wait()
 
     column = lax.broadcasted_iota(jnp.int32, (seq, sent_ref.shape[0]), 1)
     slots = slots_ref[0]
@@ -799,7 +854,6 @@
         grad_hidden * vectors[experts + 2 : experts + 3], normed_two, inverse_two
     )
     grad_branch = grad_residual.astype(bf16)
-    acc_out[...] += t_dot(mixed_ref[0], grad_branch)
     grad_mixed = dot_t(grad_branch, dense_ref[:, 3 * features :]).astype(bf16)
     low_half = lax.broadcasted_iota(jnp.int32, (1, LANES), 1) < HEAD_DIM
     scale = HEAD_DIM ** (-0.5)
@@ -834,6 +888,14 @@
     attn_input = (
         normed_one * vectors[experts : experts + 1] + vectors[experts + 1 : experts + 2]
     ).astype(bf16)
+    if add:
+
+        @pl.when(step == 0)
+        def _():
+            for move in moves:
+                move.wait()
+
+    acc_out[...] += t_dot(mixed_ref[0], grad_branch)
     acc_in[...] += t_dot(attn_input, dproj_ref[...])
     grad_input = dot_t(dproj_ref[...], dense_ref[:, : 3 * features])
     acc_small[0:1, :] += jnp.sum(grad_input * normed_one, axis=0, keepdims=True)
@@ -845,8 +907,8 @@
     @pl.when(step == pl.num_programs(0) - 1)
     def _():
         if not add:
-            ddense_ref[:, : 3 * features] = acc_in[...]
-            ddense_ref[:, 3 * features :] = acc_out[...]
+            for move in moves:
+                move.start()
             dsmall_ref[...] = acc_small[...]
         else:
             used = acc_small.shape[0] + drouter_ref.shape[0]
@@ -922,6 +984,9 @@
                 total = total + third_ref[hop - 1].astype(f32)
             ddense_ref[...] = total.astype(bf16)
         rides.finish(ride_refs)
+        if not add:
+            for move in moves:
+                move.wait()
 
 
 def attend_back(
@@ -945,18 +1010,18 @@
 
     small_grads = (8, features)
     in_specs = [
-        source(features), source(features), rows(TOP), whole(sent.shape),
+        source(features), source(features), rows(TOP), HBM,
         rows(wide), rows(features), rows(features),
-        whole(dense.shape), whole(small.shape),
+        HBM, whole(small.shape),
     ]
     operands = [images, out_grad, slots, sent, proj, mixed, residual, dense, small]
-    out_specs = [rows(features), whole((features, 4 * features))]
+    out_specs = [rows(features), HBM]
     out_shape = [
         jax.ShapeDtypeStruct((IMG_MB, seq, features), f32),
         jax.ShapeDtypeStruct((features, 4 * features), f32),
     ]
     if add:
-        in_specs += [whole(array.shape) for array in old]
+        in_specs += [HBM] + [whole(array.shape) for array in old[1:]]
         operands += list(old)
         shard = (features // ranks, 4 * features + LANES)
         inner = inner_size(experts)
@@ -990,6 +1055,7 @@
             pltpu.VMEM((features, features), f32),
             pltpu.VMEM(small_grads, f32),
             pltpu.VMEM((seq, wide), bf16),
+            *staged(sent, dense),
         ]
         + reduce_scratch
         + rides.scratch,

time: 540 us -> 525 us (0.972)
  Pallas kernels: 464 us -> 449 us
    pallas_call x2, Pallas kernels: 154 us -> 143 us  [attend_back(): pl.pallas_call(functools.partial(attend_back_kernel, experts, add, rides,...]
  transfers between devices with their start and end apart: 5 -> 5, of which waited for: 2 -> 2; matrix products, arithmetic and copies ran while one was open for 2% -> 2% of each run, Pallas kernels for 53% -> 52%
where the time goes in v4:
time: 525 us; the launch traced here: 517 us
  Pallas kernels  449 us (86%)
  waiting for transfers between devices  21.3 us (4%)
  between operations  14.5 us (3%)
  local copies, waits for them, and re-layouts  11.8 us (2%)
  other arithmetic  8.15 us (2%)
  starting transfers between devices  7.55 us (1%)
  blocking collectives  5.42 us (1%)
    pallas_call x2, Pallas kernels, expert_block(): pl.pallas_call(functools.partial(expert_kernel, experts, chunk, add, ride...  181 us
    pallas_call x2, Pallas kernels, attend_back(): pl.pallas_call(functools.partial(attend_back_kernel, experts, add, rides,...  143 us
    pallas_call x2, Pallas kernels, attend(): pl.pallas_call(functools.partial(attend_kernel, experts, rides), grid=(IM...  64.3 us
    pallas_call x1, Pallas kernels, finish(): pl.pallas_call(functools.partial(finish_kernel, inner, outer), grid=(imag...  42.4 us
    all_gather x1, waiting for transfers between devices, per_device(): weight_out = lax.all_gather(expert_out[0], 'dp', axis=0, tiled=True)  13.7 us
    pallas_call x2, Pallas kernels, dispatch(): pl.pallas_call(functools.partial(dispatch_kernel, capacity), grid=(expert...  12 us
  transfers between devices with their start and end apart: 5, of which 2 were waited for; matrix products, arithmetic and copies ran while one was open for 2% of the time, Pallas kernels for 52%

profile of v4, /device:TPU:0, one launch (start us, length us, event | category | flops | bytes accessed | tf_op | source)
XLA Modules:
  0.0 517.4 jit_solution(2271609569002636089)
XLA Ops:
  7.2 2.4 pad_maximum_fusion.1
  11.2 1.1 copy.40.routes_ref
  12.3 2.8 route.2
  15.0 6.0 %dispatch.2 = bf16[8,184,768]{2,1,0:T(8,128)(2,1)} custom-call(s32[8,197]{1,0:T(8,128)} %get-tuple-element.53.lines_ref, bf16[6,197,768]{2,1,0:T(8,128)(2,1)} %top_ref.3), custom_call_target="tpu_custom_call" | custom-call | flops 1336246272 | bytes 3168768 | tf_op jit(solution)/shard_map/dispatch/pallas_call | solution.py:237
  21.1 7.4 %all-to-all-start = ((bf16[8,184,768]{2,1,0:T(8,128)(2,1)}), bf16[8,184,768]{2,1,0:T(8,128)(2,1)S(1)}, u32[]{:S(2)}, u32[]{:S(2)}) async-start(bf16[8,184,768]{2,1,0:T(8,128)(2,1)} %dispatch.2), calls=%async_computation | async-start | bytes 4521984 | tf_op jit(solution)/shard_map/all_to_all | solution.py:1123
  28.8 5.4 %all-gather.2 = bf16[4,192,20]{1,2,0:T(8,128)(2,1)S(1)} all-gather(bf16[1,192,20]{1,2,0:T(8,128)(2,1)S(1)} %bitcast.44), channel_id=1, replica_groups=mesh['dp'=4,'expert'=8] {'dp'}, dimensions={0}, use_global_device_ids=true | all-gather | bytes 38400 | tf_op jit(solution)/shard_map/all_gather | solution.py:1105
  35.7 2.8 route.3
  38.5 6.0 %dispatch.3.refs_0_ = bf16[8,184,768]{2,1,0:T(8,128)(2,1)} custom-call(s32[8,197]{1,0:T(8,128)} %get-tuple-element.55.lines_ref, bf16[6,197,768]{2,1,0:T(8,128)(2,1)} %top_ref.3), custom_call_target="tpu_custom_call" | custom-call | flops 1336246272 | bytes 3168768 | tf_op jit(solution)/shard_map/dispatch/pallas_call | solution.py:237
  44.5 6.2 %all-gather.7.cloned.1.call-done.dense_hbm = bf16[768,3072]{1,0:T(8,128)(2,1)} async-done(((bf16[192,3072]{1,0:T(8,128)(2,1)}), bf16[768,3072]{1,0:T(8,128)(2,1)}) %all-gather.7.cloned.1.call-update) | async-done | bytes 4718608 | tf_op jit(solution)/shard_map/all_gather | solution.py:1102
  50.7 19.6 %attend.2 = (bf16[3,197,2304]{2,1,0:T(8,128)(2,1)}, bf16[3,197,768]{2,1,0:T(8,128)(2,1)}, f32[3,197,768]{2,1,0:T(8,128)}, f32[3,197,2]{2,1,0:T(8,128)}, bf16[8,184,768]{2,1,0:T(8,128)(2,1)}) custom-call(bf16[6,197,768]{2,1,0:T(8,128)(2,1)} %x_ref.7, s32[6,197,2]{2,1,0:T(8,128)} %copy.40.routes_ref, s32[8,197]{1,0:T(8,128)} %get-tuple-element.53.lines_ref, ...), custom_call_target="tpu_custom_call" | custom-call | flops 5577375744 | bytes 23961600 | tf_op jit(solution)/shard_map/attend/pallas_call | solution.py:363
  70.2 44.7 %attend.3 = (bf16[3,197,2304]{2,1,0:T(8,128)(2,1)}, bf16[3,197,768]{2,1,0:T(8,128)(2,1)}, f32[3,197,768]{2,1,0:T(8,128)}, f32[3,197,2]{2,1,0:T(8,128)}, bf16[8,1...) custom-call(bf16[6,197,768]{2,1,0:T(8,128)(2,1)} %x_ref.7, s32[6,197,2]{2,1,0:T(8,128)} %copy.40.routes_ref, ...), custom_call_target="tpu_custom_call" | custom-call | flops 5577375744 | bytes 23961600 | tf_op jit(solution)/shard_map/attend/pallas_call | solution.py:363
  115.0 13.7 %all-gather.11.cloned.1.call-done = bf16[1,3072,768]{2,1,0:T(8,128)(2,1)} async-done(((bf16[1,768,768]{2,1,0:T(8,128)(2,1)}), bf16[1,3072,768]{2,1,0:T(8,128)(2,1)}) %all-gather.11.cloned.1.call-update) | async-done | bytes 4718608 | tf_op jit(solution)/shard_map/all_gather | solution.py:1109
  128.7 91.6 %expert_block.2 = (bf16[1472,768]{1,0:T(8,128)(2,1)}, bf16[1472,768]{1,0:T(8,128)(2,1)}, f32[3072,1664]{1,0:T(8,128)}, f32[16,768]{1,0:T(8,128)}, bf16[8,184,768...) custom-call(bf16[1472,768]{1,0:T(8,128)(2,1)} %bitcast.61, bf16[1472,768]{1,0:T(8,128)(2,1)} %bitcast.36, ...), custom_call_target="tpu_custom_call" | custom-call | flops 41674604544 | bytes 37355520 | tf_op jit(solution)/shard_map/expert_block/pallas_call | solution.py:537
  220.3 89.6 %expert_block.3 = (bf16[1472,768]{1,0:T(8,128)(2,1)}, bf16[1472,768]{1,0:T(8,128)(2,1)}, bf16[3072,1664]{1,0:T(8,128)(2,1)}, f32[16,768]{1,0:T(8,128)}, bf16[8,1...) custom-call(bf16[1472,768]{1,0:T(8,128)(2,1)} %bitcast.66, bf16[1472,768]{1,0:T(8,128)(2,1)} %bitcast.65, ...), custom_call_target="tpu_custom_call" | custom-call | flops 41674604544 | bytes 37355520 | tf_op jit(solution)/shard_map/expert_block/pallas_call | solution.py:537
  310.0 43.4 %attend_back.2 = (f32[3,197,768]{2,1,0:T(8,128)}, f32[768,3072]{1,0:T(8,128)}, f32[8,768]{1,0:T(8,128)}, bf16[8,184,768]{2,1,0:T(8,128)(2,1)}) custom-call(bf16[6,197,768]{2,1,0:T(8,128)(2,1)} %x_ref.7, bf16[6,197,768]{2,1,0:T(8,128)(2,1)} %top_ref.3, s32[3,197,2]{2,1,0:T(8,128)} %get-tuple-element.51.slots_ref.slots0_ref, bf16[1472,768]{1,0:T(8,128)(2,1)} %bitcast.60, ...), custom_call_target="tpu_custom_call" | custom-call | flops 13943439360 | bytes 33398784 | tf_op jit(solution)/shard_map/attend_back/pallas_call | solution.py:1047
  353.4 99.8 %attend_back.3 = (f32[3,197,768]{2,1,0:T(8,128)}, bf16[4,24,3200]{2,1,0:T(8,128)(2,1)}, bf16[8,184,768]{2,1,0:T(8,128)(2,1)}, bf16[8,184,768]{2,1,0:T(8,128)(2,1)}) custom-call(bf16[6,197,768]{2,1,0:T(8,128)(2,1)} %x_ref.7, bf16[6,197,768]{2,1,0:T(8,128)(2,1)} %top_ref.3, ...), custom_call_target="tpu_custom_call", output_to_operand_aliasing={{2}: (14, {})} | custom-call | flops 13943439360 | bytes 33398784 | tf_op jit(solution)/shard_map/attend_back/pallas_call | solution.py:1047
  453.3 42.4 %finish.1 = (bf16[6,197,768]{2,1,0:T(8,128)(2,1)}, f32[8,24,2304]{2,1,0:T(8,128)}, f32[8,24,768]{2,1,0:T(8,128)}, f32[8,24,128]{2,1,0:T(8,128)}) custom-call(s32[3,197,2]{2,1,0:T(8,128)} %get-tuple-element.51.slots_ref.slots0_ref, s32[3,197,2]{2,1,0:T(8,128)} %get-tuple-element.52.slots_ref.slots1_ref, f32[3,197,2]{2,1,0:T(8,128)} %get-tuple-element.54.gates0_ref, ...), custom_call_target="tpu_custom_call" | custom-call | flops 5344985088 | bytes 9968640 | tf_op jit(solution)/shard_map/finish/pallas_call | solution.py:753
  495.7 1.0 copy.46
  496.7 3.7 pad_maximum_fusion
  501.5 2.1 convert_element_type.3
  503.8 2.5 slice_bitcast_fusion
  506.9 1.2 copy.51
  508.1 1.2 copy.52
  509.6 0.8 copy.53
  (54 shorter events, 5.5 us)
Async XLA Ops:
  7.2 43.5 %all-gather.7.cloned.1.call-start = ((), (), s32[]{:S(2)}) async-start(), calls=%async_computation.2 | async-start | bytes 5898240 | tf_op jit(solution)/shard_map/all_gather | solution.py:1102
  9.6 1.5 copy-start.5
  9.7 105.3 %all-gather.9.cloned.1.call-start = ((), (), s32[]{:S(2)}) async-start(), calls=%async_computation.4 | async-start | bytes 5898240 | tf_op jit(solution)/shard_map/all_gather | solution.py:1108
  10.4 118.3 %all-gather.11.cloned.1.call-start = ((), (), s32[]{:S(2)}) async-start(), calls=%async_computation.5 | async-start | bytes 5898240 | tf_op jit(solution)/shard_map/all_gather | solution.py:1109
  21.0 7.5 %copy-start.8 = (bf16[192]{0:T(256)(128)(2,1)S(1)}, bf16[192]{0:T(256)(128)(2,1)}, u32[]{:S(2)}) copy-start(bf16[192]{0:T(256)(128)(2,1)} %param.14) | copy-start | bytes 1156
  21.0 7.5 %copy-start.9 = (bf16[192]{0:T(256)(128)(2,1)S(1)}, bf16[192]{0:T(256)(128)(2,1)}, u32[]{:S(2)}) copy-start(bf16[192]{0:T(256)(128)(2,1)} %param.15) | copy-start | bytes 1156
  21.0 7.5 %copy-start.10 = (bf16[192]{0:T(256)(128)(2,1)S(1)}, bf16[192]{0:T(256)(128)(2,1)}, u32[]{:S(2)}) copy-start(bf16[192]{0:T(256)(128)(2,1)} %param.18) | copy-start | bytes 1156
  21.0 7.5 %copy-start.11 = (bf16[192]{0:T(256)(128)(2,1)S(1)}, bf16[192]{0:T(256)(128)(2,1)}, u32[]{:S(2)}) copy-start(bf16[192]{0:T(256)(128)(2,1)} %param.19) | copy-start | bytes 1156
  21.1 7.6 %copy-start.7 = (bf16[1,768]{1,0:T(2,128)(2,1)S(1)}, bf16[1,768]{1,0:T(2,128)(2,1)}, u32[]{:S(2)}) copy-start(bf16[1,768]{1,0:T(2,128)(2,1)} %param.22) | copy-start | bytes 4612
  21.1 7.7 %copy-start.6 = (bf16[192,8]{0,1:T(8,128)(2,1)S(1)}, bf16[192,8]{0,1:T(8,128)(2,1)}, u32[]{:S(2)}) copy-start(bf16[192,8]{0,1:T(8,128)(2,1)} %param.20) | copy-start | bytes 9220
  21.1 93.9 %all-to-all-start = ((bf16[8,184,768]{2,1,0:T(8,128)(2,1)}), bf16[8,184,768]{2,1,0:T(8,128)(2,1)S(1)}, u32[]{:S(2)}, u32[]{:S(2)}) async-start(bf16[8,184,768]{2,1,0:T(8,128)(2,1)} %dispatch.2), calls=%async_computation | async-start | bytes 4521984 | tf_op jit(solution)/shard_map/all_to_all | solution.py:1123
  28.5 473.1 %reduce-scatter.2.cloned.1.call-start = ((), (), s32[]{:S(2)}) async-start(), calls=%async_computation.3 | async-start | bytes 12779520 | tf_op jit(solution)/shard_map/reduce_scatter | solution.py:1141
  114.9 13.8 %copy-start = (bf16[8,184,768]{2,1,0:T(8,128)(2,1)}, bf16[8,184,768]{2,1,0:T(8,128)(2,1)S(1)}, u32[]{:S(2)}) copy-start(bf16[8,184,768]{2,1,0:T(8,128)(2,1)S(1)} %all-to-all-done) | copy-start | bytes 6782980
  453.3 43.4 %copy-start.1 = (f32[3,197,768]{2,1,0:T(8,128)S(1)}, f32[3,197,768]{2,1,0:T(8,128)}, u32[]{:S(2)}) copy-start(f32[3,197,768]{2,1,0:T(8,128)} %get-tuple-element.84) | copy-start | bytes 5446660
  503.7 3.1 copy-start.2
  506.3 1.8 copy-start.3
  508.1 1.5 copy-start.4
Sparse Core Ops, SparseCore 0:
  10.1 40.4 all-gather.6
  52.2 37.3 all-gather.8
  91.2 37.4 all-gather.10
  310.1 85.8 reduce-scatter.1

commit v5 on v4

--- a/solution.py
+++ b/solution.py
@@ -132,6 +132,10 @@
         ]
 
     def start(self, refs, more=()):
+        self.greet(more)
+        self.send(refs)
+
+    def greet(self, more):
         me = lax.axis_index("expert")
         barrier = pltpu.get_barrier_semaphore()
         for peer in more:
@@ -149,6 +153,8 @@
             )
 
         pl.semaphore_wait(barrier, self.parts - 1 + len(more))
+
+    def send(self, refs):
         for index in range(len(self.rows)):
 
             @pl.loop(1, self.parts)
@@ -168,6 +174,69 @@
                 self.copy(refs, index, offset).wait()
 
 
+class Gather:
+    def __init__(self, rows, ranks):
+        self.rows = rows
+        self.pairs = ranks // 2
+        self.ranks = ranks
+        sems = pltpu.SemaphoreType.DMA((2, self.pairs))
+        self.scratch = [sems, sems, pltpu.SemaphoreType.DMA]
+
+    def place(self, full, rank):
+        return full.at[pl.ds(pl.multiple_of(rank * self.rows, self.rows), self.rows)]
+
+    def copy(self, source, target, sems, hop, peer):
+        return pltpu.make_async_remote_copy(
+            src_ref=source,
+            dst_ref=target,
+            send_sem=sems.at[0, hop],
+            recv_sem=sems.at[1, hop],
+            device_id={"dp": peer},
+            device_id_type=pl.DeviceIdType.MESH,
+        )
+
+    def first(self, refs, hop):
+        shard, full, sems = refs
+        target = self.place(full, lax.axis_index("dp"))
+        source = target if shard is None else shard
+        return self.copy(source, target, sems[0], hop, dp_peers(self.ranks)[hop])
+
+    def second(self, refs, hop):
+        _, full, sems = refs
+        rank = lax.axis_index("dp")
+        held = self.place(full, lax.rem(rank + self.ranks - 2 * hop, self.ranks))
+        return self.copy(held, held, sems[1], hop, dp_peers(self.ranks)[0])
+
+    def own(self, refs):
+        shard, full, sems = refs
+        target = self.place(full, lax.axis_index("dp"))
+        return pltpu.make_async_copy(shard, target, sems[2])
+
+    def start(self, refs):
+        for hop in range(self.pairs):
+            self.first(refs, hop).start()
+        if refs[0] is not None:
+            self.own(refs).start()
+
+    def forward(self, refs):
+        for hop in range(1, self.pairs):
+            self.first(refs, hop).wait()
+            self.second(refs, hop).start()
+
+    def finish(self, refs):
+        if refs[0] is not None:
+            self.own(refs).wait()
+        self.first(refs, 0).wait()
+        for hop in range(1, self.pairs):
+            self.second(refs, hop).wait()
+
+
+def dp_peers(ranks):
+    rank = lax.axis_index("dp")
+    partner = rank + 1 - 2 * lax.rem(rank, 2)
+    return [partner] + [lax.rem(rank + 2 * hop, ranks) for hop in range(1, ranks // 2)]
+
+
 HBM = pl.BlockSpec(memory_space=pl.ANY)
 
 
@@ -176,7 +245,7 @@
     return buffers + [pltpu.SemaphoreType.DMA((4,))]
 
 
-def route_kernel(capacity, routes_ref, slots_ref, lines_ref):
+def route_group(capacity, routes_ref, slots_ref, first):
     seq = routes_ref.shape[1]
     row = lax.broadcasted_iota(jnp.int32, (seq, seq), 0)
     col = lax.broadcasted_iota(jnp.int32, (seq, seq), 1)
@@ -186,91 +255,106 @@
     table = jnp.full((seq, LANES), -1.0, f32)
     for choice in range(TOP):
         for image in range(IMG_MB):
-            named = routes_ref[image][:, choice : choice + 1]
+            named = routes_ref[first + image][:, choice : choice + 1]
             onehot = (lane == named).astype(f32)
             count = dot(earlier, onehot.astype(bf16)) + base
             position = jnp.sum(onehot * count, axis=1, keepdims=True).astype(jnp.int32)
             base = base + jnp.sum(onehot, axis=0, keepdims=True)
             slot = jnp.where(position < capacity, named * capacity + position, -1)
-            slots_ref[image, :, choice : choice + 1] = slot
+            slots_ref[first + image, :, choice : choice + 1] = slot
             table = jnp.where(lane == image * TOP + choice, slot.astype(f32), table)
-    lines_ref[...] = table.T[: lines_ref.shape[0]].astype(jnp.int32)
-
-
-def route(routes, group, capacity):
-    seq = routes.shape[1]
-    return pl.pallas_call(
-        functools.partial(route_kernel, capacity),
-        grid=(1,),
-        in_specs=[pl.BlockSpec((IMG_MB, seq, TOP), lambda i: (group, 0, 0))],
-        out_specs=[
-            pl.BlockSpec((IMG_MB, seq, TOP), lambda i: (0, 0, 0)),
-            pl.BlockSpec((8, seq), lambda i: (0, 0)),
-        ],
-        out_shape=[
-            jax.ShapeDtypeStruct((IMG_MB, seq, TOP), jnp.int32),
-            jax.ShapeDtypeStruct((8, seq), jnp.int32),
-        ],
-        compiler_params=params(("arbitrary",)),
-        cost_estimate=pl.CostEstimate(
-            flops=10**8, bytes_accessed=10**6, transcendentals=0
-        ),
-        name="route",
-    )(routes)
-
-
-def dispatch_kernel(capacity, lines_ref, rows_ref, out_ref):
-    first = pl.program_id(0) * capacity
+    return table.T[:8].astype(jnp.int32)
+
+
+def dispatch(lines, rows_ref, first, out_ref):
+    experts, capacity = out_ref.shape[:2]
     seq = rows_ref.shape[1]
-    slot = lax.broadcasted_iota(jnp.int32, (capacity, seq), 0) + first
-    lines = lines_ref[...]
-    acc = jnp.zeros((capacity, rows_ref.shape[2]), f32)
-    for image in range(IMG_MB):
-        at = image * TOP
-        holds = (lines[at : at + 1] == slot) | (lines[at + 1 : at + 2] == slot)
-        acc = acc + dot(holds.astype(f32).astype(bf16), rows_ref[image])
-    out_ref[0] = acc.astype(bf16)
-
-
-def dispatch(lines, rows, group, experts, capacity):
-    seq, features = rows.shape[1:]
-    return pl.pallas_call(
-        functools.partial(dispatch_kernel, capacity),
-        grid=(experts,),
-        in_specs=[
-            pl.BlockSpec((8, seq), lambda e: (0, 0)),
-            pl.BlockSpec((IMG_MB, seq, features), lambda e: (group, 0, 0)),
-        ],
-        out_specs=pl.BlockSpec((1, capacity, features), lambda e: (e, 0, 0)),
-        out_shape=jax.ShapeDtypeStruct((experts, capacity, features), bf16),
-        compiler_params=params(("arbitrary",)),
-        cost_estimate=pl.CostEstimate(
-            flops=2 * experts * capacity * IMG_MB * seq * features,
-            bytes_accessed=2 * features * (experts * capacity + IMG_MB * seq),
-            transcendentals=0,
-        ),
-        name="dispatch",
-    )(lines, rows)
-
-
-def attend_kernel(
-    experts, rides, x_ref, routes_ref, lines_ref, dense_hbm, small_ref, *refs
+    slot = lax.broadcasted_iota(jnp.int32, (capacity, seq), 0)
+
+    @pl.loop(0, experts)
+    def _(expert):
+        here = slot + expert * capacity
+        total = None
+        for index in range(IMG_MB):
+            at = index * TOP
+            holds = (lines[at : at + 1] == here) | (lines[at + 1 : at + 2] == here)
+            part = dot(holds.astype(f32).astype(bf16), rows_ref[first + index])
+            total = part if total is None else total + part
+        out_ref[expert] = total.astype(bf16)
+
+
+def front_kernel(
+    experts, capacity, ranks, rides, gathers,
+    x_ref, routes_ref, top_ref, router_ref, vectors_ref, in_hbm, out_hbm, w1_hbm, w2_hbm,
+    proj_ref, mixed_ref, residual_ref, gates_ref, slots_ref, small_ref, bias_ref,
+    dense_hbm, w1_full, w2_full, grad_rows_hbm, token_rows_hbm, grads_hbm, received_hbm,
+    dense_ref, rows_a, rows_b, hidden_ref, lines_ref, sems, *more,
 ):
-    count = len(rides.arrays) if rides else 0
-    sources, refs = refs[:count], refs[count:]
-    proj_ref, mixed_ref, residual_ref, gates_ref, rows_ref = refs[:5]
-    targets, (hidden_ref, dense_ref, load_sem, *sems) = refs[5 : 5 + count], refs[5 + count :]
     step = pl.program_id(0)
-    load = pltpu.make_async_copy(dense_hbm, dense_ref, load_sem.at[0])
+    features = x_ref.shape[2]
+    ride_a = ([rows_a], [grads_hbm], more[:3])
+    ride_b = ([rows_b], [received_hbm], more[3:6])
+    dense_part = (None, dense_ref, more[6:9])
+    w1_part = (w1_hbm, w1_full, more[9:12])
+    w2_part = (w2_hbm, w2_full, more[12:15])
+    gather_dense, gather_units = gathers
+    keep_dense = pltpu.make_async_copy(dense_ref, dense_hbm, sems.at[0])
+    keep_grads = pltpu.make_async_copy(rows_b, grad_rows_hbm, sems.at[1])
+    keep_tokens = pltpu.make_async_copy(rows_a, token_rows_hbm, sems.at[2])
 
     @pl.when(step == 0)
     def _():
-        if rides:
-            rides.start((sources, targets, sems))
-        load.start()
-        load.wait()
-
-    features = x_ref.shape[2]
+        own = features // ranks
+        rank = lax.axis_index("dp")
+        mine = pl.ds(pl.multiple_of(rank * own, own), own)
+        fills = [
+            pltpu.make_async_copy(
+                in_hbm, dense_ref.at[mine, pl.ds(0, 3 * features)], sems.at[2]
+            ),
+            pltpu.make_async_copy(
+                out_hbm, dense_ref.at[mine, pl.ds(3 * features, features)], sems.at[3]
+            ),
+        ]
+        for fill in fills:
+            fill.start()
+        given = vectors_ref.shape[0]
+        columns = jnp.concatenate(
+            [
+                router_ref[...].astype(f32),
+                vectors_ref[...].astype(f32).T,
+                jnp.zeros((own, LANES - experts - given), f32),
+            ],
+            axis=1,
+        )
+        dense_ref[mine, 4 * features :] = columns.astype(bf16)
+        rides.greet([{"dp": peer} for peer in dp_peers(ranks)])
+        for fill in fills:
+            fill.wait()
+        gather_dense.start(dense_part)
+        lines = route_group(capacity, routes_ref, slots_ref, 0)
+        lines_ref[0] = lines
+        dispatch(lines, top_ref, 0, rows_a)
+        rides.send(ride_a)
+        lines = route_group(capacity, routes_ref, slots_ref, IMG_MB)
+        lines_ref[1] = lines
+        dispatch(lines, top_ref, IMG_MB, rows_b)
+        keep_grads.start()
+        gather_dense.forward(dense_part)
+        gather_units.start(w1_part)
+        gather_units.start(w2_part)
+        gather_dense.finish(dense_part)
+        keep_dense.start()
+        small = dense_ref[:, 4 * features :].astype(f32).T
+        small_ref[...] = small[: small_ref.shape[0]].astype(bf16)
+        for line in range(given - 4):
+            at = experts + 4 + line
+            for place in range(ranks):
+                first = (place * (given - 4) + line) * own
+                bias_ref[:, first : first + own] = small[
+                    at : at + 1, place * own : (place + 1) * own
+                ].astype(bf16)
+        keep_grads.wait()
+
     image = x_ref[0].astype(f32)
     vectors = small_ref[...].astype(f32)
     normed, _ = norm_forward(image)
@@ -297,16 +381,16 @@
             part = dot(weights, jnp.where(keep, values, 0).astype(bf16))
             out = part if out is None else out + part
         mixed_ref[0, :, first : first + LANES] = out.astype(bf16)
-    residual = image + dot(mixed_ref[0], dense_ref[:, 3 * features :])
+    residual = image + dot(mixed_ref[0], dense_ref[:, 3 * features : 4 * features])
     residual_ref[0] = residual
     normed, _ = norm_forward(residual)
     hidden = (
         normed * vectors[experts + 2 : experts + 3] + vectors[experts + 3 : experts + 4]
     ).astype(bf16)
-    hidden_ref[step] = hidden
+    hidden_ref[lax.rem(step, IMG_MB)] = hidden
     probs = softmax_lanes(dot_t(hidden, small_ref[...]), experts)
     lane = lax.broadcasted_iota(jnp.int32, probs.shape, 1)
-    routes = routes_ref[0]
+    routes = routes_ref[step]
     for choice in range(TOP):
         gates_ref[0, :, choice : choice + 1] = jnp.sum(
             jnp.where(lane == routes[:, choice : choice + 1], probs, 0.0),
@@ -314,43 +398,37 @@
             keepdims=True,
         )
 
+    @pl.when(step == IMG_MB - 1)
+    def _():
+        dispatch(lines_ref[0], hidden_ref, 0, rows_b)
+        rides.send(ride_b)
+
     @pl.when(step == pl.num_programs(0) - 1)
     def _():
-        seq = x_ref.shape[1]
-        capacity = rows_ref.shape[1]
-        lines = lines_ref[...]
-        slot = lax.broadcasted_iota(jnp.int32, (capacity, seq), 0)
-
-        @pl.loop(0, experts)
-        def _(expert):
-            here = slot + expert * capacity
-            total = None
-            for index in range(IMG_MB):
-                at = index * TOP
-                holds = (lines[at : at + 1] == here) | (lines[at + 1 : at + 2] == here)
-                part = dot(holds.astype(f32).astype(bf16), hidden_ref[index])
-                total = part if total is None else total + part
-            rows_ref[expert] = total.astype(bf16)
-
-        if rides:
-            rides.finish((sources, targets, sems))
-
-
-def attend(
-    images, routes, lines, dense, small, experts, capacity, group, entries=(), collective=None
+        rides.finish(ride_a)
+        dispatch(lines_ref[1], hidden_ref, 0, rows_a)
+        keep_tokens.start()
+        gather_units.forward(w1_part)
+        gather_units.forward(w2_part)
+        gather_units.finish(w1_part)
+        gather_units.finish(w2_part)
+        keep_dense.wait()
+        rides.finish(ride_b)
+        keep_tokens.wait()
+
+
+def front(
+    images, routes, out_grad, router, vectors, attn_in, attn_out, w1, w2, experts, capacity,
+    ranks, small_rows, collective,
 ):
-    seq, features = images.shape[1:]
-    wide = 3 * features
-    first = group * IMG_MB
-    rides = Rides(entries) if entries else None
-    more = {"collective_id": collective, "has_side_effects": True} if entries else {}
-    slot_rows = (experts, capacity, features)
+    count, seq, features = images.shape
+    width = 4 * features + LANES
+    slot_rows = jax.ShapeDtypeStruct((experts, capacity, features), bf16)
+    rides = Rides([(slot_rows, 0, capacity, None)])
+    gathers = (Gather(router.shape[0], ranks), Gather(w1.shape[0], ranks))
 
     def rows(width):
         return pl.BlockSpec((1, seq, width), lambda i: (i, 0, 0))
-
-    def source(width):
-        return pl.BlockSpec((1, seq, width), lambda i: (first + i, 0, 0))
 
     def whole(shape):
         return pl.BlockSpec(
@@ -358,39 +436,60 @@
         )
 
     def out(width, dtype):
-        return jax.ShapeDtypeStruct((IMG_MB, seq, width), dtype)
-
+        return jax.ShapeDtypeStruct((count, seq, width), dtype)
+
+    units = jax.ShapeDtypeStruct((ranks * w1.shape[0], features), bf16)
     return pl.pallas_call(
-        functools.partial(attend_kernel, experts, rides),
-        grid=(IMG_MB,),
+        functools.partial(front_kernel, experts, capacity, ranks, rides, gathers),
+        grid=(count,),
         in_specs=[
-            source(features),
-            source(TOP),
-            whole(lines.shape),
-            HBM,
-            whole(small.shape),
-        ]
-        + (rides.in_specs if rides else []),
-        out_specs=[rows(wide), rows(features), rows(features), rows(TOP), whole(slot_rows)]
-        + (rides.out_specs if rides else []),
+            rows(features), whole(routes.shape), whole(out_grad.shape), whole(router.shape),
+            whole(vectors.shape), HBM, HBM, HBM, HBM,
+        ],
+        out_specs=[
+            rows(3 * features), rows(features), rows(features), rows(TOP),
+            whole(routes.shape), whole((small_rows, features)), whole((1, ranks * w1.shape[0])),
+        ]
+        + [HBM] * 7,
         out_shape=[
-            out(wide, bf16),
+            out(3 * features, bf16),
             out(features, bf16),
             out(features, f32),
             out(TOP, f32),
-            jax.ShapeDtypeStruct(slot_rows, bf16),
-        ]
-        + (rides.out_shape if rides else []),
-        scratch_shapes=[pltpu.VMEM((IMG_MB, seq, features), bf16), *staged(dense)]
-        + (rides.scratch if rides else []),
-        compiler_params=params(("arbitrary",), **more),
+            jax.ShapeDtypeStruct(routes.shape, jnp.int32),
+            jax.ShapeDtypeStruct((small_rows, features), bf16),
+            jax.ShapeDtypeStruct((1, ranks * w1.shape[0]), bf16),
+            jax.ShapeDtypeStruct((features, width), bf16),
+            units,
+            units,
+            slot_rows,
+            slot_rows,
+            slot_rows,
+            slot_rows,
+        ],
+        scratch_shapes=[
+            pltpu.VMEM((features, width), bf16),
+            pltpu.VMEM(slot_rows.shape, bf16),
+            pltpu.VMEM(slot_rows.shape, bf16),
+            pltpu.VMEM((IMG_MB, seq, features), bf16),
+            pltpu.VMEM((count // IMG_MB, 8, seq), jnp.int32),
+            pltpu.SemaphoreType.DMA((4,)),
+        ]
+        + rides.scratch
+        + rides.scratch
+        + gathers[0].scratch
+        + gathers[1].scratch
+        + gathers[1].scratch,
+        compiler_params=params(
+            ("arbitrary",), collective_id=collective, has_side_effects=True
+        ),
         cost_estimate=pl.CostEstimate(
-            flops=IMG_MB * seq * 16 * features * features,
-            bytes_accessed=4 * features * (4 * features + IMG_MB * seq * 8),
-            transcendentals=IMG_MB * HEADS * seq * seq,
+            flops=count * seq * 16 * features * features,
+            bytes_accessed=4 * features * (4 * features + count * seq * 8),
+            transcendentals=count * HEADS * seq * seq,
         ),
-        name="attend",
-    )(images, routes, lines, dense, small, *(rides.operands if rides else []))
+        name="front",
+    )(images, routes, out_grad, router, vectors, attn_in, attn_out, w1, w2)
 
 
 def expert_kernel(
@@ -579,12 +678,12 @@
 
 
 def finish_kernel(
-    inner, outer, slots0_ref, slots1_ref, gates0_ref, gates1_ref, residual0_ref, residual1_ref,
+    inner, outer, slots_ref, gates_ref, residual_ref,
     returned0_hbm, returned1_hbm, part_ref, out_ref, din_ref, dout_ref, little_ref,
     returned0_ref, returned1_ref, load_sems, second_ref, full_ref, sems2, sems3, sems4,
 ):
     step = pl.program_id(0)
-    seq = slots0_ref.shape[1]
+    seq = slots_ref.shape[1]
     features = out_ref.shape[2]
     width = part_ref.shape[2]
     tiles = width // LANES
@@ -678,7 +777,7 @@
 
     column = lax.broadcasted_iota(jnp.int32, (seq, returned0_ref.shape[0]), 1)
 
-    def mix(slots_ref, gates_ref, residual_ref, returned_ref):
+    def mix(returned_ref):
         slots = slots_ref[0]
         gates = gates_ref[0]
         total = residual_ref[0]
@@ -690,11 +789,11 @@
 
     @pl.when(step < IMG_MB)
     def _():
-        mix(slots0_ref, gates0_ref, residual0_ref, returned0_ref)
+        mix(returned0_ref)
 
     @pl.when(step >= IMG_MB)
     def _():
-        mix(slots1_ref, gates1_ref, residual1_ref, returned1_ref)
+        mix(returned1_ref)
 
     @pl.when(step == 1)
     def _():
@@ -727,24 +826,16 @@
                 little_ref[block] = full_ref[part, place, :, 4 * features :].astype(f32)
 
 
-def finish(slots, gates, residuals, returned, part, parts, collective):
+def finish(slots, gates, residual, returned, part, parts, collective):
     outer, share, width = part.shape
     inner = inner_size(parts)
-    seq = slots[0].shape[1]
-    images = IMG_MB * len(slots)
-    features = residuals[0].shape[2]
+    images, seq, features = residual.shape
     chunks = 3
 
     def whole(shape):
         return pl.BlockSpec(
             shape, lambda i: (0,) * len(shape), pipeline_mode=pl.Buffered(1)
         )
-
-    def early(width):
-        return pl.BlockSpec((1, seq, width), lambda i: (jnp.minimum(i, IMG_MB - 1), 0, 0))
-
-    def late(width):
-        return pl.BlockSpec((1, seq, width), lambda i: (jnp.maximum(i - IMG_MB, 0), 0, 0))
 
     def each(width):
         return pl.BlockSpec((1, seq, width), lambda i: (i, 0, 0))
@@ -754,7 +845,7 @@
         functools.partial(finish_kernel, inner, outer),
         grid=(images,),
         in_specs=[
-            early(TOP), late(TOP), early(TOP), late(TOP), early(features), late(features),
+            each(TOP), each(TOP), each(features),
             HBM, HBM, whole(part.shape),
         ],
         out_specs=[each(features)] + [whole((parts, share, size)) for size in outs],
@@ -777,7 +868,7 @@
             transcendentals=0,
         ),
         name="finish",
-    )(*slots, *gates, *residuals, *returned, part)
+    )(slots, gates, residual, *returned, part)
 
 
 def attend_back_kernel(
@@ -785,29 +876,78 @@
     dense_hbm, small_ref, *refs
 ):
     if add:
-        old_dense_ref, old_small_ref, drouter_ref = refs[:3]
-        refs = refs[3:]
+        old_dense_ref, old_small_ref, drouter_ref, sums_b_hbm = refs[:4]
+        refs = refs[4:]
+    else:
+        dweights_hbm, refs = refs[0], refs[1:]
     count = len(rides.arrays)
-    outs = 2 if add else 3
+    outs = 4 if add else 5
     sources, refs = refs[:count], refs[len(rides.operands) :]
     grad_x_ref, ddense_ref = refs[:2]
-    if not add:
-        dsmall_ref = refs[2]
+    if add:
+        grad_b_ref, bias_b_ref = refs[2:4]
+    else:
+        dsmall_ref, sums_b_hbm, grad_a_ref = refs[2:5]
     targets, refs = refs[outs : outs + count], refs[outs + count :]
     acc_in, acc_out, acc_small, dproj_ref = refs[:4]
     sent_ref, dense_ref, copy_sems = refs[4:7]
     refs = refs[7:]
-    more = ()
+    rank = lax.axis_index("dp")
+    core = lax.rem(rank, 2)
+    mine = rank // 2
+    pairs = ranks // 2
+    partner, *others = [{"dp": peer} for peer in dp_peers(ranks)]
+    more = [partner] + others
+
+    def remote(source, target, sems, index, peer):
+        return pltpu.make_async_remote_copy(
+            src_ref=source,
+            dst_ref=target,
+            send_sem=sems.at[0, index],
+            recv_sem=sems.at[1, index],
+            device_id=peer,
+            device_id_type=pl.DeviceIdType.MESH,
+        )
+
     if add:
         pack_ref, first_ref, second_ref, part_ref, third_ref = refs[:5]
         first_sems, second_sems, third_sems = refs[5:8]
-        refs = refs[8:]
-        rank = lax.axis_index("dp")
-        core = lax.rem(rank, 2)
-        pairs = ranks // 2
-        partner = {"dp": rank + 1 - 2 * core}
-        others = [{"dp": lax.rem(rank + 2 * hop, ranks)} for hop in range(1, pairs)]
-        more = [partner] + others
+        own_b_ref, other_b_ref, own_b_sem, other_b_sems = refs[8:12]
+        refs = refs[12:]
+    else:
+        own_w_ref, other_w_ref, other_a_ref = refs[:3]
+        own_w_sems, other_w_sems, other_a_sems, keep_b_sem = refs[3:7]
+        refs = refs[7:]
+
+    def core_swap(pair):
+        rows = other_w_ref.shape[1]
+        at = pl.multiple_of((2 * pair + 1 - core) * rows, rows)
+        source = dweights_hbm.at[pl.ds(at, rows)]
+        return remote(source, other_w_ref.at[pair], other_w_sems, pair, partner)
+
+    def core_own(pair):
+        rows = own_w_ref.shape[1]
+        at = pl.multiple_of((2 * pair + core) * rows, rows)
+        return pltpu.make_async_copy(
+            dweights_hbm.at[pl.ds(at, rows)], own_w_ref.at[pair], own_w_sems.at[pair]
+        )
+
+    def send_a(hop):
+        at = pl.ds(0, x_ref.shape[2])
+        source = own_w_ref.at[lax.rem(mine + hop, pairs), :, at]
+        return remote(source, other_a_ref.at[hop - 1], other_a_sems, hop - 1, others[hop - 1])
+
+    def keep_b():
+        at = pl.ds(x_ref.shape[2], sums_b_hbm.shape[2])
+        return pltpu.make_async_copy(own_w_ref.at[:, :, at], sums_b_hbm, keep_b_sem.at[0])
+
+    def send_b(hop):
+        source = sums_b_hbm.at[lax.rem(mine + hop, pairs)]
+        return remote(source, other_b_ref.at[hop - 1], other_b_sems, hop - 1, others[hop - 1])
+
+    def own_b():
+        return pltpu.make_async_copy(sums_b_hbm.at[mine], own_b_ref, own_b_sem.at[0])
+
     ride_refs = (sources, targets, refs)
     features = x_ref.shape[2]
     seq = x_ref.shape[1]
@@ -833,6 +973,14 @@
         for load in loads:
             load.start()
         if add:
+            own_b().start()
+            for hop in range(1, pairs):
+                send_b(hop).start()
+        else:
+            for pair in range(pairs):
+                core_swap(pair).start()
+                core_own(pair).start()
+        if add:
             for move in moves:
                 move.start()
             acc_small[...] = old_small_ref[...]
@@ -843,6 +991,19 @@
         for load in loads:
             load.wait()
 
+    if not add:
+
+        @pl.when(step == 1)
+        def _():
+            for pair in range(pairs):
+                core_swap(pair).wait()
+                core_own(pair).wait()
+                total = own_w_ref[pair].astype(f32) + other_w_ref[pair].astype(f32)
+                own_w_ref[pair] = total.astype(bf16)
+            for hop in range(1, pairs):
+                send_a(hop).start()
+            keep_b().start()
+
     column = lax.broadcasted_iota(jnp.int32, (seq, sent_ref.shape[0]), 1)
     slots = slots_ref[0]
     holds = (slots[:, 0:1] == column) | (slots[:, 1:2] == column)
@@ -854,7 +1015,7 @@
         grad_hidden * vectors[experts + 2 : experts + 3], normed_two, inverse_two
     )
     grad_branch = grad_residual.astype(bf16)
-    grad_mixed = dot_t(grad_branch, dense_ref[:, 3 * features :]).astype(bf16)
+    grad_mixed = dot_t(grad_branch, dense_ref[:, 3 * features : 4 * features]).astype(bf16)
     low_half = lax.broadcasted_iota(jnp.int32, (1, LANES), 1) < HEAD_DIM
     scale = HEAD_DIM ** (-0.5)
     for pair in range(features // LANES):
@@ -910,6 +1071,12 @@
             for move in moves:
                 move.start()
             dsmall_ref[...] = acc_small[...]
+            total = own_w_ref[mine, :, :features].astype(f32)
+            for hop in range(1, pairs):
+                send_a(hop).wait()
+                total = total + other_a_ref[hop - 1].astype(f32)
+            grad_a_ref[...] = total
+            keep_b().wait()
         else:
             used = acc_small.shape[0] + drouter_ref.shape[0]
             rest = jnp.zeros((LANES - used, features), f32)
@@ -923,34 +1090,29 @@
                     at
                 ].astype(bf16)
                 pack_ref[place[0], place[1], :, 4 * features :] = column[at].astype(bf16)
-            copy = pltpu.make_async_remote_copy(
-                src_ref=pack_ref.at[1 - core],
-                dst_ref=first_ref,
-                send_sem=first_sems.at[0],
-                recv_sem=first_sems.at[1],
-                device_id=partner,
-                device_id_type=pl.DeviceIdType.MESH,
-            )
+            copy = remote(pack_ref.at[1 - core], first_ref, first_sems, 0, partner)
             copy.start()
             copy.wait()
             for pair in range(pairs):
                 first_ref[pair] = (
                     first_ref[pair].astype(f32) + pack_ref[core, pair].astype(f32)
                 ).astype(bf16)
-            mine = rank // 2
             copies = [
-                pltpu.make_async_remote_copy(
-                    src_ref=first_ref.at[lax.rem(mine + hop, pairs)],
-                    dst_ref=second_ref.at[hop - 1],
-                    send_sem=second_sems.at[0, hop - 1],
-                    recv_sem=second_sems.at[1, hop - 1],
-                    device_id=others[hop - 1],
-                    device_id_type=pl.DeviceIdType.MESH,
+                remote(
+                    first_ref.at[lax.rem(mine + hop, pairs)], second_ref.at[hop - 1],
+                    second_sems, hop - 1, others[hop - 1],
                 )
                 for hop in range(1, pairs)
             ]
             for copy in copies:
                 copy.start()
+            own_b().wait()
+            total = own_b_ref[...].astype(f32)
+            for hop in range(1, pairs):
+                send_b(hop).wait()
+                total = total + other_b_ref[hop - 1].astype(f32)
+            grad_b_ref[...] = total[:, :features]
+            bias_b_ref[...] = total[:, features:]
             total = first_ref[mine].astype(f32)
             for copy in copies:
                 copy.wait()
@@ -966,13 +1128,9 @@
             for hop in range(1, inner):
                 peer = lax.rem(row + hop, inner)
                 copies.append(
-                    pltpu.make_async_remote_copy(
-                        src_ref=part_ref.at[peer],
-                        dst_ref=third_ref.at[hop - 1],
-                        send_sem=third_sems.at[0, hop - 1],
-                        recv_sem=third_sems.at[1, hop - 1],
-                        device_id={"expert": me - row + peer},
-                        device_id_type=pl.DeviceIdType.MESH,
+                    remote(
+                        part_ref.at[peer], third_ref.at[hop - 1], third_sems, hop - 1,
+                        {"expert": me - row + peer},
                     )
                 )
             for copy in copies:
@@ -991,7 +1149,7 @@
 
 def attend_back(
     images, out_grad, slots, sent, proj, mixed, residual, dense, small, experts, group, old,
-    entries, collective, ranks,
+    entries, collective, ranks, dweights=None, sums_b=None,
 ):
     seq, features = images.shape[1:]
     wide = 3 * features
@@ -1010,8 +1168,8 @@
 
     small_grads = (8, features)
     in_specs = [
-        source(features), source(features), rows(TOP), HBM,
-        rows(wide), rows(features), rows(features),
+        source(features), source(features), source(TOP), HBM,
+        source(wide), source(features), source(features),
         HBM, whole(small.shape),
     ]
     operands = [images, out_grad, slots, sent, proj, mixed, residual, dense, small]
@@ -1021,8 +1179,13 @@
         jax.ShapeDtypeStruct((features, 4 * features), f32),
     ]
     if add:
-        in_specs += [HBM] + [whole(array.shape) for array in old[1:]]
-        operands += list(old)
+        in_specs += [HBM] + [whole(array.shape) for array in old[1:]] + [HBM]
+        operands += list(old) + [sums_b]
+        out_specs += [whole((sums_b.shape[1], features)), whole((sums_b.shape[1], LANES))]
+        out_shape += [
+            jax.ShapeDtypeStruct((sums_b.shape[1], features), f32),
+            jax.ShapeDtypeStruct((sums_b.shape[1], LANES), f32),
+        ]
         shard = (features // ranks, 4 * features + LANES)
         inner = inner_size(experts)
         part = (experts // inner, shard[0] // experts, shard[1])
@@ -1036,14 +1199,35 @@
             pltpu.VMEM((ranks // 2 - 1, *shard), bf16),
             pltpu.VMEM((inner, *part), bf16),
             pltpu.VMEM((inner - 1, *part), bf16),
-            pltpu.SemaphoreType.DMA((2,)),
+            pltpu.SemaphoreType.DMA((2, 1)),
             pltpu.SemaphoreType.DMA((2, ranks // 2 - 1)),
             pltpu.SemaphoreType.DMA((2, inner - 1)),
+            pltpu.VMEM(sums_b.shape[1:], bf16),
+            pltpu.VMEM((ranks // 2 - 1, *sums_b.shape[1:]), bf16),
+            pltpu.SemaphoreType.DMA((1,)),
+            pltpu.SemaphoreType.DMA((2, ranks // 2 - 1)),
         ]
     else:
         out_specs.append(whole(small_grads))
         out_shape.append(jax.ShapeDtypeStruct(small_grads, f32))
-        reduce_scratch = []
+        in_specs.append(HBM)
+        operands.append(dweights)
+        units = dweights.shape[0] // ranks
+        rest = dweights.shape[1] - features
+        out_specs += [HBM, whole((units, features))]
+        out_shape += [
+            jax.ShapeDtypeStruct((ranks // 2, units, rest), bf16),
+            jax.ShapeDtypeStruct((units, features), f32),
+        ]
+        reduce_scratch = [
+            pltpu.VMEM((ranks // 2, units, dweights.shape[1]), bf16),
+            pltpu.VMEM((ranks // 2, units, dweights.shape[1]), bf16),
+            pltpu.VMEM((ranks // 2 - 1, units, features), bf16),
+            pltpu.SemaphoreType.DMA((ranks // 2,)),
+            pltpu.SemaphoreType.DMA((2, ranks // 2)),
+            pltpu.SemaphoreType.DMA((2, ranks // 2 - 1)),
+            pltpu.SemaphoreType.DMA((1,)),
+        ]
     return pl.pallas_call(
         functools.partial(attend_back_kernel, experts, add, rides, ranks),
         grid=(IMG_MB,),
@@ -1081,32 +1265,14 @@
     tok_mb = IMG_MB * SEQ
     capacity = max(2, (5 * TOP * tok_mb // (4 * experts) + 7) // 8 * 8)
     slot_rows = experts * capacity
-    micro = images.shape[0] // IMG_MB
-    small_rows = (experts + 4 + 15) // 16 * 16
-
     own = router.shape[0]
     ranks = features // own
     bias_rows = expert_bias.shape[1] // own
-    small = jnp.concatenate(
-        [
-            router.T,
-            first_gain[None],
-            first_shift[None],
-            second_gain[None],
-            second_shift[None],
-            jnp.zeros((small_rows - experts - 4, own), bf16),
-            expert_bias.reshape(bias_rows, own),
-        ],
-        axis=0,
-    )
-    dense = lax.all_gather(
-        jnp.concatenate([attn_in, attn_out], axis=1), "dp", axis=0, tiled=True
-    )
-    small = lax.all_gather(small, "dp", axis=1, tiled=True)
-    bias_row = small[small_rows:].reshape(bias_rows, -1, own).transpose(1, 0, 2).reshape(1, -1)
-    small = small[:small_rows]
-    weight_in = lax.all_gather(expert_in[0], "dp", axis=0, tiled=True)
-    weight_out = lax.all_gather(expert_out[0], "dp", axis=0, tiled=True)
+    used = experts + 4 + bias_rows
+    small_rows = (used + 15) // 16 * 16
+    vectors = jnp.concatenate(
+        [first_gain, first_shift, second_gain, second_shift, expert_bias.reshape(-1)]
+    ).reshape(4 + bias_rows, own)
 
     def flat(blocks):
         return blocks.reshape(slot_rows, features)
@@ -1114,51 +1280,37 @@
     def blocks(rows):
         return rows.reshape(experts, capacity, features)
 
-    routed = [route(routes, group, capacity) for group in range(micro)]
-    slots = [item[0] for item in routed]
-    lines = [item[1] for item in routed]
-    grad_rows = [
-        dispatch(lines[group], out_grad, group, experts, capacity) for group in range(micro)
-    ]
-    grads_0 = lax.all_to_all(grad_rows[0], "expert", split_axis=0, concat_axis=0, tiled=True)
-    *kept_0, token_rows_0 = attend(
-        images, routes, lines[0], dense, small, experts, capacity, 0
-    )
-    *kept_1, token_rows_1, received_0 = attend(
-        images, routes, lines[1], dense, small, experts, capacity, 1,
-        [(token_rows_0, 0, capacity, None)], 5,
-    )
-    saved = [kept_0, kept_1]
+    (
+        proj, mixed, residual, gates, slots, small, bias_row, dense, weight_in, weight_out,
+        grad_rows_1, token_rows_1, grads_0, received_0,
+    ) = front(
+        images, routes, out_grad, router, vectors, attn_in, attn_out, expert_in[0],
+        expert_out[0], experts, capacity, ranks, small_rows, 5,
+    )
     result_0, dx_0, *old, grads_1, received_1 = expert_block(
         flat(received_0), flat(grads_0), weight_in, weight_out, bias_row, small, experts, None,
-        [(grad_rows[1], 0, capacity, None), (token_rows_1, 0, capacity, None)], 0,
+        [(grad_rows_1, 0, capacity, None), (token_rows_1, 0, capacity, None)], 0,
     )
     early = max(8, capacity * 3 // 8 // 8 * 8)
     result_1, dx_1, dweights, drouter, sent_0, returned_0 = expert_block(
         flat(received_1), flat(grads_1), weight_in, weight_out, bias_row, small, experts, old,
         [(blocks(dx_0), 0, capacity, None), (blocks(result_0), 0, early, None)], 1,
     )
-    dweights = lax.psum_scatter(dweights, "dp", scatter_dimension=0, tiled=True)
-    proj, mixed, residual, _ = saved[0]
-    grad_x_0, *old, sent_1 = attend_back(
-        images, out_grad, slots[0], flat(sent_0), proj, mixed, residual, dense, small,
-        experts, 0, None, [(blocks(dx_1), 0, capacity, None)], 2, ranks,
-    )
-    proj, mixed, residual, _ = saved[1]
-    grad_x_1, ddense, returned_0, returned_1 = attend_back(
-        images, out_grad, slots[1], flat(sent_1), proj, mixed, residual, dense, small,
+    grad_x_0, *old, sums_b, grad_expert_in, sent_1 = attend_back(
+        images, out_grad, slots, flat(sent_0), proj, mixed, residual, dense, small,
+        experts, 0, None, [(blocks(dx_1), 0, capacity, None)], 2, ranks, dweights,
+    )
+    grad_x_1, ddense, grad_expert_out, grad_bias, returned_0, returned_1 = attend_back(
+        images, out_grad, slots, flat(sent_1), proj, mixed, residual, dense, small,
         experts, 1, old + [drouter],
         [(blocks(result_0), early, capacity, returned_0), (blocks(result_1), 0, capacity, None)],
-        3, ranks,
+        3, ranks, None, sums_b,
     )
     grad_blocks = [grad_x_0, grad_x_1]
     block_out, grad_attn_in, grad_attn_out, little = finish(
-        slots, [item[3] for item in saved], [item[2] for item in saved],
-        [flat(returned_0), flat(returned_1)],
-        ddense, experts, 4,
+        slots, gates, residual, [flat(returned_0), flat(returned_1)], ddense, experts, 4
     )
     little = little.reshape(own, -1).T
-    dweights = dweights.astype(f32)
     return (
         block_out,
         jnp.concatenate(grad_blocks, axis=0),
@@ -1169,9 +1321,9 @@
         little[2],
         little[3],
         little[8 : 8 + experts].T,
-        dweights[None, :, :features],
-        dweights[None, :, 2 * features],
-        dweights[None, :, features : 2 * features],
+        grad_expert_in[None],
+        grad_bias[None, :, 0],
+        grad_expert_out[None],
     )
 
 

time: 525 us -> 505 us (0.962)
  Pallas kernels: 449 us -> 475 us
  waiting for transfers between devices: 21.3 us -> 0 us
  between operations: 14.5 us -> 1.18 us
  starting transfers between devices: 7.55 us -> 0 us
  local copies, waits for them, and re-layouts: 11.8 us -> 18.3 us
  blocking collectives: 5.42 us -> 0 us
    pallas_call x6 -> x1, Pallas kernels: 81.8 us -> 111 us  [front(): pl.pallas_call(functools.partial(front_kernel, experts, capacity, ranks,...]
    all_gather x3 -> x0, waiting for transfers between devices: 19.9 us -> none  [the longest x1 13.7 us: per_device(): weight_out = lax.all_gather(expert_out[0], 'dp', axis=0, tiled=True)]
    all_to_all x1 -> x0, starting transfers between devices: 7.39 us -> none  [per_device(): lax.all_to_all(grad_rows[0], 'expert', split_axis=0, concat_axis=0, tiled...]
    unnamed x29 -> x21, local copies, waits for them, and re-layouts: 4.77 us -> 12 us
    all_gather x1 -> x0, blocking collectives: 5.42 us -> none  [per_device(): small = lax.all_gather(small, 'dp', axis=1, tiled=True)]
  transfers between devices with their start and end apart: 5 -> 0, of which waited for: 2 -> 0; matrix products, arithmetic and copies ran while one was open for 2% -> 0% of each run, Pallas kernels for 52% -> 0%
where the time goes in v5:
time: 505 us; the launch traced here: 499 us
  Pallas kernels  475 us (94%)
  local copies, waits for them, and re-layouts  18.3 us (4%)
    pallas_call x2, Pallas kernels, expert_block(): pl.pallas_call(functools.partial(expert_kernel, experts, chunk, add, ride...  178 us
    pallas_call x2, Pallas kernels, attend_back(): pl.pallas_call(functools.partial(attend_back_kernel, experts, add, rides,...  144 us
    pallas_call x1, Pallas kernels, front(): pl.pallas_call(functools.partial(front_kernel, experts, capacity, ranks,...  111 us
    pallas_call x1, Pallas kernels, finish(): pl.pallas_call(functools.partial(finish_kernel, inner, outer), grid=(imag...  42.1 us
    unnamed x21, local copies, waits for them, and re-layouts  12 us

profile of v5, /device:TPU:0, one launch (start us, length us, event | category | flops | bytes accessed | tf_op | source)
XLA Modules:
  0.0 499.3 jit_solution(1818807782290746148)
XLA Ops:
  0.6 0.7 reduce
  1.3 2.8 concatenate.6
  4.1 0.7 reshape.77.vectors_ref
  4.8 1.4 copy.30.router_ref
  6.2 1.8 copy.29.routes_ref
  8.0 111.0 %front.1 = (bf16[6,197,2304]{2,1,0:T(8,128)(2,1)}, bf16[6,197,768]{2,1,0:T(8,128)(2,1)}, f32[6,197,768]{2,1,0:T(8,128)}, f32[6,197,2]{2,1,0:T(8,128)}, s32[6,197...) custom-call(bf16[6,197,768]{2,1,0:T(8,128)(2,1)} %x_ref.5, ...), custom_call_target="tpu_custom_call" | custom-call | flops 11154751488 | bytes 38486016 | tf_op jit(solution)/shard_map/front/pallas_call | solution.py:442
  119.0 89.6 %expert_block.2 = (bf16[1472,768]{1,0:T(8,128)(2,1)}, bf16[1472,768]{1,0:T(8,128)(2,1)}, f32[3072,1664]{1,0:T(8,128)}, f32[16,768]{1,0:T(8,128)}, bf16[8,184,768...) custom-call(bf16[1472,768]{1,0:T(8,128)(2,1)} %bitcast.45, bf16[1472,768]{1,0:T(8,128)(2,1)} %bitcast.44, ...), custom_call_target="tpu_custom_call" | custom-call | flops 41674604544 | bytes 37355520 | tf_op jit(solution)/shard_map/expert_block/pallas_call | solution.py:636
  208.6 88.7 %expert_block.3 = (bf16[1472,768]{1,0:T(8,128)(2,1)}, bf16[1472,768]{1,0:T(8,128)(2,1)}, bf16[3072,1664]{1,0:T(8,128)(2,1)}, f32[16,768]{1,0:T(8,128)}, bf16[8,1...) custom-call(bf16[1472,768]{1,0:T(8,128)(2,1)} %bitcast.51, bf16[1472,768]{1,0:T(8,128)(2,1)} %bitcast.50, ...), custom_call_target="tpu_custom_call" | custom-call | flops 41674604544 | bytes 37355520 | tf_op jit(solution)/shard_map/expert_block/pallas_call | solution.py:636
  297.2 45.4 %attend_back.2 = (f32[3,197,768]{2,1,0:T(8,128)}, f32[768,3072]{1,0:T(8,128)}, f32[8,768]{1,0:T(8,128)}, bf16[2,768,896]{2,1,0:T(8,128)(2,1)}, f32[768,768]{1,0:T(8,128)}, /*index=5*/bf16[8,184,768]{2,1,0:T(8,128)(2,1)}) custom-call(bf16[6,197,768]{2,1,0:T(8,128)(2,1)} %x_ref.5, bf16[6,197,768]{2,1,0:T(8,128)(2,1)} %top_ref.5, ...), custom_call_target="tpu_custom_call" | custom-call | flops 13943439360 | bytes 33398784 | tf_op jit(solution)/shard_map/attend_back/pallas_call | solution.py:1231
  342.6 98.6 %attend_back.3 = (f32[3,197,768]{2,1,0:T(8,128)}, bf16[4,24,3200]{2,1,0:T(8,128)(2,1)}, f32[768,768]{1,0:T(8,128)}, f32[768,128]{1,0:T(8,128)}, bf16[8,184,768]{...) custom-call(bf16[6,197,768]{2,1,0:T(8,128)(2,1)} %x_ref.5, ...), custom_call_target="tpu_custom_call", output_to_operand_aliasing={{4}: (15, {})} | custom-call | flops 13943439360 | bytes 33398784 | tf_op jit(solution)/shard_map/attend_back/pallas_call | solution.py:1231
  441.2 42.1 %finish.1 = (bf16[6,197,768]{2,1,0:T(8,128)(2,1)}, f32[8,24,2304]{2,1,0:T(8,128)}, f32[8,24,768]{2,1,0:T(8,128)}, f32[8,24,128]{2,1,0:T(8,128)}) custom-call(s32[6,197,2]{2,1,0:T(8,128)} %get-tuple-element.54.slots_ref, f32[6,197,2]{2,1,0:T(8,128)} %get-tuple-element.55.gates_ref, f32[6,197,768]{2,1,0:T(8,128)} %get-tuple-element.56.residual_ref, ...), custom_call_target="tpu_custom_call" | custom-call | flops 5344985088 | bytes 9968640 | tf_op jit(solution)/shard_map/finish/pallas_call | solution.py:844
  483.6 0.6 broadcast_in_dim_squeeze.3
  484.1 1.0 copy.31
  485.1 0.6 fusion
  485.7 0.6 slice_bitcast_fusion
  486.3 3.8 pad_maximum_fusion
  490.1 1.2 copy.38
  491.4 0.9 copy-done.4
  492.3 1.2 copy.39
  493.7 0.8 copy.40
  494.5 0.4 copy-done
  494.9 1.4 copy.41
  496.4 1.1 copy-done.1
  497.5 1.4 copy.42
  (12 shorter events, 0.4 us)
Async XLA Ops:
  441.2 42.2 %copy-start.6 = (f32[768,128]{1,0:T(8,128)S(1)}, f32[768,128]{1,0:T(8,128)}, u32[]{:S(2)}) copy-start(f32[768,128]{1,0:T(8,128)} %get-tuple-element.94) | copy-start | bytes 1179652
  441.2 45.1 %copy-start.2 = (f32[3,197,768]{2,1,0:T(8,128)S(1)}, f32[3,197,768]{2,1,0:T(8,128)}, u32[]{:S(2)}) copy-start(f32[3,197,768]{2,1,0:T(8,128)} %get-tuple-element.88) | copy-start | bytes 5446660
  486.3 3.8 copy-start.3
  490.1 2.1 copy-start.4
  492.3 1.4 copy-start.5
  492.3 2.7 copy-start
  494.9 2.5 copy-start.1

commit v6 on v5

--- a/solution.py
+++ b/solution.py
@@ -153,6 +153,14 @@
             )
 
         pl.semaphore_wait(barrier, self.parts - 1 + len(more))
+
+    def send_hop(self, refs, hop):
+        for index in range(len(self.rows)):
+            self.copy(refs, index, hop).start()
+
+    def send_own(self, refs):
+        for copy in self.own(refs):
+            copy.start()
 
     def send(self, refs):
         for index in range(len(self.rows)):
@@ -266,13 +274,15 @@
     return table.T[:8].astype(jnp.int32)
 
 
-def dispatch(lines, rows_ref, first, out_ref):
+def dispatch(lines, rows_ref, first, out_ref, send=None):
     experts, capacity = out_ref.shape[:2]
     seq = rows_ref.shape[1]
     slot = lax.broadcasted_iota(jnp.int32, (capacity, seq), 0)
 
-    @pl.loop(0, experts)
-    def _(expert):
+    me = lax.axis_index("expert")
+
+    def fill(hop):
+        expert = lax.rem(me + hop, experts)
         here = slot + expert * capacity
         total = None
         for index in range(IMG_MB):
@@ -282,13 +292,21 @@
             total = part if total is None else total + part
         out_ref[expert] = total.astype(bf16)
 
+    @pl.loop(1, experts)
+    def _(hop):
+        fill(hop)
+        if send is not None:
+            send(hop)
+
+    fill(0)
+
 
 def front_kernel(
     experts, capacity, ranks, rides, gathers,
-    x_ref, routes_ref, top_ref, router_ref, vectors_ref, in_hbm, out_hbm, w1_hbm, w2_hbm,
+    x_ref, named_ref, top_ref, router_ref, gains_ref, own_bias_ref, in_hbm, out_hbm, w1_hbm, w2_hbm,
     proj_ref, mixed_ref, residual_ref, gates_ref, slots_ref, small_ref, bias_ref,
     dense_hbm, w1_full, w2_full, grad_rows_hbm, token_rows_hbm, grads_hbm, received_hbm,
-    dense_ref, rows_a, rows_b, hidden_ref, lines_ref, sems, *more,
+    dense_ref, rows_a, rows_b, hidden_ref, lines_ref, routes_ref, sems, *more,
 ):
     step = pl.program_id(0)
     features = x_ref.shape[2]
@@ -317,24 +335,29 @@
         ]
         for fill in fills:
             fill.start()
-        given = vectors_ref.shape[0]
+        pieces = own_bias_ref.shape[1] // own
+        own_bias = own_bias_ref[...].astype(f32)
         columns = jnp.concatenate(
-            [
-                router_ref[...].astype(f32),
-                vectors_ref[...].astype(f32).T,
-                jnp.zeros((own, LANES - experts - given), f32),
-            ],
-            axis=1,
+            [router_ref[...].astype(f32), gains_ref[...].astype(f32)]
+            + [own_bias[:, piece * own : (piece + 1) * own] for piece in range(pieces)]
+            + [jnp.zeros((LANES - experts - 4 - pieces, own), f32)],
+            axis=0,
         )
-        dense_ref[mine, 4 * features :] = columns.astype(bf16)
+        dense_ref[mine, 4 * features :] = columns.T.astype(bf16)
         rides.greet([{"dp": peer} for peer in dp_peers(ranks)])
         for fill in fills:
             fill.wait()
         gather_dense.start(dense_part)
+        images = named_ref.shape[0]
+        named = [named_ref[index].astype(f32) for index in range(images)]
+        rest = jnp.zeros((LANES - TOP * images, named_ref.shape[2]), f32)
+        named = jnp.concatenate(named + [rest], axis=0).T.astype(jnp.int32)
+        for index in range(images):
+            routes_ref[index] = named[:, TOP * index : TOP * (index + 1)]
         lines = route_group(capacity, routes_ref, slots_ref, 0)
         lines_ref[0] = lines
-        dispatch(lines, top_ref, 0, rows_a)
-        rides.send(ride_a)
+        dispatch(lines, top_ref, 0, rows_a, lambda hop: rides.send_hop(ride_a, hop))
+        rides.send_own(ride_a)
         lines = route_group(capacity, routes_ref, slots_ref, IMG_MB)
         lines_ref[1] = lines
         dispatch(lines, top_ref, IMG_MB, rows_b)
@@ -346,10 +369,10 @@
         keep_dense.start()
         small = dense_ref[:, 4 * features :].astype(f32).T
         small_ref[...] = small[: small_ref.shape[0]].astype(bf16)
-        for line in range(given - 4):
+        for line in range(pieces):
             at = experts + 4 + line
             for place in range(ranks):
-                first = (place * (given - 4) + line) * own
+                first = (place * pieces + line) * own
                 bias_ref[:, first : first + own] = small[
                     at : at + 1, place * own : (place + 1) * own
                 ].astype(bf16)
@@ -400,8 +423,8 @@
 
     @pl.when(step == IMG_MB - 1)
     def _():
-        dispatch(lines_ref[0], hidden_ref, 0, rows_b)
-        rides.send(ride_b)
+        dispatch(lines_ref[0], hidden_ref, 0, rows_b, lambda hop: rides.send_hop(ride_b, hop))
+        rides.send_own(ride_b)
 
     @pl.when(step == pl.num_programs(0) - 1)
     def _():
@@ -418,14 +441,14 @@
 
 
 def front(
-    images, routes, out_grad, router, vectors, attn_in, attn_out, w1, w2, experts, capacity,
+    images, named, out_grad, router, gains, bias, attn_in, attn_out, w1, w2, experts, capacity,
     ranks, small_rows, collective,
 ):
     count, seq, features = images.shape
     width = 4 * features + LANES
     slot_rows = jax.ShapeDtypeStruct((experts, capacity, features), bf16)
     rides = Rides([(slot_rows, 0, capacity, None)])
-    gathers = (Gather(router.shape[0], ranks), Gather(w1.shape[0], ranks))
+    gathers = (Gather(router.shape[1], ranks), Gather(w1.shape[0], ranks))
 
     def rows(width):
         return pl.BlockSpec((1, seq, width), lambda i: (i, 0, 0))
@@ -443,12 +466,12 @@
         functools.partial(front_kernel, experts, capacity, ranks, rides, gathers),
         grid=(count,),
         in_specs=[
-            rows(features), whole(routes.shape), whole(out_grad.shape), whole(router.shape),
-            whole(vectors.shape), HBM, HBM, HBM, HBM,
+            rows(features), whole(named.shape), whole(out_grad.shape), whole(router.shape),
+            whole(gains.shape), whole(bias.shape), HBM, HBM, HBM, HBM,
         ],
         out_specs=[
             rows(3 * features), rows(features), rows(features), rows(TOP),
-            whole(routes.shape), whole((small_rows, features)), whole((1, ranks * w1.shape[0])),
+            whole((count, seq, TOP)), whole((small_rows, features)), whole((1, ranks * w1.shape[0])),
         ]
         + [HBM] * 7,
         out_shape=[
@@ -456,7 +479,7 @@
             out(features, bf16),
             out(features, f32),
             out(TOP, f32),
-            jax.ShapeDtypeStruct(routes.shape, jnp.int32),
+            jax.ShapeDtypeStruct((count, seq, TOP), jnp.int32),
             jax.ShapeDtypeStruct((small_rows, features), bf16),
             jax.ShapeDtypeStruct((1, ranks * w1.shape[0]), bf16),
             jax.ShapeDtypeStruct((features, width), bf16),
@@ -473,6 +496,7 @@
             pltpu.VMEM(slot_rows.shape, bf16),
             pltpu.VMEM((IMG_MB, seq, features), bf16),
             pltpu.VMEM((count // IMG_MB, 8, seq), jnp.int32),
+            pltpu.VMEM((count, seq, TOP), jnp.int32),
             pltpu.SemaphoreType.DMA((4,)),
         ]
         + rides.scratch
@@ -489,7 +513,7 @@
             transcendentals=count * HEADS * seq * seq,
         ),
         name="front",
-    )(images, routes, out_grad, router, vectors, attn_in, attn_out, w1, w2)
+    )(images, named, out_grad, router, gains, bias, attn_in, attn_out, w1, w2)
 
 
 def expert_kernel(
@@ -680,14 +704,14 @@
 def finish_kernel(
     inner, outer, slots_ref, gates_ref, residual_ref,
     returned0_hbm, returned1_hbm, part_ref, out_ref, din_ref, dout_ref, little_ref,
-    returned0_ref, returned1_ref, load_sems, second_ref, full_ref, sems2, sems3, sems4,
+    returned0_ref, returned1_ref, load_sems, flat_ref, second_ref, full_ref, sems2, sems3, sems4,
 ):
     step = pl.program_id(0)
     seq = slots_ref.shape[1]
     features = out_ref.shape[2]
     width = part_ref.shape[2]
     tiles = width // LANES
-    chunks = 3
+    chunks = 5
     edges = [LANES * (tiles * c // chunks) for c in range(chunks + 1)]
     cuts = [pl.ds(edges[c], edges[c + 1] - edges[c]) for c in range(chunks)]
     me = lax.axis_index("expert")
@@ -823,14 +847,18 @@
                 dout_ref[block] = full_ref[part, place, :, 3 * features : 4 * features].astype(
                     f32
                 )
-                little_ref[block] = full_ref[part, place, :, 4 * features :].astype(f32)
-
-
-def finish(slots, gates, residual, returned, part, parts, collective):
+                share = full_ref.shape[2]
+                flat_ref[block * share : (block + 1) * share] = full_ref[
+                    part, place, :, 4 * features :
+                ].astype(f32)
+        little_ref[...] = flat_ref[...].T[: little_ref.shape[0]]
+
+
+def finish(slots, gates, residual, returned, part, parts, lines, collective):
     outer, share, width = part.shape
     inner = inner_size(parts)
     images, seq, features = residual.shape
-    chunks = 3
+    chunks = 5
 
     def whole(shape):
         return pl.BlockSpec(
@@ -840,7 +868,8 @@
     def each(width):
         return pl.BlockSpec((1, seq, width), lambda i: (i, 0, 0))
 
-    outs = [3 * features, features, width - 4 * features]
+    outs = [3 * features, features]
+    little = (lines, parts * share)
     return pl.pallas_call(
         functools.partial(finish_kernel, inner, outer),
         grid=(images,),
@@ -848,11 +877,14 @@
             each(TOP), each(TOP), each(features),
             HBM, HBM, whole(part.shape),
         ],
-        out_specs=[each(features)] + [whole((parts, share, size)) for size in outs],
+        out_specs=[each(features)] + [whole((parts, share, size)) for size in outs]
+        + [whole(little)],
         out_shape=[jax.ShapeDtypeStruct((images, seq, features), bf16)]
-        + [jax.ShapeDtypeStruct((parts, share, size), f32) for size in outs],
+        + [jax.ShapeDtypeStruct((parts, share, size), f32) for size in outs]
+        + [jax.ShapeDtypeStruct(little, f32)],
         scratch_shapes=[
             *staged(*returned),
+            pltpu.VMEM((parts * share, LANES), f32),
             pltpu.VMEM((outer - 1, share, width), bf16),
             pltpu.VMEM((inner, outer, share, width), bf16),
             pltpu.SemaphoreType.DMA((2, chunks, outer - 1)),
@@ -1270,9 +1302,12 @@
     bias_rows = expert_bias.shape[1] // own
     used = experts + 4 + bias_rows
     small_rows = (used + 15) // 16 * 16
-    vectors = jnp.concatenate(
-        [first_gain, first_shift, second_gain, second_shift, expert_bias.reshape(-1)]
-    ).reshape(4 + bias_rows, own)
+    line = lax.broadcasted_iota(jnp.int32, (4, own), 0)
+    gains = jnp.where(
+        line < 2,
+        jnp.where(line == 0, first_gain[None], first_shift[None]),
+        jnp.where(line == 2, second_gain[None], second_shift[None]),
+    )
 
     def flat(blocks):
         return blocks.reshape(slot_rows, features)
@@ -1284,7 +1319,8 @@
         proj, mixed, residual, gates, slots, small, bias_row, dense, weight_in, weight_out,
         grad_rows_1, token_rows_1, grads_0, received_0,
     ) = front(
-        images, routes, out_grad, router, vectors, attn_in, attn_out, expert_in[0],
+        images, routes.transpose(0, 2, 1), out_grad, router.T, gains, expert_bias, attn_in,
+        attn_out, expert_in[0],
         expert_out[0], experts, capacity, ranks, small_rows, 5,
     )
     result_0, dx_0, *old, grads_1, received_1 = expert_block(
@@ -1308,9 +1344,9 @@
     )
     grad_blocks = [grad_x_0, grad_x_1]
     block_out, grad_attn_in, grad_attn_out, little = finish(
-        slots, gates, residual, [flat(returned_0), flat(returned_1)], ddense, experts, 4
-    )
-    little = little.reshape(own, -1).T
+        slots, gates, residual, [flat(returned_0), flat(returned_1)], ddense, experts,
+        8 + small_rows, 4,
+    )
     return (
         block_out,
         jnp.concatenate(grad_blocks, axis=0),

time: 505 us -> 496 us (0.982)
  local copies, waits for them, and re-layouts: 18.3 us -> 12.2 us
where the time goes in v6:
time: 496 us; the launch traced here: 489 us
  Pallas kernels  473 us (95%)
  local copies, waits for them, and re-layouts  12.2 us (2%)
    pallas_call x2, Pallas kernels, expert_block(): pl.pallas_call(functools.partial(expert_kernel, experts, chunk, add, ride...  176 us
    pallas_call x2, Pallas kernels, attend_back(): pl.pallas_call(functools.partial(attend_back_kernel, experts, add, rides,...  144 us
    pallas_call x1, Pallas kernels, front(): pl.pallas_call(functools.partial(front_kernel, experts, capacity, ranks,...  111 us
    pallas_call x1, Pallas kernels, finish(): pl.pallas_call(functools.partial(finish_kernel, inner, outer), grid=(imag...  41.3 us

profile of v6, /device:TPU:0, one launch (start us, length us, event | category | flops | bytes accessed | tf_op | source)
XLA Modules:
  0.0 489.5 jit_solution(7393584215633989366)
XLA Ops:
  0.7 1.4 select_select_fusion.gains_ref
  2.0 110.8 %front.1 = (bf16[6,197,2304]{2,1,0:T(8,128)(2,1)}, bf16[6,197,768]{2,1,0:T(8,128)(2,1)}, f32[6,197,768]{2,1,0:T(8,128)}, f32[6,197,2]{2,1,0:T(8,128)}, s32[6,197...) custom-call(bf16[6,197,768]{2,1,0:T(8,128)(2,1)} %x_ref.5, ...), custom_call_target="tpu_custom_call" | custom-call | flops 11154751488 | bytes 38486016 | tf_op jit(solution)/shard_map/front/pallas_call | solution.py:465
  112.9 88.0 %expert_block.2 = (bf16[1472,768]{1,0:T(8,128)(2,1)}, bf16[1472,768]{1,0:T(8,128)(2,1)}, f32[3072,1664]{1,0:T(8,128)}, f32[16,768]{1,0:T(8,128)}, bf16[8,184,768...) custom-call(bf16[1472,768]{1,0:T(8,128)(2,1)} %bitcast.45, bf16[1472,768]{1,0:T(8,128)(2,1)} %bitcast.44, ...), custom_call_target="tpu_custom_call" | custom-call | flops 41674604544 | bytes 37355520 | tf_op jit(solution)/shard_map/expert_block/pallas_call | solution.py:660
  200.9 88.5 %expert_block.3 = (bf16[1472,768]{1,0:T(8,128)(2,1)}, bf16[1472,768]{1,0:T(8,128)(2,1)}, bf16[3072,1664]{1,0:T(8,128)(2,1)}, f32[16,768]{1,0:T(8,128)}, bf16[8,1...) custom-call(bf16[1472,768]{1,0:T(8,128)(2,1)} %bitcast.50, bf16[1472,768]{1,0:T(8,128)(2,1)} %bitcast.49, ...), custom_call_target="tpu_custom_call" | custom-call | flops 41674604544 | bytes 37355520 | tf_op jit(solution)/shard_map/expert_block/pallas_call | solution.py:660
  289.4 45.4 %attend_back.2 = (f32[3,197,768]{2,1,0:T(8,128)}, f32[768,3072]{1,0:T(8,128)}, f32[8,768]{1,0:T(8,128)}, bf16[2,768,896]{2,1,0:T(8,128)(2,1)}, f32[768,768]{1,0:T(8,128)}, /*index=5*/bf16[8,184,768]{2,1,0:T(8,128)(2,1)}) custom-call(bf16[6,197,768]{2,1,0:T(8,128)(2,1)} %x_ref.5, bf16[6,197,768]{2,1,0:T(8,128)(2,1)} %top_ref.5, ...), custom_call_target="tpu_custom_call" | custom-call | flops 13943439360 | bytes 33398784 | tf_op jit(solution)/shard_map/attend_back/pallas_call | solution.py:1263
  334.7 98.6 %attend_back.3 = (f32[3,197,768]{2,1,0:T(8,128)}, bf16[4,24,3200]{2,1,0:T(8,128)(2,1)}, f32[768,768]{1,0:T(8,128)}, f32[768,128]{1,0:T(8,128)}, bf16[8,184,768]{...) custom-call(bf16[6,197,768]{2,1,0:T(8,128)(2,1)} %x_ref.5, ...), custom_call_target="tpu_custom_call", output_to_operand_aliasing={{4}: (15, {})} | custom-call | flops 13943439360 | bytes 33398784 | tf_op jit(solution)/shard_map/attend_back/pallas_call | solution.py:1263
  433.3 0.0 copy-start.7
  433.3 0.0 copy-start.2
  433.4 0.0 copy-start.3
  433.4 41.3 %finish.1 = (bf16[6,197,768]{2,1,0:T(8,128)(2,1)}, f32[8,24,2304]{2,1,0:T(8,128)}, f32[8,24,768]{2,1,0:T(8,128)}, f32[24,192]{1,0:T(8,128)}) custom-call(s32[6,197,2]{2,1,0:T(8,128)} %get-tuple-element.54.slots_ref, f32[6,197,2]{2,1,0:T(8,128)} %get-tuple-element.55.gates_ref, f32[6,197,768]{2,1,0:T(8,128)} %get-tuple-element.56.residual_ref, ...), custom_call_target="tpu_custom_call" | custom-call | flops 5344985088 | bytes 9968640 | tf_op jit(solution)/shard_map/finish/pallas_call | solution.py:873
  474.7 0.2 slice_reduce_fusion
  474.8 0.6 broadcast_in_dim_squeeze.3
  475.4 1.4 fusion
  476.8 1.3 slice_bitcast_fusion
  478.1 2.2 pad_maximum_fusion
  480.3 1.2 copy.32
  481.6 0.9 copy-done.5
  482.5 1.2 copy.33
  483.7 0.2 copy-done.6
  483.9 0.8 copy.34
  484.7 0.4 copy-done
  485.1 1.4 copy.35
  486.5 1.1 copy-done.1
  487.6 1.4 copy.36
  (11 shorter events, 0.0 us)
Async XLA Ops:
  433.3 41.3 %copy-start.7 = (f32[768,128]{1,0:T(8,128)S(1)}, f32[768,128]{1,0:T(8,128)}, u32[]{:S(2)}) copy-start(f32[768,128]{1,0:T(8,128)} %get-tuple-element.94) | copy-start | bytes 1179652
  433.3 44.8 %copy-start.2 = (f32[3,197,768]{2,1,0:T(8,128)S(1)}, f32[3,197,768]{2,1,0:T(8,128)}, u32[]{:S(2)}) copy-start(f32[3,197,768]{2,1,0:T(8,128)} %get-tuple-element.88) | copy-start | bytes 5446660
  433.4 44.8 %copy-start.3 = (f32[3,197,768]{2,1,0:T(8,128)S(1)}, f32[3,197,768]{2,1,0:T(8,128)}, u32[]{:S(2)}) copy-start(f32[3,197,768]{2,1,0:T(8,128)} %get-tuple-element.89) | copy-start | bytes 5446660
  478.1 2.2 copy-start.4
  480.3 2.1 copy-start.5
  482.5 1.4 copy-start.6
  482.5 2.7 copy-start
  485.1 2.5 copy-start.1

commit v7 on v6

--- a/solution.py
+++ b/solution.py
@@ -545,6 +545,10 @@
     mine = lax.axis_index("expert")
     chunks = rows // chunk
 
+    def each_chunk(body):
+        for index in range(chunks):
+            body(pl.ds(index * chunk, chunk))
+
     @pl.when(step == 0)
     def _():
         rides.start(ride_refs)
@@ -552,8 +556,9 @@
             load.start()
         for load in loads:
             load.wait()
-        for index in range(chunks):
-            at = pl.ds(index * chunk, chunk)
+
+        @each_chunk
+        def _(at):
             probs = softmax_lanes(dot_t(x_ref[at, :], small_ref[...]), experts)
             lane = lax.broadcasted_iota(jnp.int32, probs.shape, 1)
             probs_ref[at, :] = probs
@@ -565,8 +570,8 @@
     w1 = w1_ref[...]
     w2 = w2_ref[...]
     bias = bias_ref[...].astype(f32)
-    dbias = jnp.zeros(bias.shape, f32)
-    for index in range(chunks):
+
+    def rows_step(index, dbias):
         at = pl.ds(index * chunk, chunk)
         act, slope = gelu_both(dot_t(x_ref[at, :], w1) + bias)
         act = act.astype(bf16)
@@ -574,8 +579,12 @@
         result_acc[at, :] += dot(act, w2)
         grad_pre = (dot_t(dr_ref[at, :], w2) * slope).astype(bf16)
         pre_ref[at, :] = grad_pre
-        dbias = dbias + jnp.sum(grad_pre.astype(f32), axis=0, keepdims=True)
         dx_acc[at, :] += dot(grad_pre, w1)
+        return dbias + jnp.sum(grad_pre.astype(f32), axis=0, keepdims=True)
+
+    dbias = jnp.zeros(bias.shape, f32)
+    for index in range(chunks):
+        dbias = rows_step(index, dbias)
     dw1 = t_dot(pre_ref[...], x_ref[...])
     dw2 = t_dot(act_ref[...], dr_ref[...])
     dbias = jnp.broadcast_to(dbias, (LANES, dbias.shape[1])).T
@@ -589,11 +598,13 @@
 
     @pl.when(step == last)
     def _():
-        drouter = jnp.zeros(drouter_ref.shape, f32)
         if add:
-            drouter = old_router_ref[...]
-        for index in range(chunks):
-            at = pl.ds(index * chunk, chunk)
+            drouter_ref[...] = old_router_ref[...]
+        else:
+            drouter_ref[...] = jnp.zeros(drouter_ref.shape, f32)
+
+        @each_chunk
+        def _(at):
             result = result_acc[at, :].astype(bf16)
             result_ref[at, :] = result
             grad_gate = jnp.sum(
@@ -609,8 +620,8 @@
             dx_ref[at, :] = (
                 dx_acc[at, :] + dot(high, small_ref[...]) + dot(low, small_ref[...])
             ).astype(bf16)
-            drouter = drouter + t_dot(high, x_ref[at, :]) + t_dot(low, x_ref[at, :])
-        drouter_ref[...] = drouter
+            drouter_ref[...] += t_dot(high, x_ref[at, :]) + t_dot(low, x_ref[at, :])
+
         for store in stores:
             store.start()
         rides.finish(ride_refs)
@@ -702,16 +713,16 @@
 
 
 def finish_kernel(
-    inner, outer, slots_ref, gates_ref, residual_ref,
+    inner, outer, bits, slots_ref, gates_ref, residual_ref,
     returned0_hbm, returned1_hbm, part_ref, out_ref, din_ref, dout_ref, little_ref,
-    returned0_ref, returned1_ref, load_sems, flat_ref, second_ref, full_ref, sems2, sems3, sems4,
+    returned0_ref, returned1_ref, load_sems, flat_ref, sum_ref, second_ref, full_ref, sems2, sems3, sems4,
 ):
     step = pl.program_id(0)
     seq = slots_ref.shape[1]
     features = out_ref.shape[2]
     width = part_ref.shape[2]
     tiles = width // LANES
-    chunks = 5
+    chunks = 4
     edges = [LANES * (tiles * c // chunks) for c in range(chunks + 1)]
     cuts = [pl.ds(edges[c], edges[c + 1] - edges[c]) for c in range(chunks)]
     me = lax.axis_index("expert")
@@ -720,9 +731,6 @@
 
     def row_peer(hop):
         return lax.rem(row + hop, inner)
-
-    def line_peer(hop):
-        return lax.rem(line + hop, outer)
 
     def copy(source, target, sems, chunk, hop, peer):
         return pltpu.make_async_remote_copy(
@@ -734,24 +742,50 @@
             device_id_type=pl.DeviceIdType.MESH,
         )
 
-    def reduce_lines(chunk):
+    def flip(bit):
+        size = 2**bit
+        return line + size * (1 - 2 * lax.rem(line // size, 2))
+
+    def held(bit, side):
+        size = 2**bit
+        mine = lax.rem(line // size, 2)
+        first = lax.rem(line, size) + size * (mine if side else 1 - mine)
+        return [first + 2 * size * place for place in range(outer // (2 * size))]
+
+    def slot(bit, place):
+        return sum(outer // 2 ** (lower + 1) for lower in range(bit)) + place
+
+    def reduce_lines(bit, chunk):
+        at = cuts[chunk]
+        source = part_ref if bit == 0 else sum_ref
+        return [
+            copy(
+                source.at[block, :, at], second_ref.at[slot(bit, place), :, at],
+                sems2, chunk, 1 + slot(bit, place), flip(bit) * inner + row,
+            )
+            for place, block in enumerate(held(bit, False))
+        ]
+
+    def add_lines(bit, chunk):
+        at = cuts[chunk]
+        source = part_ref if bit == 0 else sum_ref
+        for place, block in enumerate(held(bit, True)):
+            total = source[block, :, at].astype(f32) + second_ref[
+                slot(bit, place), :, at
+            ].astype(f32)
+            if bit == bits - 1:
+                full_ref[row, block, :, at] = total.astype(bf16)
+            else:
+                sum_ref[block, :, at] = total.astype(bf16)
+
+    def gather_lines(bit, chunk):
         at = cuts[chunk]
         return [
             copy(
-                part_ref.at[line_peer(hop), :, at], second_ref.at[hop - 1, :, at],
-                sems2, chunk, hop, line_peer(hop) * inner + row,
+                full_ref.at[row, block, :, at], full_ref.at[row, block, :, at],
+                sems3, chunk, 1 + slot(bit, place), flip(bit) * inner + row,
             )
-            for hop in range(1, outer)
-        ]
-
-    def gather_lines(chunk):
-        at = cuts[chunk]
-        return [
-            copy(
-                full_ref.at[row, line, :, at], full_ref.at[row, line, :, at],
-                sems3, chunk, hop, line_peer(hop) * inner + row,
-            )
-            for hop in range(1, outer)
+            for place, block in enumerate(held(bit, True))
         ]
 
     def gather_rows(chunk):
@@ -781,7 +815,7 @@
     def _():
         barrier = pltpu.get_barrier_semaphore()
         peers = [line * inner + row_peer(hop) for hop in range(1, inner)]
-        peers += [line_peer(hop) * inner + row for hop in range(1, outer)]
+        peers += [flip(bit) * inner + row for bit in range(bits)]
         for peer in peers:
             pl.semaphore_signal(
                 barrier,
@@ -791,7 +825,7 @@
             )
         pl.semaphore_wait(barrier, len(peers))
         for chunk in range(chunks):
-            start(reduce_lines(chunk))
+            start(reduce_lines(0, chunk))
         start(loads)
         wait(loads[:1])
 
@@ -819,22 +853,29 @@
     def _():
         mix(returned1_ref)
 
-    @pl.when(step == 1)
-    def _():
-        for chunk in range(chunks):
-            at = cuts[chunk]
-            wait(reduce_lines(chunk))
-            total = part_ref[line, :, at].astype(f32)
-            for hop in range(1, outer):
-                total = total + second_ref[hop - 1, :, at].astype(f32)
-            full_ref[row, line, :, at] = total.astype(bf16)
-            start(gather_lines(chunk))
-
-    @pl.when(step == 3)
-    def _():
-        for chunk in range(chunks):
-            wait(gather_lines(chunk))
+    def reduced(bit, chunk):
+        wait(reduce_lines(bit, chunk))
+        add_lines(bit, chunk)
+        if bit < bits - 1:
+            start(reduce_lines(bit + 1, chunk))
+        else:
+            start(gather_lines(bit, chunk))
+
+    def gathered(bit, chunk):
+        wait(gather_lines(bit, chunk))
+        if bit > 0:
+            start(gather_lines(bit - 1, chunk))
+        else:
             start(gather_rows(chunk))
+
+    stages = [functools.partial(reduced, bit) for bit in range(bits)]
+    stages += [functools.partial(gathered, bit) for bit in reversed(range(bits))]
+    for place, stage in enumerate(stages):
+
+        @pl.when(step == min(place + 1, 2 * IMG_MB - 1))
+        def _():
+            for chunk in range(chunks):
+                stage(chunk)
 
     @pl.when(step == 2 * IMG_MB - 1)
     def _():
@@ -857,8 +898,9 @@
 def finish(slots, gates, residual, returned, part, parts, lines, collective):
     outer, share, width = part.shape
     inner = inner_size(parts)
+    bits = outer.bit_length() - 1
     images, seq, features = residual.shape
-    chunks = 5
+    chunks = 4
 
     def whole(shape):
         return pl.BlockSpec(
@@ -871,7 +913,7 @@
     outs = [3 * features, features]
     little = (lines, parts * share)
     return pl.pallas_call(
-        functools.partial(finish_kernel, inner, outer),
+        functools.partial(finish_kernel, inner, outer, bits),
         grid=(images,),
         in_specs=[
             each(TOP), each(TOP), each(features),
@@ -885,6 +927,7 @@
         scratch_shapes=[
             *staged(*returned),
             pltpu.VMEM((parts * share, LANES), f32),
+            pltpu.VMEM((outer, share, width), bf16),
             pltpu.VMEM((outer - 1, share, width), bf16),
             pltpu.VMEM((inner, outer, share, width), bf16),
             pltpu.SemaphoreType.DMA((2, chunks, outer - 1)),
@@ -921,9 +964,9 @@
     else:
         dsmall_ref, sums_b_hbm, grad_a_ref = refs[2:5]
     targets, refs = refs[outs : outs + count], refs[outs + count :]
-    acc_in, acc_out, acc_small, dproj_ref = refs[:4]
-    sent_ref, dense_ref, copy_sems = refs[4:7]
-    refs = refs[7:]
+    acc_in, acc_out, acc_small, dproj_ref, grad_mixed_ref = refs[:5]
+    sent_ref, dense_ref, copy_sems = refs[5:8]
+    refs = refs[8:]
     rank = lax.axis_index("dp")
     core = lax.rem(rank, 2)
     mine = rank // 2
@@ -1047,15 +1090,16 @@
         grad_hidden * vectors[experts + 2 : experts + 3], normed_two, inverse_two
     )
     grad_branch = grad_residual.astype(bf16)
-    grad_mixed = dot_t(grad_branch, dense_ref[:, 3 * features : 4 * features]).astype(bf16)
+    grad_mixed_ref[...] = dot_t(grad_branch, dense_ref[:, 3 * features : 4 * features]).astype(
+        bf16
+    )
     low_half = lax.broadcasted_iota(jnp.int32, (1, LANES), 1) < HEAD_DIM
     scale = HEAD_DIM ** (-0.5)
-    for pair in range(features // LANES):
-        first = pair * LANES
-        queries = proj_ref[0, :, first : first + LANES]
-        keys = proj_ref[0, :, features + first : features + first + LANES]
-        values = proj_ref[0, :, 2 * features + first : 2 * features + first + LANES]
-        grad_out = grad_mixed[:, first : first + LANES]
+    def head_pair(first):
+        queries = proj_ref[0, :, pl.ds(first, LANES)]
+        keys = proj_ref[0, :, pl.ds(features + first, LANES)]
+        values = proj_ref[0, :, pl.ds(2 * features + first, LANES)]
+        grad_out = grad_mixed_ref[:, pl.ds(first, LANES)]
         sums = [None, None, None]
         for half in range(2):
             keep = low_half if half == 0 else jnp.logical_not(low_half)
@@ -1074,9 +1118,11 @@
             grad_queries = t_dot(grad_scores, head_keys)
             for place, part in enumerate((grad_queries, grad_keys, grad_values)):
                 sums[place] = part if half == 0 else sums[place] + part
-        dproj_ref[:, first : first + LANES] = (sums[0] * scale).astype(bf16)
-        dproj_ref[:, features + first : features + first + LANES] = sums[1].astype(bf16)
-        dproj_ref[:, 2 * features + first : 2 * features + first + LANES] = sums[2].astype(bf16)
+        dproj_ref[:, pl.ds(first, LANES)] = (sums[0] * scale).astype(bf16)
+        dproj_ref[:, pl.ds(features + first, LANES)] = sums[1].astype(bf16)
+        dproj_ref[:, pl.ds(2 * features + first, LANES)] = sums[2].astype(bf16)
+    for pair in range(features // LANES):
+        head_pair(pair * LANES)
     normed_one, inverse_one = norm_forward(x_ref[0].astype(f32))
     attn_input = (
         normed_one * vectors[experts : experts + 1] + vectors[experts + 1 : experts + 2]
@@ -1271,6 +1317,7 @@
             pltpu.VMEM((features, features), f32),
             pltpu.VMEM(small_grads, f32),
             pltpu.VMEM((seq, wide), bf16),
+            pltpu.VMEM((seq, features), bf16),
             *staged(sent, dense),
         ]
         + reduce_scratch

time: 496 us -> 495 us (level)
  no operation moved by 1% of the time
where the time goes in v7:
time: 495 us; the launch traced here: 489 us
  Pallas kernels  472 us (95%)
  local copies, waits for them, and re-layouts  12.2 us (2%)
    pallas_call x2, Pallas kernels, expert_block(): pl.pallas_call(functools.partial(expert_kernel, experts, chunk, add, ride...  176 us
    pallas_call x2, Pallas kernels, attend_back(): pl.pallas_call(functools.partial(attend_back_kernel, experts, add, rides,...  144 us
    pallas_call x1, Pallas kernels, front(): pl.pallas_call(functools.partial(front_kernel, experts, capacity, ranks,...  111 us
    pallas_call x1, Pallas kernels, finish(): pl.pallas_call(functools.partial(finish_kernel, inner, outer, bits), grid...  40.6 us

profile of v7, /device:TPU:0, one launch (start us, length us, event | category | flops | bytes accessed | tf_op | source)
XLA Modules:
  0.0 488.9 jit_solution(11030930420233544428)
XLA Ops:
  0.7 1.4 select_select_fusion.gains_ref
  2.0 110.8 %front.1 = (bf16[6,197,2304]{2,1,0:T(8,128)(2,1)}, bf16[6,197,768]{2,1,0:T(8,128)(2,1)}, f32[6,197,768]{2,1,0:T(8,128)}, f32[6,197,2]{2,1,0:T(8,128)}, s32[6,197...) custom-call(bf16[6,197,768]{2,1,0:T(8,128)(2,1)} %x_ref.5, ...), custom_call_target="tpu_custom_call" | custom-call | flops 11154751488 | bytes 38486016 | tf_op jit(solution)/shard_map/front/pallas_call | solution.py:465
  112.9 88.0 %expert_block.2 = (bf16[1472,768]{1,0:T(8,128)(2,1)}, bf16[1472,768]{1,0:T(8,128)(2,1)}, f32[3072,1664]{1,0:T(8,128)}, f32[16,768]{1,0:T(8,128)}, bf16[8,184,768...) custom-call(bf16[1472,768]{1,0:T(8,128)(2,1)} %bitcast.45, bf16[1472,768]{1,0:T(8,128)(2,1)} %bitcast.44, ...), custom_call_target="tpu_custom_call" | custom-call | flops 41674604544 | bytes 37355520 | tf_op jit(solution)/shard_map/expert_block/pallas_call | solution.py:671
  200.9 88.3 %expert_block.3 = (bf16[1472,768]{1,0:T(8,128)(2,1)}, bf16[1472,768]{1,0:T(8,128)(2,1)}, bf16[3072,1664]{1,0:T(8,128)(2,1)}, f32[16,768]{1,0:T(8,128)}, bf16[8,1...) custom-call(bf16[1472,768]{1,0:T(8,128)(2,1)} %bitcast.50, bf16[1472,768]{1,0:T(8,128)(2,1)} %bitcast.49, ...), custom_call_target="tpu_custom_call" | custom-call | flops 41674604544 | bytes 37355520 | tf_op jit(solution)/shard_map/expert_block/pallas_call | solution.py:671
  289.2 45.6 %attend_back.2 = (f32[3,197,768]{2,1,0:T(8,128)}, f32[768,3072]{1,0:T(8,128)}, f32[8,768]{1,0:T(8,128)}, bf16[2,768,896]{2,1,0:T(8,128)(2,1)}, f32[768,768]{1,0:T(8,128)}, /*index=5*/bf16[8,184,768]{2,1,0:T(8,128)(2,1)}) custom-call(bf16[6,197,768]{2,1,0:T(8,128)(2,1)} %x_ref.5, bf16[6,197,768]{2,1,0:T(8,128)(2,1)} %top_ref.5, ...), custom_call_target="tpu_custom_call" | custom-call | flops 13943439360 | bytes 33398784 | tf_op jit(solution)/shard_map/attend_back/pallas_call | solution.py:1309
  334.8 98.7 %attend_back.3 = (f32[3,197,768]{2,1,0:T(8,128)}, bf16[4,24,3200]{2,1,0:T(8,128)(2,1)}, f32[768,768]{1,0:T(8,128)}, f32[768,128]{1,0:T(8,128)}, bf16[8,184,768]{...) custom-call(bf16[6,197,768]{2,1,0:T(8,128)(2,1)} %x_ref.5, ...), custom_call_target="tpu_custom_call", output_to_operand_aliasing={{4}: (15, {})} | custom-call | flops 13943439360 | bytes 33398784 | tf_op jit(solution)/shard_map/attend_back/pallas_call | solution.py:1309
  433.5 0.0 copy-start.7
  433.5 40.6 %finish.1 = (bf16[6,197,768]{2,1,0:T(8,128)(2,1)}, f32[8,24,2304]{2,1,0:T(8,128)}, f32[8,24,768]{2,1,0:T(8,128)}, f32[24,192]{1,0:T(8,128)}) custom-call(s32[6,197,2]{2,1,0:T(8,128)} %get-tuple-element.54.slots_ref, f32[6,197,2]{2,1,0:T(8,128)} %get-tuple-element.55.gates_ref, f32[6,197,768]{2,1,0:T(8,128)} %get-tuple-element.56.residual_ref, ...), custom_call_target="tpu_custom_call" | custom-call | flops 5344985088 | bytes 9968640 | tf_op jit(solution)/shard_map/finish/pallas_call | solution.py:915
  474.1 0.2 slice_reduce_fusion
  474.3 0.6 broadcast_in_dim_squeeze.3
  474.9 1.4 fusion
  476.3 1.3 slice_bitcast_fusion
  477.6 0.0 copy-done.3
  477.6 2.2 pad_maximum_fusion
  479.8 0.0 copy-done.4
  479.8 1.2 copy.32
  481.0 0.9 copy-done.5
  481.9 1.2 copy.33
  483.1 0.2 copy-done.6
  483.3 0.8 copy.34
  484.2 0.4 copy-done
  484.6 1.4 copy.35
  486.0 1.1 copy-done.1
  487.1 1.4 copy.36
  (11 shorter events, 0.0 us)
Async XLA Ops:
  433.5 40.6 %copy-start.7 = (f32[768,128]{1,0:T(8,128)S(1)}, f32[768,128]{1,0:T(8,128)}, u32[]{:S(2)}) copy-start(f32[768,128]{1,0:T(8,128)} %get-tuple-element.94) | copy-start | bytes 1179652
  433.5 44.1 %copy-start.2 = (f32[3,197,768]{2,1,0:T(8,128)S(1)}, f32[3,197,768]{2,1,0:T(8,128)}, u32[]{:S(2)}) copy-start(f32[3,197,768]{2,1,0:T(8,128)} %get-tuple-element.88) | copy-start | bytes 5446660
  433.5 44.1 %copy-start.3 = (f32[3,197,768]{2,1,0:T(8,128)S(1)}, f32[3,197,768]{2,1,0:T(8,128)}, u32[]{:S(2)}) copy-start(f32[3,197,768]{2,1,0:T(8,128)} %get-tuple-element.89) | copy-start | bytes 5446660
  477.6 2.2 copy-start.4
  479.8 2.1 copy-start.5
  481.9 1.4 copy-start.6
  481.9 2.7 copy-start
  484.6 2.5 copy-start.1

commit v8 on v7

--- a/solution.py
+++ b/solution.py
@@ -592,7 +592,7 @@
     for part in (dw1, dw2, dbias):
         at = pl.ds(first, part.shape[1])
         if add:
-            part = part + old_w_ref[:, at]
+            part = part + old_w_ref[:, at].astype(f32)
         dw_ref[:, at] = part.astype(dw_ref.dtype)
         first += part.shape[1]
 
@@ -644,7 +644,7 @@
     steps = hidden_units // block
     chunk = row_chunk(rows)
     add = old is not None
-    out_type = bf16 if add else f32
+    out_type = bf16
     rides = Rides(entries)
 
     def whole(shape):
@@ -1374,7 +1374,7 @@
         flat(received_0), flat(grads_0), weight_in, weight_out, bias_row, small, experts, None,
         [(grad_rows_1, 0, capacity, None), (token_rows_1, 0, capacity, None)], 0,
     )
-    early = max(8, capacity * 3 // 8 // 8 * 8)
+    early = max(8, capacity * 2 // 5 // 8 * 8)
     result_1, dx_1, dweights, drouter, sent_0, returned_0 = expert_block(
         flat(received_1), flat(grads_1), weight_in, weight_out, bias_row, small, experts, old,
         [(blocks(dx_0), 0, capacity, None), (blocks(result_0), 0, early, None)], 1,

time: 495 us -> 496 us (level)
  no operation moved by 1% of the time
where the time goes in v8:
time: 496 us; the launch traced here: 490 us
  Pallas kernels  473 us (95%)
  local copies, waits for them, and re-layouts  12.2 us (2%)
    pallas_call x2, Pallas kernels, expert_block(): pl.pallas_call(functools.partial(expert_kernel, experts, chunk, add, ride...  175 us
    pallas_call x2, Pallas kernels, attend_back(): pl.pallas_call(functools.partial(attend_back_kernel, experts, add, rides,...  145 us
    pallas_call x1, Pallas kernels, front(): pl.pallas_call(functools.partial(front_kernel, experts, capacity, ranks,...  111 us
    pallas_call x1, Pallas kernels, finish(): pl.pallas_call(functools.partial(finish_kernel, inner, outer, bits), grid...  41.7 us

profile of v8, /device:TPU:0, one launch (start us, length us, event | category | flops | bytes accessed | tf_op | source)
XLA Modules:
  0.0 489.6 jit_solution(6653664715031870570)
XLA Ops:
  0.7 1.4 select_select_fusion.gains_ref
  2.0 110.8 %front.1 = (bf16[6,197,2304]{2,1,0:T(8,128)(2,1)}, bf16[6,197,768]{2,1,0:T(8,128)(2,1)}, f32[6,197,768]{2,1,0:T(8,128)}, f32[6,197,2]{2,1,0:T(8,128)}, s32[6,197...) custom-call(bf16[6,197,768]{2,1,0:T(8,128)(2,1)} %x_ref.5, ...), custom_call_target="tpu_custom_call" | custom-call | flops 11154751488 | bytes 38486016 | tf_op jit(solution)/shard_map/front/pallas_call | solution.py:465
  112.8 87.5 %expert_block.2 = (bf16[1472,768]{1,0:T(8,128)(2,1)}, bf16[1472,768]{1,0:T(8,128)(2,1)}, bf16[3072,1664]{1,0:T(8,128)(2,1)}, f32[16,768]{1,0:T(8,128)}, bf16[8,1...) custom-call(bf16[1472,768]{1,0:T(8,128)(2,1)} %bitcast.45, bf16[1472,768]{1,0:T(8,128)(2,1)} %bitcast.44, ...), custom_call_target="tpu_custom_call" | custom-call | flops 41674604544 | bytes 37355520 | tf_op jit(solution)/shard_map/expert_block/pallas_call | solution.py:671
  200.3 87.6 %expert_block.3 = (bf16[1472,768]{1,0:T(8,128)(2,1)}, bf16[1472,768]{1,0:T(8,128)(2,1)}, bf16[3072,1664]{1,0:T(8,128)(2,1)}, f32[16,768]{1,0:T(8,128)}, bf16[8,1...) custom-call(bf16[1472,768]{1,0:T(8,128)(2,1)} %bitcast.50, bf16[1472,768]{1,0:T(8,128)(2,1)} %bitcast.49, ...), custom_call_target="tpu_custom_call" | custom-call | flops 41674604544 | bytes 37355520 | tf_op jit(solution)/shard_map/expert_block/pallas_call | solution.py:671
  287.9 47.9 %attend_back.2 = (f32[3,197,768]{2,1,0:T(8,128)}, f32[768,3072]{1,0:T(8,128)}, f32[8,768]{1,0:T(8,128)}, bf16[2,768,896]{2,1,0:T(8,128)(2,1)}, f32[768,768]{1,0:T(8,128)}, /*index=5*/bf16[8,184,768]{2,1,0:T(8,128)(2,1)}) custom-call(bf16[6,197,768]{2,1,0:T(8,128)(2,1)} %x_ref.5, bf16[6,197,768]{2,1,0:T(8,128)(2,1)} %top_ref.5, ...), custom_call_target="tpu_custom_call" | custom-call | flops 13943439360 | bytes 33398784 | tf_op jit(solution)/shard_map/attend_back/pallas_call | solution.py:1309
  335.8 97.2 %attend_back.3 = (f32[3,197,768]{2,1,0:T(8,128)}, bf16[4,24,3200]{2,1,0:T(8,128)(2,1)}, f32[768,768]{1,0:T(8,128)}, f32[768,128]{1,0:T(8,128)}, bf16[8,184,768]{...) custom-call(bf16[6,197,768]{2,1,0:T(8,128)(2,1)} %x_ref.5, ...), custom_call_target="tpu_custom_call", output_to_operand_aliasing={{4}: (15, {})} | custom-call | flops 13943439360 | bytes 33398784 | tf_op jit(solution)/shard_map/attend_back/pallas_call | solution.py:1309
  433.1 0.0 copy-start.7
  433.1 0.0 copy-start.2
  433.1 0.0 copy-start.3
  433.1 41.7 %finish.1 = (bf16[6,197,768]{2,1,0:T(8,128)(2,1)}, f32[8,24,2304]{2,1,0:T(8,128)}, f32[8,24,768]{2,1,0:T(8,128)}, f32[24,192]{1,0:T(8,128)}) custom-call(s32[6,197,2]{2,1,0:T(8,128)} %get-tuple-element.54.slots_ref, f32[6,197,2]{2,1,0:T(8,128)} %get-tuple-element.55.gates_ref, f32[6,197,768]{2,1,0:T(8,128)} %get-tuple-element.56.residual_ref, ...), custom_call_target="tpu_custom_call" | custom-call | flops 5344985088 | bytes 9968640 | tf_op jit(solution)/shard_map/finish/pallas_call | solution.py:915
  474.8 0.2 slice_reduce_fusion
  475.0 0.6 broadcast_in_dim_squeeze.3
  475.6 1.4 fusion
  477.0 1.3 slice_bitcast_fusion
  478.3 2.2 pad_maximum_fusion
  480.5 1.2 copy.32
  481.7 0.9 copy-done.5
  482.6 1.2 copy.33
  483.8 0.2 copy-done.6
  484.1 0.8 copy.34
  484.9 0.4 copy-done
  485.3 1.4 copy.35
  486.7 1.1 copy-done.1
  487.8 1.4 copy.36
  (11 shorter events, 0.0 us)
Async XLA Ops:
  433.1 41.7 %copy-start.7 = (f32[768,128]{1,0:T(8,128)S(1)}, f32[768,128]{1,0:T(8,128)}, u32[]{:S(2)}) copy-start(f32[768,128]{1,0:T(8,128)} %get-tuple-element.94) | copy-start | bytes 1179652
  433.1 45.2 %copy-start.2 = (f32[3,197,768]{2,1,0:T(8,128)S(1)}, f32[3,197,768]{2,1,0:T(8,128)}, u32[]{:S(2)}) copy-start(f32[3,197,768]{2,1,0:T(8,128)} %get-tuple-element.88) | copy-start | bytes 5446660
  433.1 45.2 %copy-start.3 = (f32[3,197,768]{2,1,0:T(8,128)S(1)}, f32[3,197,768]{2,1,0:T(8,128)}, u32[]{:S(2)}) copy-start(f32[3,197,768]{2,1,0:T(8,128)} %get-tuple-element.89) | copy-start | bytes 5446660
  478.3 2.2 copy-start.4
  480.5 2.1 copy-start.5
  482.6 1.4 copy-start.6
  482.6 2.7 copy-start
  485.3 2.5 copy-start.1

commit v9 on v7

--- a/solution.py
+++ b/solution.py
@@ -1374,7 +1374,7 @@
         flat(received_0), flat(grads_0), weight_in, weight_out, bias_row, small, experts, None,
         [(grad_rows_1, 0, capacity, None), (token_rows_1, 0, capacity, None)], 0,
     )
-    early = max(8, capacity * 3 // 8 // 8 * 8)
+    early = max(8, capacity * 5 // 16 // 8 * 8)
     result_1, dx_1, dweights, drouter, sent_0, returned_0 = expert_block(
         flat(received_1), flat(grads_1), weight_in, weight_out, bias_row, small, experts, old,
         [(blocks(dx_0), 0, capacity, None), (blocks(result_0), 0, early, None)], 1,

time: 495 us -> 494 us (level)
  no operation moved by 1% of the time
where the time goes in v9:
time: 494 us; the launch traced here: 487 us
  Pallas kernels  471 us (95%)
  local copies, waits for them, and re-layouts  12.2 us (2%)
    pallas_call x2, Pallas kernels, expert_block(): pl.pallas_call(functools.partial(expert_kernel, experts, chunk, add, ride...  176 us
    pallas_call x2, Pallas kernels, attend_back(): pl.pallas_call(functools.partial(attend_back_kernel, experts, add, rides,...  143 us
    pallas_call x1, Pallas kernels, front(): pl.pallas_call(functools.partial(front_kernel, experts, capacity, ranks,...  111 us
    pallas_call x1, Pallas kernels, finish(): pl.pallas_call(functools.partial(finish_kernel, inner, outer, bits), grid...  40.1 us

profile of v9, /device:TPU:0, one launch (start us, length us, event | category | flops | bytes accessed | tf_op | source)
XLA Modules:
  0.0 487.5 jit_solution(5419892473620173366)
XLA Ops:
  0.7 1.4 select_select_fusion.gains_ref
  2.0 110.8 %front.1 = (bf16[6,197,2304]{2,1,0:T(8,128)(2,1)}, bf16[6,197,768]{2,1,0:T(8,128)(2,1)}, f32[6,197,768]{2,1,0:T(8,128)}, f32[6,197,2]{2,1,0:T(8,128)}, s32[6,197...) custom-call(bf16[6,197,768]{2,1,0:T(8,128)(2,1)} %x_ref.5, ...), custom_call_target="tpu_custom_call" | custom-call | flops 11154751488 | bytes 38486016 | tf_op jit(solution)/shard_map/front/pallas_call | solution.py:465
  112.9 88.0 %expert_block.2 = (bf16[1472,768]{1,0:T(8,128)(2,1)}, bf16[1472,768]{1,0:T(8,128)(2,1)}, f32[3072,1664]{1,0:T(8,128)}, f32[16,768]{1,0:T(8,128)}, bf16[8,184,768...) custom-call(bf16[1472,768]{1,0:T(8,128)(2,1)} %bitcast.45, bf16[1472,768]{1,0:T(8,128)(2,1)} %bitcast.44, ...), custom_call_target="tpu_custom_call" | custom-call | flops 41674604544 | bytes 37355520 | tf_op jit(solution)/shard_map/expert_block/pallas_call | solution.py:671
  200.9 88.3 %expert_block.3 = (bf16[1472,768]{1,0:T(8,128)(2,1)}, bf16[1472,768]{1,0:T(8,128)(2,1)}, bf16[3072,1664]{1,0:T(8,128)(2,1)}, f32[16,768]{1,0:T(8,128)}, bf16[8,1...) custom-call(bf16[1472,768]{1,0:T(8,128)(2,1)} %bitcast.50, bf16[1472,768]{1,0:T(8,128)(2,1)} %bitcast.49, ...), custom_call_target="tpu_custom_call" | custom-call | flops 41674604544 | bytes 37355520 | tf_op jit(solution)/shard_map/expert_block/pallas_call | solution.py:671
  289.2 44.1 %attend_back.2 = (f32[3,197,768]{2,1,0:T(8,128)}, f32[768,3072]{1,0:T(8,128)}, f32[8,768]{1,0:T(8,128)}, bf16[2,768,896]{2,1,0:T(8,128)(2,1)}, f32[768,768]{1,0:T(8,128)}, /*index=5*/bf16[8,184,768]{2,1,0:T(8,128)(2,1)}) custom-call(bf16[6,197,768]{2,1,0:T(8,128)(2,1)} %x_ref.5, bf16[6,197,768]{2,1,0:T(8,128)(2,1)} %top_ref.5, ...), custom_call_target="tpu_custom_call" | custom-call | flops 13943439360 | bytes 33398784 | tf_op jit(solution)/shard_map/attend_back/pallas_call | solution.py:1309
  333.3 99.2 %attend_back.3 = (f32[3,197,768]{2,1,0:T(8,128)}, bf16[4,24,3200]{2,1,0:T(8,128)(2,1)}, f32[768,768]{1,0:T(8,128)}, f32[768,128]{1,0:T(8,128)}, bf16[8,184,768]{...) custom-call(bf16[6,197,768]{2,1,0:T(8,128)(2,1)} %x_ref.5, ...), custom_call_target="tpu_custom_call", output_to_operand_aliasing={{4}: (15, {})} | custom-call | flops 13943439360 | bytes 33398784 | tf_op jit(solution)/shard_map/attend_back/pallas_call | solution.py:1309
  432.5 0.0 copy-start.7
  432.6 0.0 copy-start.2
  432.6 0.0 copy-start.3
  432.6 40.1 %finish.1 = (bf16[6,197,768]{2,1,0:T(8,128)(2,1)}, f32[8,24,2304]{2,1,0:T(8,128)}, f32[8,24,768]{2,1,0:T(8,128)}, f32[24,192]{1,0:T(8,128)}) custom-call(s32[6,197,2]{2,1,0:T(8,128)} %get-tuple-element.54.slots_ref, f32[6,197,2]{2,1,0:T(8,128)} %get-tuple-element.55.gates_ref, f32[6,197,768]{2,1,0:T(8,128)} %get-tuple-element.56.residual_ref, ...), custom_call_target="tpu_custom_call" | custom-call | flops 5344985088 | bytes 9968640 | tf_op jit(solution)/shard_map/finish/pallas_call | solution.py:915
  472.7 0.2 slice_reduce_fusion
  472.8 0.6 broadcast_in_dim_squeeze.3
  473.4 1.4 fusion
  474.8 1.3 slice_bitcast_fusion
  476.2 2.2 pad_maximum_fusion
  478.3 1.2 copy.32
  479.6 0.9 copy-done.5
  480.5 1.2 copy.33
  481.7 0.2 copy-done.6
  481.9 0.8 copy.34
  482.7 0.4 copy-done
  483.1 1.4 copy.35
  484.5 1.1 copy-done.1
  485.7 1.4 copy.36
  (11 shorter events, 0.0 us)
Async XLA Ops:
  432.5 40.1 %copy-start.7 = (f32[768,128]{1,0:T(8,128)S(1)}, f32[768,128]{1,0:T(8,128)}, u32[]{:S(2)}) copy-start(f32[768,128]{1,0:T(8,128)} %get-tuple-element.94) | copy-start | bytes 1179652
  432.6 43.6 %copy-start.2 = (f32[3,197,768]{2,1,0:T(8,128)S(1)}, f32[3,197,768]{2,1,0:T(8,128)}, u32[]{:S(2)}) copy-start(f32[3,197,768]{2,1,0:T(8,128)} %get-tuple-element.88) | copy-start | bytes 5446660
  432.6 43.6 %copy-start.3 = (f32[3,197,768]{2,1,0:T(8,128)S(1)}, f32[3,197,768]{2,1,0:T(8,128)}, u32[]{:S(2)}) copy-start(f32[3,197,768]{2,1,0:T(8,128)} %get-tuple-element.89) | copy-start | bytes 5446660
  476.2 2.2 copy-start.4
  478.3 2.1 copy-start.5
  480.5 1.4 copy-start.6
  480.5 2.7 copy-start
  483.1 2.5 copy-start.1
